TPU v7x, 256 devices: a whole 4x4x8 slice. The times are simulated.
256 devices in a mesh: gx: 8 (over x, y_hi), gy: 4 (over y_lo, core), gz: 8 (over z).
Axes of the slice: x: 4, y: 4 (y_hi: 2, y_lo: 2; y = y_hi * 2 + y_lo), z: 8, core: 2. Of those that a mesh axis runs over, the one named last changes fastest.
Arguments:
- local_pos: float32 [16, 8, 8, 3, 64], P('gx', 'gy', 'gz'), as said below
- counts: int32 [16, 8, 8], P('gx', 'gy', 'gz'), may hold values from 8 to 64, as said below
- species: int32 [16, 8, 8, 64], P('gx', 'gy', 'gz'), may hold values from 0 to 9
- features: bfloat16 [16, 8, 8, 64, 128], P('gx', 'gy', 'gz'), may hold values from -6 to 6
- radial_weights: float32 [2, 8, 128], replicated, may hold values from -2 to 2
- coupling: float32 [3, 10, 128], replicated, may hold values from -3 to 3
- mixing: float32 [128, 128], replicated, may hold values from -0.5 to 0.5
- hidden_weights: float32 [128, 16], replicated, may hold values from -0.5 to 0.5
- output_weights: float32 [16], replicated, may hold values from -1.5 to 1.5
Outputs:
- atom_energy: float32 [16, 8, 8, 64], P('gx', 'gy', 'gz')
- forces: float32 [16, 8, 8, 3, 64], P('gx', 'gy', 'gz')
- feature_grad: float32 [16, 8, 8, 64, 128], P('gx', 'gy', 'gz')
Inputs may be any that keep to these rules, and one draw needn't show every extreme that they name: `counts`: every cell holds between 8 and 64 atoms, and at least one cell is full. `local_pos`: the slots of a cell sit on distinct sites of a 4 x 4 x 4 lattice of spacing 7 / 4, each moved by at most 0.3 spacings along each coordinate, so any two slots are 0.4 spacings apart or more.
All inputs are finite; a program needn't handle non-finite values.
Results may differ from a plain program's by a relative error of at most 0.0048.
Values may be sent and summed in bfloat16 or wider, within the bound.
No kernel may reach another device: no remote copies, remote signals or barrier semaphores. Data moves between devices by JAX's collectives and lax.ppermute only.
A program may use at most 64 MiB of HBM per device.

v0:
```python
import functools

import jax
import jax.numpy as jnp
import numpy as np
from jax import lax
from jax.experimental import pallas as pl
from jax.experimental.pallas import tpu as pltpu
from jax.sharding import PartitionSpec as P

SIDE = 7.0
CUTOFF = 5.0
LAT = 4
SLOTS = LAT**3
NB = 8
CHAN = 128
EXTRA = 8
ROWS = SLOTS + EXTRA
COLROWS = 16
RUN = 3 * COLROWS
INNER = [(a, b) for a in (-1, 0, 1) for b in (-1, 0, 1)]
OUTER = [(a, b) for a in (-2, 2) for b in (-1, 0, 1)] + [(b, a) for a in (-2, 2) for b in (-1, 0, 1)]
WINDOW = []
_at = 0
for _a, _b in INNER:
    WINDOW.append((_a, _b, 4, 40, _at))
    _at += 40
for _a, _b in OUTER:
    WINDOW.append((_a, _b, 8, 32, _at))
    _at += 32
USED = _at
NJ = 768
TILE = 128
FAR = 1000.0


def offset_table():
    table = np.zeros((4, 8, NJ), np.float32)
    table[:, :3, USED:] = FAR
    for parity in range(4):
        px, py = parity // 2, parity % 2
        for a, b, first, count, at in WINDOW:
            table[parity, 0, at : at + count] = SIDE * ((px + a) // 2)
            table[parity, 1, at : at + count] = SIDE * ((py + b) // 2)
            run = np.arange(first, first + count)
            table[parity, 2, at : at + count] = SIDE * (run // COLROWS - 1)
    return table


def pick_table():
    table = np.zeros((8, CHAN), np.float32)
    for group in range(8):
        for part in range(3):
            for comp in range(3):
                table[comp, 16 * group + 3 * part + comp] = 1.0
    return table


def spread_table():
    table = np.zeros((16, CHAN), np.float32)
    for group in range(8):
        for part in range(2):
            for comp in range(3):
                table[3 * part + comp, 16 * group + comp] = 1.0
    return table


def poly_coeffs():
    v = 0.5 * np.cos(np.pi * (np.arange(400) + 0.5) / 400)
    sines = np.polynomial.polynomial.polyfit(v * v, np.sin(np.pi * v) / v, 5)
    cosines = np.polynomial.polynomial.polyfit(v * v, np.cos(np.pi * v), 6)
    return [float(c) for c in sines], [float(c) for c in cosines]


SIN_C, COS_C = poly_coeffs()


def horner(coeffs, x):
    value = coeffs[-1] * x + coeffs[-2]
    for c in coeffs[-3::-1]:
        value = value * x + c
    return value


def dot(a, b, dims, precision=None):
    return lax.dot_general(a, b, (dims, ((), ())), preferred_element_type=jnp.float32, precision=precision)


NN = ((1,), (0,))
NT = ((1,), (1,))
TN = ((0,), (0,))


def site_onehot(pos, count):
    site = jnp.clip(jnp.floor(pos * (LAT / SIDE)).astype(jnp.int32), 0, LAT - 1)
    sx, sy, sz = site[0:1], site[1:2], site[2:3]
    row = (((sx >> 1) * 2 + (sy >> 1)) * 4 + sz) * 4 + (sx & 1) * 2 + (sy & 1)
    slot = lax.broadcasted_iota(jnp.int32, (1, SLOTS), 1)
    row = jnp.where(slot < count, row, -1)
    return lax.broadcasted_iota(jnp.int32, (SLOTS, SLOTS), 0) == row


def lane_group(rows):
    return lax.broadcasted_iota(jnp.int32, (rows, CHAN), 1) >> 4


def sort_kernel(count_ref, pos_ref, kind_ref, feat_ref, msg_ref, parts_ref):
    group = lane_group(EXTRA)
    parts_ref[...] = jnp.zeros_like(parts_ref)
    for cell in range(pos_ref.shape[0]):
        pos = pos_ref[cell]
        hot = site_onehot(pos, count_ref[cell]).astype(jnp.bfloat16)
        first = pos.astype(jnp.bfloat16).astype(jnp.float32)
        left = pos - first
        second = left.astype(jnp.bfloat16).astype(jnp.float32)
        third = left - second
        kind = kind_ref[cell : cell + 1].astype(jnp.float32)
        for g in range(8):
            parts_ref[cell, 16 * g : 16 * g + 3] = first
            parts_ref[cell, 16 * g + 3 : 16 * g + 6] = second
            parts_ref[cell, 16 * g + 6 : 16 * g + 9] = third
            parts_ref[cell, 16 * g + 9 : 16 * g + 10] = kind
            parts_ref[cell, 16 * g + 10 : 16 * g + 11] = jnp.ones_like(kind)
        msg_ref[cell, :SLOTS] = dot(hot, feat_ref[cell], NN).astype(jnp.bfloat16)
        spread = dot(hot, parts_ref[cell].astype(jnp.bfloat16), NT)
        extra = jnp.zeros((EXTRA, CHAN), jnp.float32)
        for g in range(8):
            extra = extra + jnp.where(group == g, spread[8 * g : 8 * g + 8], 0.0)
        msg_ref[cell, SLOTS:] = extra.astype(jnp.bfloat16)


def column_base(x, y):
    return (x * 8 + y) * RUN


def main_kernel(
    own_ref, xl_ref, xh_ref, yl_ref, yh_ref, zl_ref, zh_ref,
    off_ref, pick_ref, spread_ref, rw_ref, coup_ref, mix_ref, hid_ref, ow_ref,
    mid_ref, zlo_ref, zho_ref, energy_ref,
    feat_ext, pos_ext, feat_win, pos_win, edges, saved, sums, d_sums, d_half, d_far,
):
    group8 = lane_group(8)

    def place(ref, cell, cx, cy, cz):
        for cc in range(4):
            base = column_base(2 * cx + cc // 2, 2 * cy + cc % 2) + cz * COLROWS
            base = base if isinstance(base, int) else pl.multiple_of(base, 16)
            feat_ext[pl.ds(base, COLROWS)] = ref[cell, COLROWS * cc : COLROWS * cc + COLROWS].astype(jnp.float32)
            scalars = ref[cell, SLOTS:].astype(jnp.float32)
            for h in range(2):
                pos_ext[pl.ds(base + 8 * h, 8)] = jnp.where(group8 == 2 * cc + h, scalars, 0.0)

    for cell in range(4):
        place(own_ref, cell, 1 + cell // 2, 1 + cell % 2, 1)
        place(yl_ref, cell, cell, 0, 1)
        place(yh_ref, cell, cell, 3, 1)
    for cell in range(2):
        place(xl_ref, cell, 0, 1 + cell, 1)
        place(xh_ref, cell, 3, 1 + cell, 1)

    def place_z(cell, carry):
        place(zl_ref, cell, cell // 4, cell % 4, 0)
        place(zh_ref, cell, cell // 4, cell % 4, 2)
        return carry

    lax.fori_loop(0, 16, place_z, 0)

    lane = lax.broadcasted_iota(jnp.int32, (COLROWS, CHAN), 1) & 15
    pick = pick_ref[...].astype(jnp.bfloat16)
    amp = float(np.sqrt(2.0 / CUTOFF))
    root3 = float(np.sqrt(3.0))

    def own_scalar(rows, lanes):
        return jnp.sum(jnp.where(lanes, rows, 0.0), axis=1, keepdims=True)

    def forward(g, carry):
        gx, gy = g // 4 + 2, g % 4 + 2
        base = column_base(gx, gy)
        for a, b, first, count, at in WINDOW:
            start = base + (a * 8 + b) * RUN + first
            feat_win[g, at : at + count] = feat_ext[pl.ds(start, count)].astype(jnp.bfloat16)
            pos_win[at : at + count] = pos_ext[pl.ds(start, count)].astype(jnp.bfloat16)
        feat_win[g, USED:] = jnp.zeros((NJ - USED, CHAN), jnp.bfloat16)
        pos_win[USED:] = jnp.zeros((NJ - USED, CHAN), jnp.bfloat16)
        own = pos_ext[pl.ds(pl.multiple_of(base + COLROWS, 16), COLROWS)]
        parity = (gx & 1) * 2 + (gy & 1)
        far = dot(pick, pos_win[...], NT) + off_ref[parity]
        coords = [
            own_scalar(own, (lane == c) | (lane == 3 + c) | (lane == 6 + c)) for c in range(3)
        ]
        for t in range(NJ // TILE):
            at = slice(t * TILE, t * TILE + TILE)
            dx, dy, dz = (far[c : c + 1, at] - coords[c] for c in range(3))
            square = dx * dx + dy * dy + dz * dz
            clear = jnp.maximum(square, 0.25)
            inv = lax.rsqrt(clear)
            u = jnp.minimum(clear * inv * (1.0 / CUTOFF), 1.0)
            inside = (square >= 0.25) & (square < CUTOFF * CUTOFF)
            v = u - 0.5
            v2 = v * v
            sine = horner(COS_C, v2)
            cosine = -(horner(SIN_C, v2) * v)
            u2 = u * u
            u4 = u2 * u2
            u5 = u4 * u
            env = 1.0 + u4 * u2 * (u * (48.0 - 21.0 * u) - 28.0)
            env = jnp.where(inside, env, 0.0)
            slope = (-168.0 / CUTOFF) * u5 * ((1.0 - u) * (1.0 - u))
            slope = jnp.where(inside, slope, 0.0) - env * inv
            ux, uy, uz = dx * inv, dy * inv, dz * inv
            saved[g, 0, :, at] = ux
            saved[g, 1, :, at] = uy
            saved[g, 2, :, at] = uz
            saved[g, 3, :, at] = inv
            saved[g, 4, :, at] = sine
            saved[g, 5, :, at] = cosine
            saved[g, 6, :, at] = env
            saved[g, 7, :, at] = slope
            yx, yy, yz = root3 * ux, root3 * uy, root3 * uz
            twice = 2.0 * cosine
            before = jnp.zeros_like(env)
            radial = amp * sine * inv * env
            for b in range(NB):
                r0 = b * 4 * COLROWS
                edges[g, r0 : r0 + 16, at] = radial.astype(jnp.bfloat16)
                edges[g, r0 + 16 : r0 + 32, at] = (radial * yx).astype(jnp.bfloat16)
                edges[g, r0 + 32 : r0 + 48, at] = (radial * yy).astype(jnp.bfloat16)
                edges[g, r0 + 48 : r0 + 64, at] = (radial * yz).astype(jnp.bfloat16)
                before, radial = radial, twice * radial - before
        summed = dot(edges[g], feat_win[g], NN)
        for m in range(4):
            total = jnp.zeros((COLROWS, CHAN), jnp.float32)
            for b in range(NB):
                r0 = (b * 4 + m) * COLROWS
                total = total + rw_ref[min(m, 1), b : b + 1] * summed[r0 : r0 + 16]
            sums[m, pl.ds(pl.multiple_of(g * COLROWS, 16), COLROWS)] = total
        return carry

    lax.fori_loop(0, 16, forward, 0)

    high = lax.Precision.HIGHEST
    head = dot(mix_ref[...], hid_ref[...], NN, high)
    ow = ow_ref[...]

    def readout(k, carry):
        kinds, occs = [], []
        for s in range(4):
            g = k * 4 + s
            start = column_base(g // 4 + 2, g % 4 + 2) + COLROWS
            own = pos_ext[pl.ds(pl.multiple_of(start, 16), COLROWS)]
            kinds.append(own_scalar(own, lane == 9))
            occs.append(own_scalar(own, lane == 10))
        kind = jnp.concatenate(kinds, axis=0)
        occ = jnp.concatenate(occs, axis=0)
        rows = pl.ds(pl.multiple_of(k * 64, 64), 64)
        scalar = sums[0, rows]
        vectors = [sums[m, rows] for m in (1, 2, 3)]
        weights = []
        for q in range(3):
            w = jnp.zeros((64, CHAN), jnp.float32)
            for s in range(coup_ref.shape[1]):
                w = jnp.where(kind == float(s), coup_ref[q, s : s + 1], w)
            weights.append(w)
        length = vectors[0] * vectors[0] + vectors[1] * vectors[1] + vectors[2] * vectors[2]
        product = weights[0] * scalar + weights[1] * scalar * scalar + weights[2] * length
        hidden = dot(product, head, NN, high)
        logistic = jax.nn.sigmoid(hidden)
        energy = occ * jnp.sum(ow * hidden * logistic, axis=1, keepdims=True)
        energy_ref[rows] = jnp.broadcast_to(energy, (64, CHAN))
        d_hidden = occ * ow * logistic * (1.0 + hidden * (1.0 - logistic))
        d_product = dot(d_hidden, head, NT, high)
        d_sums[0, rows] = d_product * (weights[0] + 2.0 * weights[1] * scalar)
        for m in range(3):
            d_sums[m + 1, rows] = 2.0 * weights[2] * vectors[m] * d_product
        return carry

    lax.fori_loop(0, 4, readout, 0)

    feat_ext[...] = jnp.zeros_like(feat_ext)
    d_pos = pos_ext
    d_pos[...] = jnp.zeros_like(d_pos)
    spread = spread_ref[...].astype(jnp.bfloat16)
    d_far[...] = jnp.zeros_like(d_far)

    def backward(g, carry):
        base = column_base(g // 4 + 2, g % 4 + 2)
        rows = pl.ds(pl.multiple_of(g * COLROWS, 16), COLROWS)
        for m in range(4):
            d_sum = d_sums[m, rows]
            for b in range(NB):
                r0 = (b * 4 + m) * COLROWS
                d_half[r0 : r0 + 16] = (rw_ref[min(m, 1), b : b + 1] * d_sum).astype(jnp.bfloat16)
        totals = [jnp.zeros((COLROWS, TILE), jnp.float32)] * 3
        for t in range(NJ // TILE):
            at = slice(t * TILE, t * TILE + TILE)
            d_edge = dot(d_half[...], feat_win[g, at], NT)
            ux, uy, uz, inv, sine, cosine, env, slope = (saved[g, k, :, at] for k in range(8))
            yx, yy, yz = root3 * ux, root3 * uy, root3 * uz
            twice = 2.0 * cosine
            s_old, s_now = jnp.zeros_like(sine), sine
            c_old, c_now = jnp.ones_like(sine), cosine
            s_sum, c_sum = 0.0, 0.0
            grads = [0.0, 0.0, 0.0]
            for b in range(NB):
                r0 = b * 4 * COLROWS
                e0, e1, e2, e3 = (d_edge[r0 + 16 * m : r0 + 16 * m + 16] for m in range(4))
                w = e0 + yx * e1 + yy * e2 + yz * e3
                s_sum = s_sum + w * s_now
                c_sum = c_sum + w * (c_now * float(b + 1))
                grads = [grads[0] + e1 * s_now, grads[1] + e2 * s_now, grads[2] + e3 * s_now]
                if b + 1 < NB:
                    s_old, s_now = s_now, twice * s_now - s_old
                    c_old, c_now = c_now, twice * c_now - c_old
            scale = amp * inv
            along = scale * (float(np.pi / CUTOFF) * env * c_sum + slope * s_sum)
            across = (root3 * scale) * env * inv
            inner = grads[0] * ux + grads[1] * uy + grads[2] * uz
            along = along - across * inner
            ds = [along * ux + across * grads[0], along * uy + across * grads[1], along * uz + across * grads[2]]
            for c in range(3):
                totals[c] = totals[c] + ds[c]
                column = jnp.sum(ds[c], axis=0, keepdims=True)
                hi = column.astype(jnp.bfloat16)
                d_far[c : c + 1, at] = hi
                d_far[3 + c : 4 + c, at] = (column - hi.astype(jnp.float32)).astype(jnp.bfloat16)
        d_feat = dot(edges[g], d_half[...], TN)
        d_spread = dot(d_far[...], spread, TN)
        for a, b, first, count, at in WINDOW:
            start = pl.ds(base + (a * 8 + b) * RUN + first, count)
            feat_ext[start] = feat_ext[start] + d_feat[at : at + count]
            d_pos[start] = d_pos[start] + d_spread[at : at + count]
        mine = pl.ds(pl.multiple_of(base + COLROWS, 16), COLROWS)
        back = jnp.zeros((COLROWS, CHAN), jnp.float32)
        for c in range(3):
            back = jnp.where(lane == c, jnp.sum(totals[c], axis=1, keepdims=True), back)
        d_pos[mine] = d_pos[mine] - back
        return carry

    lax.fori_loop(0, 16, backward, 0)

    def collect(cell, carry):
        for cz, out in ((0, zlo_ref), (1, mid_ref), (2, zho_ref)):
            scalars = jnp.zeros((EXTRA, CHAN), jnp.float32)
            for cc in range(4):
                base = column_base(2 * (cell // 4) + cc // 2, 2 * (cell % 4) + cc % 2) + cz * COLROWS
                base = pl.multiple_of(base, 16)
                out[cell, COLROWS * cc : COLROWS * cc + COLROWS] = feat_ext[pl.ds(base, COLROWS)].astype(out.dtype)
                for h in range(2):
                    scalars = scalars + jnp.where(group8 == 2 * cc + h, d_pos[pl.ds(base + 8 * h, 8)], 0.0)
            out[cell, SLOTS:] = scalars.astype(out.dtype)
        return carry

    lax.fori_loop(0, 16, collect, 0)


def finish_kernel(count_ref, pos_ref, mid_ref, low_ref, high_ref, energy_ref, e_ref, f_ref, g_ref):
    for cell in range(4):
        hot = site_onehot(pos_ref[cell], count_ref[cell]).astype(jnp.float32)
        arrived = low_ref[cell] if cell < 2 else high_ref[cell - 2]
        total = mid_ref[cell] + arrived.astype(jnp.float32)
        turned = hot.T.astype(jnp.bfloat16)
        rest = total[:SLOTS]
        grad = jnp.zeros((SLOTS, CHAN), jnp.float32)
        for _ in range(3):
            piece = rest.astype(jnp.bfloat16)
            grad = grad + dot(turned, piece, NN)
            rest = rest - piece.astype(jnp.float32)
        g_ref[cell] = grad
        lane = lax.broadcasted_iota(jnp.int32, (EXTRA, CHAN), 1)
        for c in range(3):
            column = jnp.concatenate(
                [
                    jnp.sum(jnp.where(lane == 16 * g + c, total[SLOTS:], 0.0), axis=1, keepdims=True)
                    for g in range(8)
                ],
                axis=0,
            )
            f_ref[cell, c : c + 1] = -jnp.sum(hot * column, axis=0, keepdims=True)
        pieces = []
        for cc in range(4):
            g = (2 * (cell // 2) + cc // 2) * 4 + 2 * (cell % 2) + cc % 2
            pieces.append(energy_ref[g * COLROWS : g * COLROWS + COLROWS, 0:1])
        e_ref[cell : cell + 1] = jnp.sum(hot * jnp.concatenate(pieces, axis=0), axis=0, keepdims=True)


SMEM = pl.BlockSpec(memory_space=pltpu.SMEM)
VMEM = pl.BlockSpec(memory_space=pltpu.VMEM)


def shifted(low_part, high_part, axis):
    count = lax.axis_size(axis)
    up = [(i, (i + 1) % count) for i in range(count)]
    down = [(target, source) for source, target in up]
    from_below = lax.ppermute(high_part, axis, up)
    from_above = lax.ppermute(low_part, axis, down)
    return from_below, from_above


def body(local_pos, counts, species, features, radial_weights, coupling, mixing, hidden_weights, output_weights):
    cells = 4
    pos = local_pos.reshape(cells, 3, SLOTS)
    count = counts.reshape(cells)
    bf16, f32 = jnp.bfloat16, jnp.float32
    own = pl.pallas_call(
        sort_kernel,
        name="sort",
        out_shape=jax.ShapeDtypeStruct((cells, ROWS, CHAN), bf16),
        in_specs=[SMEM, VMEM, VMEM, VMEM],
        out_specs=VMEM,
        scratch_shapes=[pltpu.VMEM((cells, CHAN, SLOTS), f32)],
    )(count, pos, species.reshape(cells, SLOTS), features.reshape(cells, SLOTS, CHAN))
    block = own.reshape(2, 2, ROWS, CHAN)
    xl, xh = shifted(block[:1], block[1:], "gx")
    wide = jnp.concatenate([xl, block, xh], axis=0)
    yl, yh = shifted(wide[:, :1], wide[:, 1:], "gy")
    layer = jnp.concatenate([yl, wide, yh], axis=1)
    zl, zh = shifted(layer, layer, "gz")

    sixteen = jax.ShapeDtypeStruct((16, ROWS, CHAN), bf16)
    mid, z_low, z_high, energy = pl.pallas_call(
        main_kernel,
        name="pairs",
        out_shape=(
            jax.ShapeDtypeStruct((16, ROWS, CHAN), f32),
            sixteen,
            sixteen,
            jax.ShapeDtypeStruct((16 * COLROWS, CHAN), f32),
        ),
        in_specs=[VMEM] * 15,
        out_specs=(VMEM,) * 4,
        scratch_shapes=[
            pltpu.VMEM((64 * RUN, CHAN), f32),
            pltpu.VMEM((64 * RUN, CHAN), f32),
            pltpu.VMEM((16, NJ, CHAN), bf16),
            pltpu.VMEM((NJ, CHAN), bf16),
            pltpu.VMEM((16, 4 * NB * COLROWS, NJ), bf16),
            pltpu.VMEM((16, 8, COLROWS, NJ), f32),
            pltpu.VMEM((4, 16 * COLROWS, CHAN), f32),
            pltpu.VMEM((4, 16 * COLROWS, CHAN), f32),
            pltpu.VMEM((4 * NB * COLROWS, CHAN), bf16),
            pltpu.VMEM((16, NJ), bf16),
        ],
        compiler_params=pltpu.CompilerParams(vmem_limit_bytes=56 << 20),
    )(
        own,
        xl.reshape(2, ROWS, CHAN),
        xh.reshape(2, ROWS, CHAN),
        yl.reshape(4, ROWS, CHAN),
        yh.reshape(4, ROWS, CHAN),
        zl.reshape(16, ROWS, CHAN),
        zh.reshape(16, ROWS, CHAN),
        jnp.asarray(offset_table()),
        jnp.asarray(pick_table()),
        jnp.asarray(spread_table()),
        radial_weights,
        coupling,
        mixing,
        hidden_weights,
        output_weights.reshape(1, -1),
    )
    from_below, from_above = shifted(z_low, z_high, "gz")
    plane = (mid + from_below.astype(f32) + from_above.astype(f32)).reshape(4, 4, ROWS, CHAN)
    from_below, from_above = shifted(plane[:, :1].astype(bf16), plane[:, 3:].astype(bf16), "gy")
    rows = plane[:, 1:3] + jnp.concatenate([from_below, from_above], axis=1).astype(f32)
    from_below, from_above = shifted(rows[:1].astype(bf16), rows[3:].astype(bf16), "gx")
    atom_energy, forces, feature_grad = pl.pallas_call(
        finish_kernel,
        name="finish",
        out_shape=(
            jax.ShapeDtypeStruct((cells, SLOTS), f32),
            jax.ShapeDtypeStruct((cells, 3, SLOTS), f32),
            jax.ShapeDtypeStruct((cells, SLOTS, CHAN), f32),
        ),
        in_specs=[SMEM] + [VMEM] * 5,
        out_specs=(VMEM,) * 3,
    )(
        count,
        pos,
        rows[1:3].reshape(cells, ROWS, CHAN),
        from_below.reshape(2, ROWS, CHAN),
        from_above.reshape(2, ROWS, CHAN),
        energy,
    )
    return (
        atom_energy.reshape(species.shape),
        forces.reshape(local_pos.shape),
        feature_grad.reshape(features.shape),
    )


def solution(mesh):
    placed = (
        P("gx", "gy", "gz", None, None),
        P("gx", "gy", "gz"),
        P("gx", "gy", "gz", None),
        P("gx", "gy", "gz", None, None),
        P(),
        P(),
        P(),
        P(),
        P(),
    )
    return jax.shard_map(
        body,
        mesh=mesh,
        in_specs=placed,
        out_specs=(
            P("gx", "gy", "gz", None),
            P("gx", "gy", "gz", None, None),
            P("gx", "gy", "gz", None, None),
        ),
        check_vma=False,
    )
```

profile of v0, /device:TPU:1, one launch (start us, length us, event | category | flops | bytes accessed | tf_op | source)
XLA Modules:
  0.0 97.3 jit_solution(8988921749018418121)
XLA Ops:
  0.6 0.0 copy-start.9
  0.6 0.5 broadcast.3
  1.2 1.3 %reduce.3 = s32[2,2]{1,0:T(2,128)S(1)} reduce(s32[2,2,1]{1,2,0:T(1,128)} %param.13, s32[]{:T(128)} %broadcast.3), dimensions={2}, to_apply=%param.13.reduce_sub_computation.3 | reduce | bytes 36 | tf_op args[1]
  2.5 0.6 reshape.65.count_ref
  3.1 0.0 copy-done.9
  3.1 0.6 copy.29.pos_ref
  3.7 1.8 %sort.1.own_ref = bf16[4,72,128]{2,1,0:T(8,128)(2,1)} custom-call(s32[4]{0:T(128)} %reshape.65.count_ref, f32[4,3,64]{2,1,0:T(4,128)} %copy.29.pos_ref, s32[4,64]{1,0:T(4,128)} %bitcast.42, bf16[4,64,128]{2,1,0:T(8,128)(2,1)} %bitcast.37), custom_call_target="tpu_custom_call" | custom-call | tf_op jit(solution)/shard_map/sort/pallas_call | solution.py:404
  5.5 0.8 slice_bitcast_fusion
  6.3 0.0 copy-start
  6.3 3.8 %collective-permute-start = (bf16[1,2,72,128]{3,2,0,1:T(8,128)(2,1)S(1)}, bf16[1,2,72,128]{3,2,0,1:T(8,128)(2,1)S(1)}, u32[]{:S(2)}, u32[]{:S(2)}) collective-permute-start(bf16[1,2,72,128]{3,2,0,1:T(8,128)(2,1)S(1)} %get-tuple-element.32), channel_id=1, source_target_pairs={{0,32},{32,64},{64,96},{96,128},{128,160},{160,192},{192,224},{224... | collective-permute-start | bytes 110600 | tf_op jit(solution)/shard_map/ppermute | solution.py:394
  10.1 2.3 %collective-permute-start.1 = (bf16[1,2,72,128]{3,2,0,1:T(8,128)(2,1)S(1)}, bf16[1,2,72,128]{3,2,0,1:T(8,128)(2,1)S(1)}, u32[]{:S(2)}, u32[]{:S(2)}) collective-permute-start(bf16[1,2,72,128]{3,2,0,1:T(8,128)(2,1)S(1)} %get-tuple-element.31), channel_id=1, source_target_pairs={{32,0},{64,32},{96,64},{128,96},{160,128},{192,160},{224,192},{0,2... | collective-permute-start | bytes 110600 | tf_op jit(solution)/shard_map/ppermute | solution.py:395
  12.4 1.3 %collective-permute-done = bf16[1,2,72,128]{3,2,0,1:T(8,128)(2,1)S(1)} collective-permute-done((bf16[1,2,72,128]{3,2,0,1:T(8,128)(2,1)S(1)}, bf16[1,2,72,128]{3,2,0,1:T(8,128)(2,1)S(1)}, u32[]{:S(2)}, u32[]{:S(2)}) %collective-permute-start) | collective-permute-done | bytes 36896 | tf_op jit(solution)/shard_map/ppermute | solution.py:394
  13.6 0.0 copy-start.3
  13.6 0.6 copy-done.3
  14.2 0.0 copy-done
  14.3 0.1 collective-permute-done.1
  14.4 0.0 copy-start.4
  14.4 0.6 copy-done.4
  15.0 3.4 %collective-permute-start.3 = (bf16[4,1,72,128]{3,2,0,1:T(8,128)(2,1)S(1)}, bf16[4,1,72,128]{3,2,0,1:T(8,128)(2,1)S(1)}, u32[]{:S(2)}, u32[]{:S(2)}) collective-permute-start(bf16[4,1,72,128]{3,2,0,1:T(8,128)(2,1)S(1)} %get-tuple-element.29), channel_id=1, source_target_pairs={{8,0},{16,8},{24,16},{0,24},{9,1},{17,9},{25,17},{1,25},{10,2},{18... | collective-permute-start | bytes 221192 | tf_op jit(solution)/shard_map/ppermute | solution.py:395
  18.5 0.0 copy-start.7
  18.5 0.0 collective-permute-start.2
  18.5 1.5 %collective-permute-done.3 = bf16[4,1,72,128]{3,2,0,1:T(8,128)(2,1)S(1)} collective-permute-done((bf16[4,1,72,128]{3,2,0,1:T(8,128)(2,1)S(1)}, bf16[4,1,72,128]{3,2,0,1:T(8,128)(2,1)S(1)}, u32[]{:S(2)}, u32[]{:S(2)}) %collective-permute-start.3) | collective-permute-done | bytes 73760 | tf_op jit(solution)/shard_map/ppermute | solution.py:395
  20.0 0.0 copy-start.1
  20.0 0.4 collective-permute-done.2
  20.4 0.0 copy-start.2
  20.4 0.2 copy-done.1
  20.6 0.4 copy-done.2
  21.0 0.0 copy-start.8
  21.0 5.9 %collective-permute-start.5 = (bf16[4,4,72,128]{3,2,0,1:T(8,128)(2,1)S(1)}, bf16[4,4,72,128]{3,2,0,1:T(8,128)(2,1)S(1)}, u32[]{:S(2)}, u32[]{:S(2)}) collective-permute-start(bf16[4,4,72,128]{3,2,0,1:T(8,128)(2,1)S(1)} %pad_maximum_fusion), channel_id=1, source_target_pairs={{1,0},{2,1},{3,2},{4,3},{5,4},{6,5},{7,6},{0,7},{9,8},{10,9},{11,1... | collective-permute-start | bytes 884744 | tf_op jit(solution)/shard_map/ppermute | solution.py:395
  26.9 0.0 collective-permute-start.4
  26.9 0.0 copy-done.7
  26.9 0.6 copy.27.coup_ref
  27.6 0.0 copy-done.8
  27.6 0.7 copy.28.hid_ref
  28.3 4.3 %collective-permute-done.5 = bf16[4,4,72,128]{3,2,0,1:T(8,128)(2,1)S(1)} collective-permute-done((bf16[4,4,72,128]{3,2,0,1:T(8,128)(2,1)S(1)}, bf16[4,4,72,128]{3,2,0,1:T(8,128)(2,1)S(1)}, u32[]{:S(2)}, u32[]{:S(2)}) %collective-permute-start.5) | collective-permute-done | bytes 294944 | tf_op jit(solution)/shard_map/ppermute | solution.py:395
  32.6 0.7 copy.26
  33.3 2.4 %collective-permute-done.4 = bf16[4,4,72,128]{3,2,0,1:T(8,128)(2,1)S(1)} collective-permute-done((bf16[4,4,72,128]{3,2,0,1:T(8,128)(2,1)S(1)}, bf16[4,4,72,128]{3,2,0,1:T(8,128)(2,1)S(1)}, u32[]{:S(2)}, u32[]{:S(2)}) %collective-permute-start.4) | collective-permute-done | bytes 294944 | tf_op jit(solution)/shard_map/ppermute | solution.py:394
  35.7 0.7 copy.25
  36.4 30.7 %pairs.1 = (f32[16,72,128]{2,1,0:T(8,128)}, bf16[16,72,128]{2,1,0:T(8,128)(2,1)}, bf16[16,72,128]{2,1,0:T(8,128)(2,1)}, f32[256,128]{1,0:T(8,128)}) custom-call(bf16[4,72,128]{2,1,0:T(8,128)(2,1)} %sort.1.own_ref, bf16[2,72,128]{2,1,0:T(8,128)(2,1)} %bitcast.35, bf16[2,72,128]{2,1,0:T(8,128)(2,1)} %bitcast.36, bf16[4,72,128]{2,1,0:T(8,128)(2,1)} %bitcast.34, ...), custom_call_target="tpu_custom_call" | custom-call | tf_op jit(solution)/shard_map/pairs/pallas_call | solution.py:420
  67.1 0.0 collective-permute-start.6
  67.2 2.7 %collective-permute-start.7 = (bf16[16,72,128]{2,1,0:T(8,128)(2,1)}, bf16[16,72,128]{2,1,0:T(8,128)(2,1)S(1)}, u32[]{:S(2)}, u32[]{:S(2)}) collective-permute-start(bf16[16,72,128]{2,1,0:T(8,128)(2,1)} %get-tuple-element.12), channel_id=1, source_target_pairs={{1,0},{2,1},{3,2},{4,3},{5,4},{6,5},{7,6},{0,7},{9,8},{10,9},{11,1... | collective-permute-start | bytes 884744 | tf_op jit(solution)/shard_map/ppermute | solution.py:395
  69.8 5.4 %collective-permute-done.6 = bf16[16,72,128]{2,1,0:T(8,128)(2,1)S(1)} collective-permute-done((bf16[16,72,128]{2,1,0:T(8,128)(2,1)}, bf16[16,72,128]{2,1,0:T(8,128)(2,1)S(1)}, u32[]{:S(2)}, u32[]{:S(2)}) %collective-permute-start.6) | collective-permute-done | bytes 294944 | tf_op jit(solution)/shard_map/ppermute | solution.py:394
  75.2 0.0 collective-permute-done.7
  75.2 1.1 %convert_add_fusion = f32[16,72,128]{2,1,0:T(8,128)S(1)} fusion(bf16[16,72,128]{2,1,0:T(8,128)(2,1)S(1)} %collective-permute-done.7, f32[16,72,128]{2,1,0:T(8,128)} %get-tuple-element.10, bf16[16,72,128]{2,1,0:T(8,128)(2,1)S(1)} %collective-permute-done.6), kind=kLoop, calls=%fused_computation | loop fusion | flops 589824 | bytes 1769472 | tf_op jit(solution)/shard_map/add | solution.py:462
  76.5 2.7 %collective-permute-start.8 = (bf16[4,1,72,128]{3,2,1,0:T(8,128)(2,1)S(1)}, bf16[4,1,72,128]{3,2,1,0:T(8,128)(2,1)S(1)}, u32[]{:S(2)}, u32[]{:S(2)}) collective-permute-start(bf16[4,1,72,128]{3,2,1,0:T(8,128)(2,1)S(1)} %get-tuple-element.25), channel_id=1, source_target_pairs={{0,8},{8,16},{16,24},{24,0},{1,9},{9,17},{17,25},{25,1},{2,10},{10... | collective-permute-start | bytes 221192 | tf_op jit(solution)/shard_map/ppermute | solution.py:394
  79.2 0.2 collective-permute-start.9
  79.4 1.2 %collective-permute-done.8 = bf16[4,1,72,128]{3,2,1,0:T(8,128)(2,1)S(1)} collective-permute-done((bf16[4,1,72,128]{3,2,1,0:T(8,128)(2,1)S(1)}, bf16[4,1,72,128]{3,2,1,0:T(8,128)(2,1)S(1)}, u32[]{:S(2)}, u32[]{:S(2)}) %collective-permute-start.8) | collective-permute-done | bytes 73760 | tf_op jit(solution)/shard_map/ppermute | solution.py:394
  80.6 2.6 %collective-permute-done.9 = bf16[4,1,72,128]{3,2,1,0:T(8,128)(2,1)S(1)} collective-permute-done((bf16[4,1,72,128]{3,2,1,0:T(8,128)(2,1)S(1)}, bf16[4,1,72,128]{3,2,1,0:T(8,128)(2,1)S(1)}, u32[]{:S(2)}, u32[]{:S(2)}) %collective-permute-start.9) | collective-permute-done | bytes 73760 | tf_op jit(solution)/shard_map/ppermute | solution.py:395
  83.2 0.1 fusion
  83.2 3.6 %collective-permute-start.11 = (bf16[1,2,72,128]{3,2,1,0:T(8,128)(2,1)S(1)}, bf16[1,2,72,128]{3,2,1,0:T(8,128)(2,1)S(1)}, u32[]{:S(2)}, u32[]{:S(2)}) collective-permute-start(bf16[1,2,72,128]{3,2,1,0:T(8,128)(2,1)S(1)} %get-tuple-element.27), channel_id=1, source_target_pairs={{32,0},{64,32},{96,64},{128,96},{160,128},{192,160},{224,192},{0,2... | collective-permute-start | bytes 110600 | tf_op jit(solution)/shard_map/ppermute | solution.py:395
  86.8 0.0 collective-permute-start.10
  86.8 0.7 slice.59
  87.5 0.4 collective-permute-done.11
  87.9 0.0 copy-start.5
  87.9 5.4 %collective-permute-done.10 = bf16[1,2,72,128]{3,2,1,0:T(8,128)(2,1)S(1)} collective-permute-done((bf16[1,2,72,128]{3,2,1,0:T(8,128)(2,1)S(1)}, bf16[1,2,72,128]{3,2,1,0:T(8,128)(2,1)S(1)}, u32[]{:S(2)}, u32[]{:S(2)}) %collective-permute-start.10) | collective-permute-done | bytes 36896 | tf_op jit(solution)/shard_map/ppermute | solution.py:394
  93.3 0.0 copy-start.6
  93.3 0.0 copy-done.5
  93.3 0.6 copy-done.6
  93.9 2.1 %finish.1 = (f32[4,64]{1,0:T(4,128)}, f32[4,3,64]{2,1,0:T(4,128)}, f32[4,64,128]{2,1,0:T(8,128)}) custom-call(s32[4]{0:T(128)} %reshape.65.count_ref, f32[4,3,64]{2,1,0:T(4,128)} %copy.29.pos_ref, f32[4,72,128]{2,1,0:T(8,128)} %bitcast.32, bf16[2,72,128]{2,1,0:T(8,128)(2,1)} %bitcast.39, bf16[2,72,128]{2,1,0:T(8,128)(2,1)} %bitcast.38, ...), custom_call_target="tpu_custom_call" | custom-call | tf_op jit(solution)/shard_map/finish/pallas_call | solution.py:466
  96.0 1.3 %copy.31 = f32[2,2,1,3,64]{4,2,3,1,0:T(1,128)} copy(f32[2,2,1,3,64]{4,3,1,0,2:T(4,128)} %bitcast.41) | data formatting | bytes 6144
  (9 shorter events, 0.1 us)
Async XLA Ops:
  0.6 2.5 %copy-start.9 = (f32[2,2,1,3,64]{4,2,3,1,0:T(1,128)S(1)}, f32[2,2,1,3,64]{4,2,3,1,0:T(1,128)}, u32[]{:S(2)}) copy-start(f32[2,2,1,3,64]{4,2,3,1,0:T(1,128)} %param.12) | copy-start | bytes 9220
  6.3 8.0 %copy-start = (bf16[4,72,128]{2,1,0:T(8,128)(2,1)S(1)}, bf16[4,72,128]{2,1,0:T(8,128)(2,1)}, u32[]{:S(2)}) copy-start(bf16[4,72,128]{2,1,0:T(8,128)(2,1)} %sort.1.own_ref) | copy-start | bytes 221188
  6.3 7.4 %collective-permute-start = (bf16[1,2,72,128]{3,2,0,1:T(8,128)(2,1)S(1)}, bf16[1,2,72,128]{3,2,0,1:T(8,128)(2,1)S(1)}, u32[]{:S(2)}, u32[]{:S(2)}) collective-permute-start(bf16[1,2,72,128]{3,2,0,1:T(8,128)(2,1)S(1)} %get-tuple-element.32), channel_id=1, source_target_pairs={{0,32},{32,64},{64,96},{96,128},{128,160},{160,192},{192,224},{224... | collective-permute-start | bytes 110600 | tf_op jit(solution)/shard_map/ppermute | solution.py:394
  10.1 4.3 %collective-permute-start.1 = (bf16[1,2,72,128]{3,2,0,1:T(8,128)(2,1)S(1)}, bf16[1,2,72,128]{3,2,0,1:T(8,128)(2,1)S(1)}, u32[]{:S(2)}, u32[]{:S(2)}) collective-permute-start(bf16[1,2,72,128]{3,2,0,1:T(8,128)(2,1)S(1)} %get-tuple-element.31), channel_id=1, source_target_pairs={{32,0},{64,32},{96,64},{128,96},{160,128},{192,160},{224,192},{0,2... | collective-permute-start | bytes 110600 | tf_op jit(solution)/shard_map/ppermute | solution.py:395
  13.6 0.6 copy-start.3
  14.4 0.6 copy-start.4
  15.0 5.0 %collective-permute-start.3 = (bf16[4,1,72,128]{3,2,0,1:T(8,128)(2,1)S(1)}, bf16[4,1,72,128]{3,2,0,1:T(8,128)(2,1)S(1)}, u32[]{:S(2)}, u32[]{:S(2)}) collective-permute-start(bf16[4,1,72,128]{3,2,0,1:T(8,128)(2,1)S(1)} %get-tuple-element.29), channel_id=1, source_target_pairs={{8,0},{16,8},{24,16},{0,24},{9,1},{17,9},{25,17},{1,25},{10,2},{18... | collective-permute-start | bytes 221192 | tf_op jit(solution)/shard_map/ppermute | solution.py:395
  18.5 8.5 %copy-start.7 = (f32[3,10,128]{2,0,1:T(4,128)S(1)}, f32[3,10,128]{2,0,1:T(4,128)}, u32[]{:S(2)}) copy-start(f32[3,10,128]{2,0,1:T(4,128)} %param.17) | copy-start | bytes 46084
  18.5 1.9 %collective-permute-start.2 = (bf16[4,1,72,128]{3,2,0,1:T(8,128)(2,1)S(1)}, bf16[4,1,72,128]{3,2,0,1:T(8,128)(2,1)S(1)}, u32[]{:S(2)}, u32[]{:S(2)}) collective-permute-start(bf16[4,1,72,128]{3,2,0,1:T(8,128)(2,1)S(1)} %get-tuple-element.30), channel_id=1, source_target_pairs={{0,8},{8,16},{16,24},{24,0},{1,9},{9,17},{17,25},{25,1},{2,10},{10... | collective-permute-start | bytes 221192 | tf_op jit(solution)/shard_map/ppermute | solution.py:394
  20.0 0.6 copy-start.1
  20.4 0.6 copy-start.2
  21.0 6.5 %copy-start.8 = (f32[128,16]{0,1:T(8,128)S(1)}, f32[128,16]{0,1:T(8,128)}, u32[]{:S(2)}) copy-start(f32[128,16]{0,1:T(8,128)} %param.19) | copy-start | bytes 24580
  21.0 11.5 %collective-permute-start.5 = (bf16[4,4,72,128]{3,2,0,1:T(8,128)(2,1)S(1)}, bf16[4,4,72,128]{3,2,0,1:T(8,128)(2,1)S(1)}, u32[]{:S(2)}, u32[]{:S(2)}) collective-permute-start(bf16[4,4,72,128]{3,2,0,1:T(8,128)(2,1)S(1)} %pad_maximum_fusion), channel_id=1, source_target_pairs={{1,0},{2,1},{3,2},{4,3},{5,4},{6,5},{7,6},{0,7},{9,8},{10,9},{11,1... | collective-permute-start | bytes 884744 | tf_op jit(solution)/shard_map/ppermute | solution.py:395
  26.9 8.7 %collective-permute-start.4 = (bf16[4,4,72,128]{3,2,0,1:T(8,128)(2,1)S(1)}, bf16[4,4,72,128]{3,2,0,1:T(8,128)(2,1)S(1)}, u32[]{:S(2)}, u32[]{:S(2)}) collective-permute-start(bf16[4,4,72,128]{3,2,0,1:T(8,128)(2,1)S(1)} %pad_maximum_fusion), channel_id=1, source_target_pairs={{0,1},{1,2},{2,3},{3,4},{4,5},{5,6},{6,7},{7,0},{8,9},{9,10},{10,1... | collective-permute-start | bytes 884744 | tf_op jit(solution)/shard_map/ppermute | solution.py:394
  67.1 8.1 %collective-permute-start.6 = (bf16[16,72,128]{2,1,0:T(8,128)(2,1)}, bf16[16,72,128]{2,1,0:T(8,128)(2,1)S(1)}, u32[]{:S(2)}, u32[]{:S(2)}) collective-permute-start(bf16[16,72,128]{2,1,0:T(8,128)(2,1)} %get-tuple-element.11), channel_id=1, source_target_pairs={{0,1},{1,2},{2,3},{3,4},{4,5},{5,6},{6,7},{7,0},{8,9},{9,10},{10,1... | collective-permute-start | bytes 884744 | tf_op jit(solution)/shard_map/ppermute | solution.py:394
  67.2 8.1 %collective-permute-start.7 = (bf16[16,72,128]{2,1,0:T(8,128)(2,1)}, bf16[16,72,128]{2,1,0:T(8,128)(2,1)S(1)}, u32[]{:S(2)}, u32[]{:S(2)}) collective-permute-start(bf16[16,72,128]{2,1,0:T(8,128)(2,1)} %get-tuple-element.12), channel_id=1, source_target_pairs={{1,0},{2,1},{3,2},{4,3},{5,4},{6,5},{7,6},{0,7},{9,8},{10,9},{11,1... | collective-permute-start | bytes 884744 | tf_op jit(solution)/shard_map/ppermute | solution.py:395
  76.5 4.1 %collective-permute-start.8 = (bf16[4,1,72,128]{3,2,1,0:T(8,128)(2,1)S(1)}, bf16[4,1,72,128]{3,2,1,0:T(8,128)(2,1)S(1)}, u32[]{:S(2)}, u32[]{:S(2)}) collective-permute-start(bf16[4,1,72,128]{3,2,1,0:T(8,128)(2,1)S(1)} %get-tuple-element.25), channel_id=1, source_target_pairs={{0,8},{8,16},{16,24},{24,0},{1,9},{9,17},{17,25},{25,1},{2,10},{10... | collective-permute-start | bytes 221192 | tf_op jit(solution)/shard_map/ppermute | solution.py:394
  79.2 4.0 %collective-permute-start.9 = (bf16[4,1,72,128]{3,2,1,0:T(8,128)(2,1)S(1)}, bf16[4,1,72,128]{3,2,1,0:T(8,128)(2,1)S(1)}, u32[]{:S(2)}, u32[]{:S(2)}) collective-permute-start(bf16[4,1,72,128]{3,2,1,0:T(8,128)(2,1)S(1)} %get-tuple-element.26), channel_id=1, source_target_pairs={{8,0},{16,8},{24,16},{0,24},{9,1},{17,9},{25,17},{1,25},{10,2},{18... | collective-permute-start | bytes 221192 | tf_op jit(solution)/shard_map/ppermute | solution.py:395
  83.2 4.7 %collective-permute-start.11 = (bf16[1,2,72,128]{3,2,1,0:T(8,128)(2,1)S(1)}, bf16[1,2,72,128]{3,2,1,0:T(8,128)(2,1)S(1)}, u32[]{:S(2)}, u32[]{:S(2)}) collective-permute-start(bf16[1,2,72,128]{3,2,1,0:T(8,128)(2,1)S(1)} %get-tuple-element.27), channel_id=1, source_target_pairs={{32,0},{64,32},{96,64},{128,96},{160,128},{192,160},{224,192},{0,2... | collective-permute-start | bytes 110600 | tf_op jit(solution)/shard_map/ppermute | solution.py:395
  86.8 6.4 %collective-permute-start.10 = (bf16[1,2,72,128]{3,2,1,0:T(8,128)(2,1)S(1)}, bf16[1,2,72,128]{3,2,1,0:T(8,128)(2,1)S(1)}, u32[]{:S(2)}, u32[]{:S(2)}) collective-permute-start(bf16[1,2,72,128]{3,2,1,0:T(8,128)(2,1)S(1)} %get-tuple-element.28), channel_id=1, source_target_pairs={{0,32},{32,64},{64,96},{96,128},{128,160},{160,192},{192,224},{224... | collective-permute-start | bytes 110600 | tf_op jit(solution)/shard_map/ppermute | solution.py:394
  87.9 5.4 %copy-start.5 = (bf16[1,2,72,128]{3,2,1,0:T(8,128)(2,1)}, bf16[1,2,72,128]{3,2,1,0:T(8,128)(2,1)S(1)}, u32[]{:S(2)}) copy-start(bf16[1,2,72,128]{3,2,1,0:T(8,128)(2,1)S(1)} %collective-permute-done.11) | copy-start | bytes 110596
  93.3 0.6 copy-start.6
where the time goes:
time: 98.4 us; the launch traced here: 97.3 us
  Pallas kernels  34.6 us (35%)
  waiting for transfers between devices  24.9 us (25%)
  starting transfers between devices  24.7 us (25%)
  local copies, waits for them, and re-layouts  9.75 us (10%)
  other arithmetic  2.61 us (3%)
    pallas_call x1, Pallas kernels, body(): pl.pallas_call(main_kernel, name='pairs', out_shape=(jax.ShapeDtypeStruct...  30.7 us
    ppermute x6, starting transfers between devices, shifted(): from_above = lax.ppermute(low_part, axis, down)  18.1 us
    ppermute x6, waiting for transfers between devices, shifted(): from_below = lax.ppermute(high_part, axis, up)  16 us
    ppermute x6, waiting for transfers between devices, shifted(): from_above = lax.ppermute(low_part, axis, down)  8.91 us
    ppermute x6, starting transfers between devices, shifted(): from_below = lax.ppermute(high_part, axis, up)  6.54 us
    unnamed x27, local copies, waits for them, and re-layouts  5.57 us
    pallas_call x1, Pallas kernels, body(): pl.pallas_call(finish_kernel, name='finish', out_shape=(jax.ShapeDtypeStr...  2.13 us
  transfers between devices with their start and end apart: 12, of which 11 were waited for; matrix products, arithmetic and copies ran while one was open for 3% of the time, Pallas kernels for 0%

commit v1 on v0

v1 whole, which is shorter than its diff:
```python
import functools

import jax
import jax.numpy as jnp
import numpy as np
from jax import lax
from jax.experimental import pallas as pl
from jax.experimental.pallas import tpu as pltpu
from jax.sharding import PartitionSpec as P

SIDE = 7.0
CUTOFF = 5.0
LAT = 4
SLOTS = LAT**3
NB = 8
CHAN = 128
EXTRA = 8
ROWS = SLOTS + EXTRA
COLROWS = 16
RUN = 3 * COLROWS
INNER = [(a, b) for a in (-1, 0, 1) for b in (-1, 0, 1)]
OUTER = [(a, b) for a in (-2, 2) for b in (-1, 0, 1)] + [(b, a) for a in (-2, 2) for b in (-1, 0, 1)]
NEAR, REST = [], []
_at = 0
for _a, _b in INNER + OUTER[:7]:
    NEAR.append((_a, _b, COLROWS, COLROWS, _at))
    _at += COLROWS
NJ_NEAR = _at
_at = 0
for _a, _b in OUTER[7:]:
    REST.append((_a, _b, COLROWS, COLROWS, _at))
    _at += COLROWS
for _first, _inner, _count in ((8, False, 8), (32, False, 8), (4, True, 12), (32, True, 12)):
    for _a, _b in INNER if _inner else OUTER:
        REST.append((_a, _b, _first, _count, _at))
        _at += _count
USED = _at
NJ_REST = 512
TILE = 128
FAR = 1000.0
GROUPS = 16
TERMS = 4 * NB * COLROWS


def offset_table(pieces, size):
    table = np.zeros((4, 8, size), np.float32)
    used = sum(piece[3] for piece in pieces)
    table[:, :3, used:] = FAR
    for parity in range(4):
        px, py = parity // 2, parity % 2
        for a, b, first, count, at in pieces:
            table[parity, 0, at : at + count] = SIDE * ((px + a) // 2)
            table[parity, 1, at : at + count] = SIDE * ((py + b) // 2)
            run = np.arange(first, first + count)
            table[parity, 2, at : at + count] = SIDE * (run // COLROWS - 1)
    return table


def pick_table():
    table = np.zeros((8, CHAN), np.float32)
    for group in range(8):
        for part in range(3):
            for comp in range(3):
                table[comp, 16 * group + 3 * part + comp] = 1.0
    return table


def spread_table():
    table = np.zeros((16, CHAN), np.float32)
    for group in range(8):
        for part in range(2):
            for comp in range(3):
                table[3 * part + comp, 16 * group + comp] = 1.0
    return table


def poly_coeffs():
    v = 0.5 * np.cos(np.pi * (np.arange(400) + 0.5) / 400)
    sines = np.polynomial.polynomial.polyfit(v * v, np.sin(np.pi * v) / v, 5)
    cosines = np.polynomial.polynomial.polyfit(v * v, np.cos(np.pi * v), 6)
    return [float(c) for c in sines], [float(c) for c in cosines]


SIN_C, COS_C = poly_coeffs()


def horner(coeffs, x):
    value = coeffs[-1] * x + coeffs[-2]
    for c in coeffs[-3::-1]:
        value = value * x + c
    return value


def dot(a, b, dims, precision=None):
    return lax.dot_general(a, b, (dims, ((), ())), preferred_element_type=jnp.float32, precision=precision)


NN = ((1,), (0,))
NT = ((1,), (1,))
TN = ((0,), (0,))


def site_onehot(pos, count):
    sx, sy, sz = (jnp.clip(jnp.floor(p * (LAT / SIDE)).astype(jnp.int32), 0, LAT - 1) for p in pos)
    row = (((sx >> 1) * 2 + (sy >> 1)) * 4 + sz) * 4 + (sx & 1) * 2 + (sy & 1)
    slot = lax.broadcasted_iota(jnp.int32, (1, SLOTS), 1)
    row = jnp.where(slot < count, row, -1)
    return lax.broadcasted_iota(jnp.int32, (SLOTS, SLOTS), 0) == row


def lane_group(rows):
    return lax.broadcasted_iota(jnp.int32, (rows, CHAN), 1) >> 4


def sort_kernel(count_hbm, pos_hbm, kind_hbm, feat_hbm, low_ref, high_ref, parts_ref, count_ref, pos_ref, kind_ref, feat_ref, sem):
    copies = [
        pltpu.make_async_copy(source, target, sem.at[k])
        for k, (source, target) in enumerate(
            ((count_hbm, count_ref), (pos_hbm, pos_ref), (kind_hbm, kind_ref), (feat_hbm, feat_ref))
        )
    ]
    for copy in copies:
        copy.start()
    group = lane_group(EXTRA)
    parts_ref[...] = jnp.zeros_like(parts_ref)
    for copy in copies:
        copy.wait()
    for cell in range(4):
        x, y = cell // 2, cell % 2
        pos = [pos_ref[3 * cell + c] for c in range(3)]
        hot = site_onehot(pos, count_ref[x, 0, y]).astype(jnp.bfloat16)
        lines = []
        for left in pos:
            first = left.astype(jnp.bfloat16).astype(jnp.float32)
            left = left - first
            second = left.astype(jnp.bfloat16).astype(jnp.float32)
            lines.append((first, second, left - second))
        kind = kind_ref[cell].astype(jnp.float32)
        for g in range(8):
            for part in range(3):
                for c in range(3):
                    at = 16 * g + 3 * part + c
                    parts_ref[cell, at : at + 1] = lines[c][part]
            parts_ref[cell, 16 * g + 9 : 16 * g + 10] = kind
            parts_ref[cell, 16 * g + 10 : 16 * g + 11] = jnp.ones_like(kind)
        out = high_ref if x else low_ref
        out[y, :SLOTS] = dot(hot, feat_ref[cell], NN).astype(jnp.bfloat16)
        spread = dot(hot, parts_ref[cell].astype(jnp.bfloat16), NT)
        extra = jnp.zeros((EXTRA, CHAN), jnp.float32)
        for g in range(8):
            extra = extra + jnp.where(group == g, spread[8 * g : 8 * g + 8], 0.0)
        out[y, SLOTS:] = extra.astype(jnp.bfloat16)


def place(msg, cell, feat_ext, pos_ext, run, shift):
    group = lane_group(8)
    scalars = msg[cell, SLOTS:].astype(jnp.float32)
    for cc in range(4):
        x, y = 2 * (cell % 4) + cc // 2, 2 * (cell // 4) + cc % 2
        base = pl.multiple_of((x * 8 + y) * run + shift, COLROWS)
        feat_ext[pl.ds(base, COLROWS)] = msg[cell, COLROWS * cc : COLROWS * cc + COLROWS].astype(jnp.float32)
        for h in range(2):
            pos_ext[pl.ds(base + 8 * h, 8)] = jnp.where(group == 2 * cc + h, scalars, 0.0)


def column(g, run):
    return ((g // 4 + 2) * 8 + g % 4 + 2) * run


def own_scalar(rows, lanes):
    return jnp.sum(jnp.where(lanes, rows, 0.0), axis=1, keepdims=True)


def lane_kind():
    return lax.broadcasted_iota(jnp.int32, (COLROWS, CHAN), 1) & 15


AMP = float(np.sqrt(2.0 / CUTOFF))
ROOT3 = float(np.sqrt(3.0))


def take_window(g, pieces, run, skip, feat_ext, pos_ext, feat_win, pos_win):
    base = column(g, run)
    for a, b, first, count, at in pieces:
        start = base + (a * 8 + b) * run + first - skip
        feat_win[g, at : at + count] = feat_ext[pl.ds(start, count)].astype(jnp.bfloat16)
        pos_win[at : at + count] = pos_ext[pl.ds(start, count)].astype(jnp.bfloat16)
    own = pos_ext[pl.ds(pl.multiple_of(base + COLROWS - skip, COLROWS), COLROWS)]
    return own


def edge_columns(g, own, far, edges, saved, size):
    lane = lane_kind()
    coords = [own_scalar(own, (lane == c) | (lane == 3 + c) | (lane == 6 + c)) for c in range(3)]
    for t in range(size // TILE):
        at = slice(t * TILE, t * TILE + TILE)
        dx, dy, dz = (far[c : c + 1, at] - coords[c] for c in range(3))
        square = dx * dx + dy * dy + dz * dz
        clear = jnp.maximum(square, 0.25)
        inv = lax.rsqrt(clear)
        u = jnp.minimum(clear * inv * (1.0 / CUTOFF), 1.0)
        inside = (square >= 0.25) & (square < CUTOFF * CUTOFF)
        v = u - 0.5
        v2 = v * v
        sine = horner(COS_C, v2)
        cosine = -(horner(SIN_C, v2) * v)
        u2 = u * u
        u4 = u2 * u2
        u5 = u4 * u
        env = 1.0 + u4 * u2 * (u * (48.0 - 21.0 * u) - 28.0)
        env = jnp.where(inside, env, 0.0)
        slope = (-168.0 / CUTOFF) * u5 * ((1.0 - u) * (1.0 - u))
        slope = jnp.where(inside, slope, 0.0) - env * inv
        ux, uy, uz = dx * inv, dy * inv, dz * inv
        for k, value in enumerate((ux, uy, uz, inv, sine, cosine, env, slope)):
            saved[g, k, :, at] = value
        yx, yy, yz = ROOT3 * ux, ROOT3 * uy, ROOT3 * uz
        twice = 2.0 * cosine
        before = jnp.zeros_like(env)
        radial = AMP * sine * inv * env
        for b in range(NB):
            r0 = b * 4 * COLROWS
            edges[g, r0 : r0 + 16, at] = radial.astype(jnp.bfloat16)
            edges[g, r0 + 16 : r0 + 32, at] = (radial * yx).astype(jnp.bfloat16)
            edges[g, r0 + 32 : r0 + 48, at] = (radial * yy).astype(jnp.bfloat16)
            edges[g, r0 + 48 : r0 + 64, at] = (radial * yz).astype(jnp.bfloat16)
            before, radial = radial, twice * radial - before


def group_rows(g):
    return pl.ds(pl.multiple_of(g * COLROWS, COLROWS), COLROWS)


def contract(g, edges, feat_win, rw_ref, sums, start_ref=None):
    summed = dot(edges[g], feat_win[g], NN)
    rows = group_rows(g)
    for m in range(4):
        total = jnp.zeros((COLROWS, CHAN), jnp.float32) if start_ref is None else start_ref[m, rows]
        for b in range(NB):
            r0 = (b * 4 + m) * COLROWS
            total = total + rw_ref[min(m, 1), b : b + 1] * summed[r0 : r0 + 16]
        sums[m, rows] = total


def back_group(g, size, pieces, run, skip, edges, feat_win, saved, d_sums, rw_ref, spread, d_half, d_far, d_feat_ext, d_pos_ext):
    lane = lane_kind()
    base = column(g, run)
    rows = group_rows(g)
    for m in range(4):
        d_sum = d_sums[m, rows]
        for b in range(NB):
            r0 = (b * 4 + m) * COLROWS
            d_half[r0 : r0 + 16] = (rw_ref[min(m, 1), b : b + 1] * d_sum).astype(jnp.bfloat16)
    totals = [jnp.zeros((COLROWS, TILE), jnp.float32)] * 3
    for t in range(size // TILE):
        at = slice(t * TILE, t * TILE + TILE)
        d_edge = dot(d_half[...], feat_win[g, at], NT)
        ux, uy, uz, inv, sine, cosine, env, slope = (saved[g, k, :, at] for k in range(8))
        yx, yy, yz = ROOT3 * ux, ROOT3 * uy, ROOT3 * uz
        twice = 2.0 * cosine
        s_old, s_now = jnp.zeros_like(sine), sine
        c_old, c_now = jnp.ones_like(sine), cosine
        s_sum, c_sum = 0.0, 0.0
        grads = [0.0, 0.0, 0.0]
        for b in range(NB):
            r0 = b * 4 * COLROWS
            e0, e1, e2, e3 = (d_edge[r0 + 16 * m : r0 + 16 * m + 16] for m in range(4))
            w = e0 + yx * e1 + yy * e2 + yz * e3
            s_sum = s_sum + w * s_now
            c_sum = c_sum + w * (c_now * float(b + 1))
            grads = [grads[0] + e1 * s_now, grads[1] + e2 * s_now, grads[2] + e3 * s_now]
            if b + 1 < NB:
                s_old, s_now = s_now, twice * s_now - s_old
                c_old, c_now = c_now, twice * c_now - c_old
        scale = AMP * inv
        along = scale * (float(np.pi / CUTOFF) * env * c_sum + slope * s_sum)
        across = (ROOT3 * scale) * env * inv
        inner = grads[0] * ux + grads[1] * uy + grads[2] * uz
        along = along - across * inner
        ds = [along * ux + across * grads[0], along * uy + across * grads[1], along * uz + across * grads[2]]
        for c in range(3):
            totals[c] = totals[c] + ds[c]
            far_sum = jnp.sum(ds[c], axis=0, keepdims=True)
            hi = far_sum.astype(jnp.bfloat16)
            d_far[c : c + 1, at] = hi
            d_far[3 + c : 4 + c, at] = (far_sum - hi.astype(jnp.float32)).astype(jnp.bfloat16)
    d_feat = dot(edges[g], d_half[...], TN)
    d_spread = dot(d_far[...], spread, TN)
    for a, b, first, count, at in pieces:
        start = pl.ds(base + (a * 8 + b) * run + first - skip, count)
        d_feat_ext[start] = d_feat_ext[start] + d_feat[at : at + count]
        d_pos_ext[start] = d_pos_ext[start] + d_spread[at : at + count]
    mine = pl.ds(pl.multiple_of(base + COLROWS - skip, COLROWS), COLROWS)
    back = jnp.zeros((COLROWS, CHAN), jnp.float32)
    for c in range(3):
        back = jnp.where(lane == c, jnp.sum(totals[c], axis=1, keepdims=True), back)
    d_pos_ext[mine] = d_pos_ext[mine] - back


def collect(cell, outs, d_feat_ext, d_pos_ext, run):
    group = lane_group(8)
    for shift, out, more in outs:
        scalars = jnp.zeros((EXTRA, CHAN), jnp.float32)
        for cc in range(4):
            x, y = 2 * (cell % 4) + cc // 2, 2 * (cell // 4) + cc % 2
            base = pl.multiple_of((x * 8 + y) * run + shift, COLROWS)
            rows = d_feat_ext[pl.ds(base, COLROWS)]
            if more is not None:
                rows = rows + more[cell, COLROWS * cc : COLROWS * cc + COLROWS]
            out[cell, COLROWS * cc : COLROWS * cc + COLROWS] = rows.astype(out.dtype)
            for h in range(2):
                scalars = scalars + jnp.where(group == 2 * cc + h, d_pos_ext[pl.ds(base + 8 * h, 8)], 0.0)
        if more is not None:
            scalars = scalars + more[cell, SLOTS:]
        out[cell, SLOTS:] = scalars.astype(out.dtype)


def near_kernel(layer_ref, off_ref, pick_ref, rw_ref, sums, feat_win, edges, saved, feat_ext, pos_ext, pos_win):
    def spread_cell(cell, carry):
        place(layer_ref, cell, feat_ext, pos_ext, COLROWS, 0)
        return carry

    lax.fori_loop(0, 16, spread_cell, 0)
    pick = pick_ref[...].astype(jnp.bfloat16)

    def forward(k, carry):
        for g in (4 * k, 4 * k + 1, 4 * k + 2, 4 * k + 3):
            own = take_window(g, NEAR, COLROWS, COLROWS, feat_ext, pos_ext, feat_win, pos_win)
            parity = ((g // 4) & 1) * 2 + (g & 1)
            far = dot(pick, pos_win[...], NT) + off_ref[parity]
            edge_columns(g, own, far, edges, saved, NJ_NEAR)
        for g in (4 * k, 4 * k + 1, 4 * k + 2, 4 * k + 3):
            contract(g, edges, feat_win, rw_ref, sums)
        return carry

    lax.fori_loop(0, GROUPS // 4, forward, 0)


def rest_kernel(
    layer_ref, zl_ref, zh_ref, near_sums, off_ref, pick_ref, spread_ref, rw_ref, coup_ref, mix_ref, hid_ref, ow_ref,
    zlo_ref, zho_ref, mid_ref, energy_ref, d_sums,
    feat_ext, pos_ext, feat_win, pos_win, edges, saved, sums, d_half, d_far,
):
    def spread_cell(cell, carry):
        place(layer_ref, cell, feat_ext, pos_ext, RUN, COLROWS)
        place(zl_ref, cell, feat_ext, pos_ext, RUN, 0)
        place(zh_ref, cell, feat_ext, pos_ext, RUN, 2 * COLROWS)
        return carry

    lax.fori_loop(0, 16, spread_cell, 0)
    pick = pick_ref[...].astype(jnp.bfloat16)
    lane = lane_kind()
    pos_win[USED:] = jnp.zeros((NJ_REST - USED, CHAN), jnp.bfloat16)

    def forward(k, carry):
        for g in (4 * k, 4 * k + 1, 4 * k + 2, 4 * k + 3):
            own = take_window(g, REST, RUN, 0, feat_ext, pos_ext, feat_win, pos_win)
            feat_win[g, USED:] = jnp.zeros((NJ_REST - USED, CHAN), jnp.bfloat16)
            parity = ((g // 4) & 1) * 2 + (g & 1)
            far = dot(pick, pos_win[...], NT) + off_ref[parity]
            edge_columns(g, own, far, edges, saved, NJ_REST)
        for g in (4 * k, 4 * k + 1, 4 * k + 2, 4 * k + 3):
            contract(g, edges, feat_win, rw_ref, sums, near_sums)
        return carry

    lax.fori_loop(0, GROUPS // 4, forward, 0)

    high = lax.Precision.HIGHEST
    head = dot(mix_ref[...], hid_ref[...], NT, high)
    ow = ow_ref[...]

    def readout(k, carry):
        kinds, occs = [], []
        for s in range(4):
            start = column(k * 4 + s, RUN) + COLROWS
            own = pos_ext[pl.ds(pl.multiple_of(start, COLROWS), COLROWS)]
            kinds.append(own_scalar(own, lane == 9))
            occs.append(own_scalar(own, lane == 10))
        kind = jnp.concatenate(kinds, axis=0)
        occ = jnp.concatenate(occs, axis=0)
        rows = pl.ds(pl.multiple_of(k * 64, 64), 64)
        scalar = sums[0, rows]
        vectors = [sums[m, rows] for m in (1, 2, 3)]
        weights = []
        for q in range(3):
            w = jnp.zeros((64, CHAN), jnp.float32)
            for s in range(coup_ref.shape[0]):
                w = jnp.where(kind == float(s), coup_ref[s, q : q + 1], w)
            weights.append(w)
        length = vectors[0] * vectors[0] + vectors[1] * vectors[1] + vectors[2] * vectors[2]
        product = weights[0] * scalar + weights[1] * scalar * scalar + weights[2] * length
        hidden = dot(product, head, NN, high)
        logistic = jax.nn.sigmoid(hidden)
        energy = occ * jnp.sum(ow * hidden * logistic, axis=1, keepdims=True)
        energy_ref[rows] = jnp.broadcast_to(energy, (64, CHAN))
        d_hidden = occ * ow * logistic * (1.0 + hidden * (1.0 - logistic))
        d_product = dot(d_hidden, head, NT, high)
        d_sums[0, rows] = d_product * (weights[0] + 2.0 * weights[1] * scalar)
        for m in range(3):
            d_sums[m + 1, rows] = 2.0 * weights[2] * vectors[m] * d_product
        return carry

    lax.fori_loop(0, 4, readout, 0)

    def clear(c, carry):
        rows = pl.ds(pl.multiple_of(c * RUN, RUN), RUN)
        feat_ext[rows] = jnp.zeros((RUN, CHAN), jnp.float32)
        pos_ext[rows] = jnp.zeros((RUN, CHAN), jnp.float32)
        return carry

    lax.fori_loop(0, 64, clear, 0, unroll=2)
    d_far[...] = jnp.zeros_like(d_far)
    spread = spread_ref[...].astype(jnp.bfloat16)

    def backward(k, carry):
        for s in range(2):
            back_group(
                2 * k + s, NJ_REST, REST, RUN, 0, edges, feat_win, saved, d_sums, rw_ref, spread,
                d_half.at[s], d_far.at[s], feat_ext, pos_ext,
            )
        return carry

    lax.fori_loop(0, GROUPS // 2, backward, 0)

    def gather_cell(cell, carry):
        collect(cell, ((0, zlo_ref, None), (COLROWS, mid_ref, None), (2 * COLROWS, zho_ref, None)), feat_ext, pos_ext, RUN)
        return carry

    lax.fori_loop(0, 16, gather_cell, 0)


def near_back_kernel(
    edges, feat_win, saved, d_sums, rest_mid, spread_ref, rw_ref, mid_ref, feat_ext, pos_ext, d_half, d_far
):
    feat_ext[...] = jnp.zeros_like(feat_ext)
    pos_ext[...] = jnp.zeros_like(pos_ext)
    d_far[...] = jnp.zeros_like(d_far)
    spread = spread_ref[...].astype(jnp.bfloat16)

    def backward(k, carry):
        for s in range(2):
            back_group(
                2 * k + s, NJ_NEAR, NEAR, COLROWS, COLROWS, edges, feat_win, saved, d_sums, rw_ref, spread,
                d_half.at[s], d_far.at[s], feat_ext, pos_ext,
            )
        return carry

    lax.fori_loop(0, GROUPS // 2, backward, 0)

    def gather_cell(cell, carry):
        collect(cell, ((0, mid_ref, rest_mid),), feat_ext, pos_ext, COLROWS)
        return carry

    lax.fori_loop(0, 16, gather_cell, 0)


def finish_kernel(count_ref, pos_ref, mid_ref, low_ref, high_ref, energy_ref, e_ref, f_ref, g_ref):
    lane = lax.broadcasted_iota(jnp.int32, (EXTRA, CHAN), 1)
    for cell in range(4):
        x, y = cell // 2, cell % 2
        hot = site_onehot([pos_ref[3 * cell + c] for c in range(3)], count_ref[x, 0, y]).astype(jnp.float32)
        arrived = high_ref[y] if x else low_ref[y]
        total = mid_ref[y, 1 + x] + arrived.astype(jnp.float32)
        turned = hot.T.astype(jnp.bfloat16)
        rest = total[:SLOTS]
        grad = jnp.zeros((SLOTS, CHAN), jnp.float32)
        for _ in range(3):
            piece = rest.astype(jnp.bfloat16)
            grad = grad + dot(turned, piece, NN)
            rest = rest - piece.astype(jnp.float32)
        g_ref[cell] = grad
        for c in range(3):
            force = jnp.concatenate(
                [
                    jnp.sum(jnp.where(lane == 16 * g + c, total[SLOTS:], 0.0), axis=1, keepdims=True)
                    for g in range(8)
                ],
                axis=0,
            )
            f_ref[3 * cell + c] = -jnp.sum(hot * force, axis=0, keepdims=True)
        pieces = []
        for cc in range(4):
            g = (2 * x + cc // 2) * 4 + 2 * y + cc % 2
            pieces.append(energy_ref[g * COLROWS : g * COLROWS + COLROWS, 0:1])
        e_ref[cell] = jnp.sum(hot * jnp.concatenate(pieces, axis=0), axis=0, keepdims=True)


SMEM = pl.BlockSpec(memory_space=pltpu.SMEM)
VMEM = pl.BlockSpec(memory_space=pltpu.VMEM)
HBM = pl.BlockSpec(memory_space=pltpu.HBM)


NEAR_LIMIT = 12 << 10
REST_LIMIT = 30 << 10
SORT_LIMIT = 65000


def shifted(low_part, high_part, axis):
    count = lax.axis_size(axis)
    up = [(i, (i + 1) % count) for i in range(count)]
    down = [(target, source) for source, target in up]
    from_below = lax.ppermute(high_part, axis, up)
    from_above = lax.ppermute(low_part, axis, down)
    return from_below, from_above


def call(kernel, name, outs, scratch, ins, limit, flops, spaces=()):
    shapes = tuple(jax.ShapeDtypeStruct(*out) for out in outs)
    moved = sum(int(np.prod(out.shape)) * out.dtype.itemsize for out in shapes)
    return pl.pallas_call(
        kernel,
        name=name,
        out_shape=shapes,
        in_specs=[*spaces] + [VMEM] * (len(ins) - len(spaces)),
        out_specs=(VMEM,) * len(shapes),
        scratch_shapes=[pltpu.VMEM(*one) if isinstance(one, tuple) else one for one in scratch],
        compiler_params=pltpu.CompilerParams(vmem_limit_bytes=limit << 10),
        cost_estimate=pl.CostEstimate(flops=flops, bytes_accessed=moved, transcendentals=0),
    )(*ins)


def body(local_pos, counts, species, features, radial_weights, coupling, mixing, hidden_weights, output_weights):
    bf16, f32 = jnp.bfloat16, jnp.float32
    pos = local_pos.reshape(12, 1, SLOTS)
    count = counts.transpose(0, 2, 1)
    low, high = call(
        sort_kernel,
        "sort",
        [((2, ROWS, CHAN), bf16)] * 2,
        [
            pltpu.VMEM((4, CHAN, SLOTS), f32),
            pltpu.SMEM((2, 1, 2), jnp.int32),
            pltpu.VMEM((12, 1, SLOTS), f32),
            pltpu.VMEM((4, 1, SLOTS), jnp.int32),
            pltpu.VMEM((4, SLOTS, CHAN), bf16),
            pltpu.SemaphoreType.DMA((4,)),
        ],
        (count, pos, species.reshape(4, 1, SLOTS), features.reshape(4, SLOTS, CHAN)),
        SORT_LIMIT,
        10**7,
        (HBM,) * 4,
    )
    low, high = low.reshape(2, 1, ROWS, CHAN), high.reshape(2, 1, ROWS, CHAN)
    xl, xh = shifted(low, high, "gx")
    wide = jnp.concatenate([xl, low, high, xh], axis=1)
    yl, yh = shifted(wide[:1], wide[1:], "gy")
    layer = jnp.concatenate([yl, wide, yh], axis=0)
    zl, zh = shifted(layer, layer, "gz")
    layer, zl, zh = (part.reshape(16, ROWS, CHAN) for part in (layer, zl, zh))

    near_off = jnp.asarray(offset_table(NEAR, NJ_NEAR))
    rest_off = jnp.asarray(offset_table(REST, NJ_REST))
    pick, spread = jnp.asarray(pick_table()), jnp.asarray(spread_table())
    ext = ((64 * RUN, CHAN), f32)
    near_ext = ((64 * COLROWS, CHAN), f32)
    rows = ((4, GROUPS * COLROWS, CHAN), f32)
    sums, near_win, near_edges, near_saved = call(
        near_kernel,
        "near",
        [rows, ((GROUPS, NJ_NEAR, CHAN), bf16), ((GROUPS, TERMS, NJ_NEAR), bf16), ((GROUPS, 8, COLROWS, NJ_NEAR), f32)],
        [near_ext, near_ext, ((NJ_NEAR, CHAN), bf16)],
        (layer, near_off, pick, radial_weights),
        NEAR_LIMIT,
        2 * TERMS * NJ_NEAR * CHAN * GROUPS,
    )
    z_low, z_high, rest_mid, energy, d_sums = call(
        rest_kernel,
        "rest",
        [((16, ROWS, CHAN), bf16)] * 2 + [((16, ROWS, CHAN), f32), ((GROUPS * COLROWS, CHAN), f32), rows],
        [
            ext,
            ext,
            ((GROUPS, NJ_REST, CHAN), bf16),
            ((NJ_REST, CHAN), bf16),
            ((GROUPS, TERMS, NJ_REST), bf16),
            ((GROUPS, 8, COLROWS, NJ_REST), f32),
            rows,
            ((2, TERMS, CHAN), bf16),
            ((2, 16, NJ_REST), bf16),
        ],
        (
            layer, zl, zh, sums, rest_off, pick, spread, radial_weights,
            coupling.transpose(1, 0, 2), mixing, hidden_weights.T, output_weights.reshape(1, -1),
        ),
        REST_LIMIT,
        6 * TERMS * NJ_REST * CHAN * GROUPS,
    )
    (mid,) = call(
        near_back_kernel,
        "near_back",
        [((16, ROWS, CHAN), f32)],
        [near_ext, near_ext, ((2, TERMS, CHAN), bf16), ((2, 16, NJ_NEAR), bf16)],
        (near_edges, near_win, near_saved, d_sums, rest_mid, spread, radial_weights),
        NEAR_LIMIT,
        4 * TERMS * NJ_NEAR * CHAN * GROUPS,
    )
    four = (4, 4, ROWS, CHAN)
    from_below, from_above = shifted(z_low.reshape(four), z_high.reshape(four), "gz")
    mid = mid.reshape(four)

    def summed(part):
        return mid[part] + from_below[part].astype(f32) + from_above[part].astype(f32)

    y_below, y_above = shifted(summed(slice(0, 1)).astype(bf16), summed(slice(3, 4)).astype(bf16), "gy")
    strip = summed(slice(1, 3)) + jnp.concatenate([y_below, y_above], axis=0).astype(f32)
    x_below, x_above = shifted(strip[:, :1].astype(bf16), strip[:, 3:].astype(bf16), "gx")
    atom_energy, forces, feature_grad = call(
        finish_kernel,
        "finish",
        [((4, 1, SLOTS), f32), ((12, 1, SLOTS), f32), ((4, SLOTS, CHAN), f32)],
        [],
        (count, pos, strip, x_below.reshape(2, ROWS, CHAN), x_above.reshape(2, ROWS, CHAN), energy),
        8 << 10,
        10**7,
        (SMEM,),
    )
    return (
        atom_energy.reshape(species.shape),
        forces.reshape(local_pos.shape),
        feature_grad.reshape(features.shape),
    )


def solution(mesh):
    placed = (
        P("gx", "gy", "gz", None, None),
        P("gx", "gy", "gz"),
        P("gx", "gy", "gz", None),
        P("gx", "gy", "gz", None, None),
        P(),
        P(),
        P(),
        P(),
        P(),
    )
    return jax.shard_map(
        body,
        mesh=mesh,
        in_specs=placed,
        out_specs=(
            P("gx", "gy", "gz", None),
            P("gx", "gy", "gz", None, None),
            P("gx", "gy", "gz", None, None),
        ),
        check_vma=False,
    )
```

time: 98.4 us -> 83.7 us (0.85)
  local copies, waits for them, and re-layouts: 9.75 us -> 2.37 us
  starting transfers between devices: 24.7 us -> 21.3 us
  waiting for transfers between devices: 24.9 us -> 22.8 us
    ppermute x6, starting transfers between devices: 18.1 us -> 12.1 us  [shifted(): from_above = lax.ppermute(low_part, axis, down)]
    unnamed x27 -> x26, local copies, waits for them, and re-layouts: 5.57 us -> 2.19 us
    ppermute x6, starting transfers between devices: 6.54 us -> 9.14 us  [shifted(): from_below = lax.ppermute(high_part, axis, up)]
    ppermute x6, waiting for transfers between devices: 16 us -> 13.8 us  [shifted(): from_below = lax.ppermute(high_part, axis, up)]
    concatenate x1 -> x2, other arithmetic: 0.04 us -> 1.64 us  [the longest x1 0.83 us: body(): layer = jnp.concatenate([yl, wide, yh], axis=0)]
    slice x5 -> x3, local copies, waits for them, and re-layouts: 1.49 us -> 0.04 us  [the longest x1 0.02 us: summed(): mid[part] + from_below[part].astype(f32) + from_above[part].astype(f32)]
    unnamed x1 -> x0, other arithmetic: 1.34 us -> none
    reshape x2, local copies, waits for them, and re-layouts: 1.19 us -> 0.05 us  [the longest x1 0.02 us: body(): z_high.reshape(four)]
  transfers between devices with their start and end apart: 12 -> 12, of which waited for: 11 -> 11; matrix products, arithmetic and copies ran while one was open for 3% -> 0% of each run, Pallas kernels for 0% -> 13%
where the time goes in v1:
time: 83.7 us; the launch traced here: 83.3 us
  Pallas kernels  34.2 us (41%)
  waiting for transfers between devices  22.8 us (27%)
  starting transfers between devices  21.3 us (25%)
  local copies, waits for them, and re-layouts  2.37 us (3%)
  other arithmetic  1.77 us (2%)
  between operations  0.89 us (1%)
    pallas_call x5, Pallas kernels, call(): pl.pallas_call(kernel, name=name, out_shape=shapes, in_specs=[*spaces] +...  34.2 us
    ppermute x6, waiting for transfers between devices, shifted(): from_below = lax.ppermute(high_part, axis, up)  13.8 us
    ppermute x6, starting transfers between devices, shifted(): from_above = lax.ppermute(low_part, axis, down)  12.1 us
    ppermute x6, starting transfers between devices, shifted(): from_below = lax.ppermute(high_part, axis, up)  9.14 us
    ppermute x6, waiting for transfers between devices, shifted(): from_above = lax.ppermute(low_part, axis, down)  9.04 us
    unnamed x26, local copies, waits for them, and re-layouts  2.19 us
  transfers between devices with their start and end apart: 12, of which 11 were waited for; matrix products, arithmetic and copies ran while one was open for 0% of the time, Pallas kernels for 13%

profile of v1, /device:TPU:1, one launch (start us, length us, event | category | flops | bytes accessed | tf_op | source)
XLA Modules:
  0.0 83.3 jit_solution(3142673209166362299)
XLA Ops:
  0.6 0.0 copy-start.12
  0.6 0.0 copy-start.3
  0.7 0.0 copy-start.9
  0.7 0.0 copy-start.2
  0.7 0.0 copy-start.8
  0.7 0.0 copy-start.7
  0.7 0.0 copy-start.5
  0.7 0.0 copy-start.6
  0.7 1.9 %sort.1 = (bf16[2,72,128]{2,1,0:T(8,128)(2,1)}, bf16[2,72,128]{2,1,0:T(8,128)(2,1)}) custom-call(s32[2,1,2]{2,1,0:T(1,128)} %bitcast.52, f32[12,1,64]{2,1,0:T(1,128)} %bitcast.50, s32[4,1,64]{2,1,0:T(1,128)} %bitcast.65, bf16[4,64,128]{2,1,0:T(8,128)(2,1)} %bitcast.64), custom_call_target="tpu_custom_call" | custom-call | flops 10000000 | bytes 73728 | tf_op jit(solution)/shard_map/sort/pallas_call | solution.py:510
  2.6 6.0 %collective-permute-start.1 = (bf16[2,1,72,128]{3,2,0,1:T(8,128)(2,1)}, bf16[2,1,72,128]{3,2,0,1:T(8,128)(2,1)S(1)}, u32[]{:S(2)}, u32[]{:S(2)}) collective-permute-start(bf16[2,1,72,128]{3,2,0,1:T(8,128)(2,1)} %bitcast.58), channel_id=1, source_target_pairs={{32,0},{64,32},{96,64},{128,96},{160,128},{192,160},{224,192},{0,2... | collective-permute-start | bytes 110600 | tf_op jit(solution)/shard_map/ppermute | solution.py:503
  8.6 0.0 collective-permute-start
  8.6 1.4 %collective-permute-done.1 = bf16[2,1,72,128]{3,2,0,1:T(8,128)(2,1)S(1)} collective-permute-done((bf16[2,1,72,128]{3,2,0,1:T(8,128)(2,1)}, bf16[2,1,72,128]{3,2,0,1:T(8,128)(2,1)S(1)}, u32[]{:S(2)}, u32[]{:S(2)}) %collective-permute-start.1) | collective-permute-done | bytes 36896 | tf_op jit(solution)/shard_map/ppermute | solution.py:503
  10.0 5.3 %collective-permute-done = bf16[2,1,72,128]{3,2,0,1:T(8,128)(2,1)S(1)} collective-permute-done((bf16[2,1,72,128]{3,2,0,1:T(8,128)(2,1)}, bf16[2,1,72,128]{3,2,0,1:T(8,128)(2,1)S(1)}, u32[]{:S(2)}, u32[]{:S(2)}) %collective-permute-start) | collective-permute-done | bytes 36896 | tf_op jit(solution)/shard_map/ppermute | solution.py:502
  15.2 0.8 pad_maximum_fusion.1
  16.1 2.5 %collective-permute-start.2 = (bf16[1,4,72,128]{3,2,0,1:T(8,128)(2,1)S(1)}, bf16[1,4,72,128]{3,2,0,1:T(8,128)(2,1)S(1)}, u32[]{:S(2)}, u32[]{:S(2)}) collective-permute-start(bf16[1,4,72,128]{3,2,0,1:T(8,128)(2,1)S(1)} %get-tuple-element.43), channel_id=1, source_target_pairs={{0,8},{8,16},{16,24},{24,0},{1,9},{9,17},{17,25},{25,1},{2,10},{10... | collective-permute-start | bytes 221192 | tf_op jit(solution)/shard_map/ppermute | solution.py:502
  18.5 0.0 collective-permute-start.3
  18.5 1.4 %collective-permute-done.2 = bf16[1,4,72,128]{3,2,0,1:T(8,128)(2,1)S(1)} collective-permute-done((bf16[1,4,72,128]{3,2,0,1:T(8,128)(2,1)S(1)}, bf16[1,4,72,128]{3,2,0,1:T(8,128)(2,1)S(1)}, u32[]{:S(2)}, u32[]{:S(2)}) %collective-permute-start.2) | collective-permute-done | bytes 73760 | tf_op jit(solution)/shard_map/ppermute | solution.py:502
  19.9 2.4 %collective-permute-done.3 = bf16[1,4,72,128]{3,2,0,1:T(8,128)(2,1)S(1)} collective-permute-done((bf16[1,4,72,128]{3,2,0,1:T(8,128)(2,1)S(1)}, bf16[1,4,72,128]{3,2,0,1:T(8,128)(2,1)S(1)}, u32[]{:S(2)}, u32[]{:S(2)}) %collective-permute-start.3) | collective-permute-done | bytes 73760 | tf_op jit(solution)/shard_map/ppermute | solution.py:503
  22.3 0.8 pad_maximum_fusion
  23.1 5.7 %collective-permute-start.5 = (bf16[4,4,72,128]{3,2,0,1:T(8,128)(2,1)S(1)}, bf16[4,4,72,128]{3,2,0,1:T(8,128)(2,1)S(1)}, u32[]{:S(2)}, u32[]{:S(2)}) collective-permute-start(bf16[4,4,72,128]{3,2,0,1:T(8,128)(2,1)S(1)} %pad_maximum_fusion), channel_id=1, source_target_pairs={{1,0},{2,1},{3,2},{4,3},{5,4},{6,5},{7,6},{0,7},{9,8},{10,9},{11,1... | collective-permute-start | bytes 884744 | tf_op jit(solution)/shard_map/ppermute | solution.py:503
  28.8 0.0 collective-permute-start.4
  28.8 0.0 copy-start.1
  28.8 0.7 copy-done.1
  29.5 0.0 copy-start.10
  29.5 0.8 copy-done.10
  30.3 0.0 copy-start.11
  30.3 0.7 copy-done.11
  31.0 3.6 %near.1 = (f32[4,256,128]{2,1,0:T(8,128)S(1)}, bf16[16,256,128]{2,1,0:T(8,128)(2,1)S(1)}, bf16[16,512,256]{2,1,0:T(8,128)(2,1)S(1)}, f32[16,8,16,256]{3,2,1,0:T(8,128)S(1)}) custom-call(bf16[16,72,128]{2,1,0:T(8,128)(2,1)S(1)} %bitcast.42, f32[4,8,256]{2,1,0:T(8,128)S(1)} %copy-done.10, f32[8,128]{1,0:T(8,128)S(1)} %copy-done.11, f32[2,8,128]{2,1,0:T(8,128)S(1)} %copy-done.1), custom_call_target="tpu_custom_call" | custom-call | flops 536870912 | bytes 7864320 | tf_op jit(solution)/shard_map/near/pallas_call | solution.py:510
  34.6 0.8 collective-permute-done.5
  35.5 3.1 %collective-permute-done.4 = bf16[4,4,72,128]{3,2,0,1:T(8,128)(2,1)S(1)} collective-permute-done((bf16[4,4,72,128]{3,2,0,1:T(8,128)(2,1)S(1)}, bf16[4,4,72,128]{3,2,0,1:T(8,128)(2,1)S(1)}, u32[]{:S(2)}, u32[]{:S(2)}) %collective-permute-start.4) | collective-permute-done | bytes 294944 | tf_op jit(solution)/shard_map/ppermute | solution.py:502
  38.6 0.0 copy-done.12
  38.6 0.0 copy-done.3
  38.6 0.0 copy-done.9
  38.6 0.0 copy-done.2
  38.6 0.0 copy-done.8
  38.7 0.0 copy-done.7
  38.7 0.0 copy-done.5
  38.7 0.0 copy-done.6
  38.7 19.7 %rest.1 = (bf16[16,72,128]{2,1,0:T(8,128)(2,1)S(1)}, bf16[16,72,128]{2,1,0:T(8,128)(2,1)S(1)}, f32[16,72,128]{2,1,0:T(8,128)S(1)}, f32[256,128]{1,0:T(8,128)S(1)}, f32[4,256,128]{2,1,0:T(8,128)S(1)}) custom-call(bf16[16,72,128]{2,1,0:T(8,128)(2,1)S(1)} %bitcast.43, bf16[16,72,128]{2,1,0:T(8,128)(2,1)S(1)} %bitcast.46, bf16[16,72,128]{2,1,0:T(8,128)(2,1)S(1)} %bitcast.44, ...), custom_call_target="tpu_custom_call" | custom-call | flops 3221225472 | bytes 1835008 | tf_op jit(solution)/shard_map/rest/pallas_call | solution.py:510
  58.5 0.4 collective-permute-start.7
  58.9 1.1 %collective-permute-start.6 = (bf16[4,4,72,128]{3,2,0,1:T(8,128)(2,1)S(1)}, bf16[4,4,72,128]{3,2,0,1:T(8,128)(2,1)S(1)}, u32[]{:S(2)}, u32[]{:S(2)}) collective-permute-start(bf16[4,4,72,128]{3,2,0,1:T(8,128)(2,1)S(1)} %copy.28), channel_id=1, source_target_pairs={{0,1},{1,2},{2,3},{3,4},{4,5},{5,6},{6,7},{7,0},{8,9},{9,10},{10,1... | collective-permute-start | bytes 884744 | tf_op jit(solution)/shard_map/ppermute | solution.py:502
  60.0 0.0 copy-start
  60.0 0.0 copy-start.4
  60.0 7.3 %near_back.1 = f32[16,72,128]{2,1,0:T(8,128)S(1)} custom-call(bf16[16,512,256]{2,1,0:T(8,128)(2,1)S(1)} %get-tuple-element.19.edges, bf16[16,256,128]{2,1,0:T(8,128)(2,1)S(1)} %get-tuple-element.20.feat_win, f32[16,8,16,256]{3,2,1,0:T(8,128)S(1)} %get-tuple-element.21.saved, f32[4,256,128]{2,1,0:T(8,128)S(1)} %get-tuple-element.23.d_sums, ...), custom_call_target="tpu_custom_call" | custom-call | flops 1073741824 | bytes 589824 | tf_op jit(solution)/shard_map/near_back/pallas_call | solution.py:510
  67.4 0.0 collective-permute-done.7
  67.4 0.4 collective-permute-done.6
  67.8 0.1 fusion.7
  67.8 2.6 %collective-permute-start.8 = (bf16[1,4,72,128]{3,2,0,1:T(8,128)(2,1)S(1)}, bf16[1,4,72,128]{3,2,0,1:T(8,128)(2,1)S(1)}, u32[]{:S(2)}, u32[]{:S(2)}) collective-permute-start(bf16[1,4,72,128]{3,2,0,1:T(8,128)(2,1)S(1)} %get-tuple-element.39), channel_id=1, source_target_pairs={{0,8},{8,16},{16,24},{24,0},{1,9},{9,17},{17,25},{25,1},{2,10},{10... | collective-permute-start | bytes 221192 | tf_op jit(solution)/shard_map/ppermute | solution.py:502
  70.4 0.0 collective-permute-start.9
  70.4 1.4 %collective-permute-done.8 = bf16[1,4,72,128]{3,2,0,1:T(8,128)(2,1)S(1)} collective-permute-done((bf16[1,4,72,128]{3,2,0,1:T(8,128)(2,1)S(1)}, bf16[1,4,72,128]{3,2,0,1:T(8,128)(2,1)S(1)}, u32[]{:S(2)}, u32[]{:S(2)}) %collective-permute-start.8) | collective-permute-done | bytes 73760 | tf_op jit(solution)/shard_map/ppermute | solution.py:502
  71.8 3.2 %collective-permute-done.9 = bf16[1,4,72,128]{3,2,0,1:T(8,128)(2,1)S(1)} collective-permute-done((bf16[1,4,72,128]{3,2,0,1:T(8,128)(2,1)S(1)}, bf16[1,4,72,128]{3,2,0,1:T(8,128)(2,1)S(1)}, u32[]{:S(2)}, u32[]{:S(2)}) %collective-permute-start.9) | collective-permute-done | bytes 73760 | tf_op jit(solution)/shard_map/ppermute | solution.py:503
  75.0 0.1 fusion.8
  75.1 0.1 collective-permute-start.11
  75.2 3.0 %collective-permute-start.10 = (bf16[2,1,72,128]{3,2,0,1:T(8,128)(2,1)S(1)}, bf16[2,1,72,128]{3,2,0,1:T(8,128)(2,1)S(1)}, u32[]{:S(2)}, u32[]{:S(2)}) collective-permute-start(bf16[2,1,72,128]{3,2,0,1:T(8,128)(2,1)S(1)} %get-tuple-element.42), channel_id=1, source_target_pairs={{0,32},{32,64},{64,96},{96,128},{128,160},{160,192},{192,224},{224... | collective-permute-start | bytes 110600 | tf_op jit(solution)/shard_map/ppermute | solution.py:502
  78.2 1.3 %collective-permute-done.11 = bf16[2,1,72,128]{3,2,0,1:T(8,128)(2,1)S(1)} collective-permute-done((bf16[2,1,72,128]{3,2,0,1:T(8,128)(2,1)S(1)}, bf16[2,1,72,128]{3,2,0,1:T(8,128)(2,1)S(1)}, u32[]{:S(2)}, u32[]{:S(2)}) %collective-permute-start.11) | collective-permute-done | bytes 36896 | tf_op jit(solution)/shard_map/ppermute | solution.py:503
  79.5 2.2 %collective-permute-done.10 = bf16[2,1,72,128]{3,2,0,1:T(8,128)(2,1)S(1)} collective-permute-done((bf16[2,1,72,128]{3,2,0,1:T(8,128)(2,1)S(1)}, bf16[2,1,72,128]{3,2,0,1:T(8,128)(2,1)S(1)}, u32[]{:S(2)}, u32[]{:S(2)}) %collective-permute-start.10) | collective-permute-done | bytes 36896 | tf_op jit(solution)/shard_map/ppermute | solution.py:502
  81.7 0.0 copy-done
  81.7 0.0 copy-done.4
  81.7 1.6 %finish.1 = (f32[4,1,64]{2,1,0:T(1,128)}, f32[12,1,64]{2,1,0:T(1,128)}, f32[4,64,128]{2,1,0:T(8,128)}) custom-call(s32[2,1,2]{2,1,0:T(1,128)S(1)} %bitcast.53, f32[12,1,64]{2,1,0:T(1,128)S(1)} %bitcast.51, f32[2,4,72,128]{3,2,1,0:T(8,128)S(1)} %copy.32.mid_ref, bf16[2,72,128]{2,1,0:T(8,128)(2,1)S(1)} %bitcast.49, bf16[2,72,128]{2,1,0:T(8,128)(2,1)S(1)} %bitcast.48, ...), custom_call_target="tpu_custom_call" | custom-call | flops 10000000 | bytes 135168 | tf_op jit(solution)/shard_map/finish/pallas_call | solution.py:510
  (9 shorter events, 0.2 us)
Async XLA Ops:
  0.6 38.0 %copy-start.12 = (f32[8,128]{1,0:T(8,128)S(1)}, f32[8,128]{1,0:T(8,128)}, u32[]{:S(2)}) copy-start(f32[8,128]{1,0:T(8,128)} %constant.10.clone.pick_ref) | copy-start | bytes 12292
  0.6 38.0 %copy-start.3 = (f32[16,128]{1,0:T(8,128)S(1)}, f32[16,128]{1,0:T(8,128)}, u32[]{:S(2)}) copy-start(f32[16,128]{1,0:T(8,128)} %constant.11.clone.spread_ref) | copy-start | bytes 24580
  0.7 38.0 %copy-start.9 = (f32[4,8,512]{2,1,0:T(8,128)S(1)}, f32[4,8,512]{2,1,0:T(8,128)}, u32[]{:S(2)}) copy-start(f32[4,8,512]{2,1,0:T(8,128)} %constant.9.clone.off_ref) | copy-start | bytes 196612
  0.7 38.0 %copy-start.2 = (f32[2,8,128]{2,1,0:T(8,128)S(1)}, f32[2,8,128]{2,1,0:T(8,128)}, u32[]{:S(2)}) copy-start(f32[2,8,128]{2,1,0:T(8,128)} %rw_ref.5) | copy-start | bytes 24580
  0.7 38.0 %copy-start.8 = (f32[16]{0:T(128)S(1)}, f32[16]{0:T(128)}, u32[]{:S(2)}) copy-start(f32[16]{0:T(128)} %param.21) | copy-start | bytes 196
  0.7 38.0 %copy-start.7 = (f32[128,16]{0,1:T(8,128)S(1)}, f32[128,16]{0,1:T(8,128)}, u32[]{:S(2)}) copy-start(f32[128,16]{0,1:T(8,128)} %param.20) | copy-start | bytes 24580
  0.7 38.0 %copy-start.5 = (f32[128,128]{1,0:T(8,128)S(1)}, f32[128,128]{1,0:T(8,128)}, u32[]{:S(2)}) copy-start(f32[128,128]{1,0:T(8,128)} %mix_ref.1) | copy-start | bytes 196612
  0.7 38.0 %copy-start.6 = (f32[3,10,128]{2,0,1:T(4,128)S(1)}, f32[3,10,128]{2,0,1:T(4,128)}, u32[]{:S(2)}) copy-start(f32[3,10,128]{2,0,1:T(4,128)} %param.18) | copy-start | bytes 46084
  2.6 7.4 %collective-permute-start.1 = (bf16[2,1,72,128]{3,2,0,1:T(8,128)(2,1)}, bf16[2,1,72,128]{3,2,0,1:T(8,128)(2,1)S(1)}, u32[]{:S(2)}, u32[]{:S(2)}) collective-permute-start(bf16[2,1,72,128]{3,2,0,1:T(8,128)(2,1)} %bitcast.58), channel_id=1, source_target_pairs={{32,0},{64,32},{96,64},{128,96},{160,128},{192,160},{224,192},{0,2... | collective-permute-start | bytes 110600 | tf_op jit(solution)/shard_map/ppermute | solution.py:503
  8.6 6.6 %collective-permute-start = (bf16[2,1,72,128]{3,2,0,1:T(8,128)(2,1)}, bf16[2,1,72,128]{3,2,0,1:T(8,128)(2,1)S(1)}, u32[]{:S(2)}, u32[]{:S(2)}) collective-permute-start(bf16[2,1,72,128]{3,2,0,1:T(8,128)(2,1)} %bitcast.61), channel_id=1, source_target_pairs={{0,32},{32,64},{64,96},{96,128},{128,160},{160,192},{192,224},{224... | collective-permute-start | bytes 110600 | tf_op jit(solution)/shard_map/ppermute | solution.py:502
  16.1 3.9 %collective-permute-start.2 = (bf16[1,4,72,128]{3,2,0,1:T(8,128)(2,1)S(1)}, bf16[1,4,72,128]{3,2,0,1:T(8,128)(2,1)S(1)}, u32[]{:S(2)}, u32[]{:S(2)}) collective-permute-start(bf16[1,4,72,128]{3,2,0,1:T(8,128)(2,1)S(1)} %get-tuple-element.43), channel_id=1, source_target_pairs={{0,8},{8,16},{16,24},{24,0},{1,9},{9,17},{17,25},{25,1},{2,10},{10... | collective-permute-start | bytes 221192 | tf_op jit(solution)/shard_map/ppermute | solution.py:502
  18.5 3.8 %collective-permute-start.3 = (bf16[1,4,72,128]{3,2,0,1:T(8,128)(2,1)S(1)}, bf16[1,4,72,128]{3,2,0,1:T(8,128)(2,1)S(1)}, u32[]{:S(2)}, u32[]{:S(2)}) collective-permute-start(bf16[1,4,72,128]{3,2,0,1:T(8,128)(2,1)S(1)} %get-tuple-element.44), channel_id=1, source_target_pairs={{8,0},{16,8},{24,16},{0,24},{9,1},{17,9},{25,17},{1,25},{10,2},{18... | collective-permute-start | bytes 221192 | tf_op jit(solution)/shard_map/ppermute | solution.py:503
  23.1 12.3 %collective-permute-start.5 = (bf16[4,4,72,128]{3,2,0,1:T(8,128)(2,1)S(1)}, bf16[4,4,72,128]{3,2,0,1:T(8,128)(2,1)S(1)}, u32[]{:S(2)}, u32[]{:S(2)}) collective-permute-start(bf16[4,4,72,128]{3,2,0,1:T(8,128)(2,1)S(1)} %pad_maximum_fusion), channel_id=1, source_target_pairs={{1,0},{2,1},{3,2},{4,3},{5,4},{6,5},{7,6},{0,7},{9,8},{10,9},{11,1... | collective-permute-start | bytes 884744 | tf_op jit(solution)/shard_map/ppermute | solution.py:503
  28.8 9.8 %collective-permute-start.4 = (bf16[4,4,72,128]{3,2,0,1:T(8,128)(2,1)S(1)}, bf16[4,4,72,128]{3,2,0,1:T(8,128)(2,1)S(1)}, u32[]{:S(2)}, u32[]{:S(2)}) collective-permute-start(bf16[4,4,72,128]{3,2,0,1:T(8,128)(2,1)S(1)} %pad_maximum_fusion), channel_id=1, source_target_pairs={{0,1},{1,2},{2,3},{3,4},{4,5},{5,6},{6,7},{7,0},{8,9},{9,10},{10,1... | collective-permute-start | bytes 884744 | tf_op jit(solution)/shard_map/ppermute | solution.py:502
  28.8 0.7 copy-start.1
  29.5 0.8 copy-start.10
  30.3 0.7 copy-start.11
  58.5 8.9 %collective-permute-start.7 = (bf16[4,4,72,128]{3,2,0,1:T(8,128)(2,1)S(1)}, bf16[4,4,72,128]{3,2,0,1:T(8,128)(2,1)S(1)}, u32[]{:S(2)}, u32[]{:S(2)}) collective-permute-start(bf16[4,4,72,128]{3,2,0,1:T(8,128)(2,1)S(1)} %copy.30), channel_id=1, source_target_pairs={{1,0},{2,1},{3,2},{4,3},{5,4},{6,5},{7,6},{0,7},{9,8},{10,9},{11,1... | collective-permute-start | bytes 884744 | tf_op jit(solution)/shard_map/ppermute | solution.py:503
  58.9 8.9 %collective-permute-start.6 = (bf16[4,4,72,128]{3,2,0,1:T(8,128)(2,1)S(1)}, bf16[4,4,72,128]{3,2,0,1:T(8,128)(2,1)S(1)}, u32[]{:S(2)}, u32[]{:S(2)}) collective-permute-start(bf16[4,4,72,128]{3,2,0,1:T(8,128)(2,1)S(1)} %copy.28), channel_id=1, source_target_pairs={{0,1},{1,2},{2,3},{3,4},{4,5},{5,6},{6,7},{7,0},{8,9},{9,10},{10,1... | collective-permute-start | bytes 884744 | tf_op jit(solution)/shard_map/ppermute | solution.py:502
  60.0 21.7 %copy-start = (f32[2,2,1,3,64]{4,2,3,1,0:T(1,128)S(1)}, f32[2,2,1,3,64]{4,2,3,1,0:T(1,128)}, u32[]{:S(2)}) copy-start(f32[2,2,1,3,64]{4,2,3,1,0:T(1,128)} %param.13) | copy-start | bytes 9220
  60.0 21.7 %copy-start.4 = (s32[2,2,1]{1,2,0:T(1,128)S(1)}, s32[2,2,1]{1,2,0:T(1,128)}, u32[]{:S(2)}) copy-start(s32[2,2,1]{1,2,0:T(1,128)} %param.14) | copy-start | bytes 52
  67.8 4.0 %collective-permute-start.8 = (bf16[1,4,72,128]{3,2,0,1:T(8,128)(2,1)S(1)}, bf16[1,4,72,128]{3,2,0,1:T(8,128)(2,1)S(1)}, u32[]{:S(2)}, u32[]{:S(2)}) collective-permute-start(bf16[1,4,72,128]{3,2,0,1:T(8,128)(2,1)S(1)} %get-tuple-element.39), channel_id=1, source_target_pairs={{0,8},{8,16},{16,24},{24,0},{1,9},{9,17},{17,25},{25,1},{2,10},{10... | collective-permute-start | bytes 221192 | tf_op jit(solution)/shard_map/ppermute | solution.py:502
  70.4 4.6 %collective-permute-start.9 = (bf16[1,4,72,128]{3,2,0,1:T(8,128)(2,1)S(1)}, bf16[1,4,72,128]{3,2,0,1:T(8,128)(2,1)S(1)}, u32[]{:S(2)}, u32[]{:S(2)}) collective-permute-start(bf16[1,4,72,128]{3,2,0,1:T(8,128)(2,1)S(1)} %get-tuple-element.40), channel_id=1, source_target_pairs={{8,0},{16,8},{24,16},{0,24},{9,1},{17,9},{25,17},{1,25},{10,2},{18... | collective-permute-start | bytes 221192 | tf_op jit(solution)/shard_map/ppermute | solution.py:503
  75.1 4.4 %collective-permute-start.11 = (bf16[2,1,72,128]{3,2,0,1:T(8,128)(2,1)S(1)}, bf16[2,1,72,128]{3,2,0,1:T(8,128)(2,1)S(1)}, u32[]{:S(2)}, u32[]{:S(2)}) collective-permute-start(bf16[2,1,72,128]{3,2,0,1:T(8,128)(2,1)S(1)} %get-tuple-element.41), channel_id=1, source_target_pairs={{32,0},{64,32},{96,64},{128,96},{160,128},{192,160},{224,192},{0,2... | collective-permute-start | bytes 110600 | tf_op jit(solution)/shard_map/ppermute | solution.py:503
  75.2 6.5 %collective-permute-start.10 = (bf16[2,1,72,128]{3,2,0,1:T(8,128)(2,1)S(1)}, bf16[2,1,72,128]{3,2,0,1:T(8,128)(2,1)S(1)}, u32[]{:S(2)}, u32[]{:S(2)}) collective-permute-start(bf16[2,1,72,128]{3,2,0,1:T(8,128)(2,1)S(1)} %get-tuple-element.42), channel_id=1, source_target_pairs={{0,32},{32,64},{64,96},{96,128},{128,160},{160,192},{192,224},{224... | collective-permute-start | bytes 110600 | tf_op jit(solution)/shard_map/ppermute | solution.py:502

commit v2 on v1

--- a/solution.py
+++ b/solution.py
@@ -65,13 +65,24 @@
     return table
 
 
-def spread_table():
-    table = np.zeros((16, CHAN), np.float32)
-    for group in range(8):
-        for part in range(2):
-            for comp in range(3):
-                table[3 * part + comp, 16 * group + comp] = 1.0
-    return table
+def constant_table():
+    parts = [pick_table()]
+    for pieces, size in ((NEAR, NJ_NEAR), (REST, NJ_REST)):
+        table = offset_table(pieces, size).reshape(4, 8, size // TILE, TILE)
+        parts.append(table.transpose(0, 2, 1, 3).reshape(-1, TILE))
+    return np.concatenate(parts, axis=0)
+
+
+RADIAL = 0
+COUPLE = 16
+NSPEC = 10
+MIXING = 48
+HIDDEN = 176
+OUTPUT = 192
+PICK = 200
+NEAR_OFF = PICK + 8
+REST_OFF = NEAR_OFF + 4 * 8 * (NJ_NEAR // TILE)
+PACKED = REST_OFF + 4 * 8 * (NJ_REST // TILE)
 
 
 def poly_coeffs():
@@ -93,6 +104,16 @@
 
 def dot(a, b, dims, precision=None):
     return lax.dot_general(a, b, (dims, ((), ())), preferred_element_type=jnp.float32, precision=precision)
+
+
+def halves(x):
+    first = x.astype(jnp.bfloat16)
+    return first, (x - first.astype(jnp.float32)).astype(jnp.bfloat16)
+
+
+def dot_parts(a, parts, dims):
+    a0, a1 = halves(a)
+    return dot(a0, parts[0], dims) + (dot(a0, parts[1], dims) + dot(a1, parts[0], dims))
 
 
 NN = ((1,), (0,))
@@ -112,11 +133,25 @@
     return lax.broadcasted_iota(jnp.int32, (rows, CHAN), 1) >> 4
 
 
-def sort_kernel(count_hbm, pos_hbm, kind_hbm, feat_hbm, low_ref, high_ref, parts_ref, count_ref, pos_ref, kind_ref, feat_ref, sem):
+def sort_kernel(
+    count_hbm, pos_hbm, kind_hbm, feat_hbm, radial_hbm, couple_hbm, mix_hbm, hidden_hbm, output_hbm, const_hbm,
+    out_ref, pack_ref, parts_ref, count_ref, pos_ref, kind_ref, feat_ref, couple_ref, output_ref, sem,
+):
     copies = [
         pltpu.make_async_copy(source, target, sem.at[k])
         for k, (source, target) in enumerate(
-            ((count_hbm, count_ref), (pos_hbm, pos_ref), (kind_hbm, kind_ref), (feat_hbm, feat_ref))
+            (
+                (count_hbm, count_ref),
+                (pos_hbm, pos_ref),
+                (kind_hbm, kind_ref),
+                (feat_hbm, feat_ref),
+                (couple_hbm, couple_ref),
+                (output_hbm, output_ref),
+                (radial_hbm, pack_ref.at[RADIAL:COUPLE]),
+                (mix_hbm, pack_ref.at[MIXING:HIDDEN]),
+                (hidden_hbm, pack_ref.at[HIDDEN:OUTPUT]),
+                (const_hbm, pack_ref.at[PICK:PACKED]),
+            )
         )
     ]
     for copy in copies:
@@ -125,6 +160,9 @@
     parts_ref[...] = jnp.zeros_like(parts_ref)
     for copy in copies:
         copy.wait()
+    for s in range(NSPEC):
+        pack_ref[COUPLE + 3 * s : COUPLE + 3 * s + 3] = couple_ref[s]
+    pack_ref[OUTPUT : OUTPUT + 1, : output_ref.shape[1]] = output_ref[...]
     for cell in range(4):
         x, y = cell // 2, cell % 2
         pos = [pos_ref[3 * cell + c] for c in range(3)]
@@ -143,13 +181,13 @@
                     parts_ref[cell, at : at + 1] = lines[c][part]
             parts_ref[cell, 16 * g + 9 : 16 * g + 10] = kind
             parts_ref[cell, 16 * g + 10 : 16 * g + 11] = jnp.ones_like(kind)
-        out = high_ref if x else low_ref
-        out[y, :SLOTS] = dot(hot, feat_ref[cell], NN).astype(jnp.bfloat16)
+        at = 2 * y + x
+        out_ref[at, :SLOTS] = dot(hot, feat_ref[cell], NN).astype(jnp.bfloat16)
         spread = dot(hot, parts_ref[cell].astype(jnp.bfloat16), NT)
         extra = jnp.zeros((EXTRA, CHAN), jnp.float32)
         for g in range(8):
             extra = extra + jnp.where(group == g, spread[8 * g : 8 * g + 8], 0.0)
-        out[y, SLOTS:] = extra.astype(jnp.bfloat16)
+        out_ref[at, SLOTS:] = extra.astype(jnp.bfloat16)
 
 
 def place(msg, cell, feat_ext, pos_ext, run, shift):
@@ -189,12 +227,13 @@
     return own
 
 
-def edge_columns(g, own, far, edges, saved, size):
+def edge_columns(g, own, far, pack_ref, off_at, edges, saved, size):
     lane = lane_kind()
     coords = [own_scalar(own, (lane == c) | (lane == 3 + c) | (lane == 6 + c)) for c in range(3)]
     for t in range(size // TILE):
         at = slice(t * TILE, t * TILE + TILE)
-        dx, dy, dz = (far[c : c + 1, at] - coords[c] for c in range(3))
+        there = far[:, at] + pack_ref[pl.ds(pl.multiple_of(off_at + 8 * t, 8), 8)]
+        dx, dy, dz = (there[c : c + 1] - coords[c] for c in range(3))
         square = dx * dx + dy * dy + dz * dz
         clear = jnp.maximum(square, 0.25)
         inv = lax.rsqrt(clear)
@@ -231,18 +270,18 @@
     return pl.ds(pl.multiple_of(g * COLROWS, COLROWS), COLROWS)
 
 
-def contract(g, edges, feat_win, rw_ref, sums, start_ref=None):
+def contract(g, edges, feat_win, pack_ref, sums, start_ref=None):
     summed = dot(edges[g], feat_win[g], NN)
     rows = group_rows(g)
     for m in range(4):
         total = jnp.zeros((COLROWS, CHAN), jnp.float32) if start_ref is None else start_ref[m, rows]
         for b in range(NB):
             r0 = (b * 4 + m) * COLROWS
-            total = total + rw_ref[min(m, 1), b : b + 1] * summed[r0 : r0 + 16]
+            total = total + pack_ref[8 * min(m, 1) + b : 8 * min(m, 1) + b + 1] * summed[r0 : r0 + 16]
         sums[m, rows] = total
 
 
-def back_group(g, size, pieces, run, skip, edges, feat_win, saved, d_sums, rw_ref, spread, d_half, d_far, d_feat_ext, d_pos_ext):
+def back_group(g, size, pieces, run, skip, edges, feat_win, saved, d_sums, pack_ref, d_half, d_far, d_win, d_feat_ext, d_pos_ext):
     lane = lane_kind()
     base = column(g, run)
     rows = group_rows(g)
@@ -250,7 +289,7 @@
         d_sum = d_sums[m, rows]
         for b in range(NB):
             r0 = (b * 4 + m) * COLROWS
-            d_half[r0 : r0 + 16] = (rw_ref[min(m, 1), b : b + 1] * d_sum).astype(jnp.bfloat16)
+            d_half[r0 : r0 + 16] = (pack_ref[8 * min(m, 1) + b : 8 * min(m, 1) + b + 1] * d_sum).astype(jnp.bfloat16)
     totals = [jnp.zeros((COLROWS, TILE), jnp.float32)] * 3
     for t in range(size // TILE):
         at = slice(t * TILE, t * TILE + TILE)
@@ -280,16 +319,13 @@
         ds = [along * ux + across * grads[0], along * uy + across * grads[1], along * uz + across * grads[2]]
         for c in range(3):
             totals[c] = totals[c] + ds[c]
-            far_sum = jnp.sum(ds[c], axis=0, keepdims=True)
-            hi = far_sum.astype(jnp.bfloat16)
-            d_far[c : c + 1, at] = hi
-            d_far[3 + c : 4 + c, at] = (far_sum - hi.astype(jnp.float32)).astype(jnp.bfloat16)
-    d_feat = dot(edges[g], d_half[...], TN)
-    d_spread = dot(d_far[...], spread, TN)
+            d_far[c : c + 1, at] = jnp.sum(ds[c], axis=0, keepdims=True)
+    d_win[0] = dot(edges[g], d_half[...], TN)
+    d_win[1, :, :8] = d_far[...].T
     for a, b, first, count, at in pieces:
         start = pl.ds(base + (a * 8 + b) * run + first - skip, count)
-        d_feat_ext[start] = d_feat_ext[start] + d_feat[at : at + count]
-        d_pos_ext[start] = d_pos_ext[start] + d_spread[at : at + count]
+        d_feat_ext[start] = d_feat_ext[start] + d_win[0, at : at + count]
+        d_pos_ext[start] = d_pos_ext[start] + d_win[1, at : at + count]
     mine = pl.ds(pl.multiple_of(base + COLROWS - skip, COLROWS), COLROWS)
     back = jnp.zeros((COLROWS, CHAN), jnp.float32)
     for c in range(3):
@@ -298,7 +334,7 @@
 
 
 def collect(cell, outs, d_feat_ext, d_pos_ext, run):
-    group = lane_group(8)
+    lane8 = lax.broadcasted_iota(jnp.int32, (8, CHAN), 1)
     for shift, out, more in outs:
         scalars = jnp.zeros((EXTRA, CHAN), jnp.float32)
         for cc in range(4):
@@ -309,37 +345,40 @@
                 rows = rows + more[cell, COLROWS * cc : COLROWS * cc + COLROWS]
             out[cell, COLROWS * cc : COLROWS * cc + COLROWS] = rows.astype(out.dtype)
             for h in range(2):
-                scalars = scalars + jnp.where(group == 2 * cc + h, d_pos_ext[pl.ds(base + 8 * h, 8)], 0.0)
+                place_at = 16 * (2 * cc + h)
+                block = d_pos_ext[pl.ds(base + 8 * h, 8)]
+                block = jnp.where(lane8 < 6, block, 0.0)
+                scalars = scalars + (pltpu.roll(block, place_at, 1) if place_at else block)
         if more is not None:
             scalars = scalars + more[cell, SLOTS:]
         out[cell, SLOTS:] = scalars.astype(out.dtype)
 
 
-def near_kernel(layer_ref, off_ref, pick_ref, rw_ref, sums, feat_win, edges, saved, feat_ext, pos_ext, pos_win):
+def near_kernel(layer_ref, pack_ref, sums, feat_win, edges, saved, feat_ext, pos_ext, pos_win):
     def spread_cell(cell, carry):
         place(layer_ref, cell, feat_ext, pos_ext, COLROWS, 0)
         return carry
 
     lax.fori_loop(0, 16, spread_cell, 0)
-    pick = pick_ref[...].astype(jnp.bfloat16)
+    pick = pack_ref[PICK : PICK + 8].astype(jnp.bfloat16)
 
     def forward(k, carry):
         for g in (4 * k, 4 * k + 1, 4 * k + 2, 4 * k + 3):
             own = take_window(g, NEAR, COLROWS, COLROWS, feat_ext, pos_ext, feat_win, pos_win)
             parity = ((g // 4) & 1) * 2 + (g & 1)
-            far = dot(pick, pos_win[...], NT) + off_ref[parity]
-            edge_columns(g, own, far, edges, saved, NJ_NEAR)
+            far = dot(pick, pos_win[...], NT)
+            edge_columns(g, own, far, pack_ref, NEAR_OFF + parity * (8 * NJ_NEAR // TILE), edges, saved, NJ_NEAR)
         for g in (4 * k, 4 * k + 1, 4 * k + 2, 4 * k + 3):
-            contract(g, edges, feat_win, rw_ref, sums)
+            contract(g, edges, feat_win, pack_ref, sums)
         return carry
 
     lax.fori_loop(0, GROUPS // 4, forward, 0)
 
 
 def rest_kernel(
-    layer_ref, zl_ref, zh_ref, near_sums, off_ref, pick_ref, spread_ref, rw_ref, coup_ref, mix_ref, hid_ref, ow_ref,
-    zlo_ref, zho_ref, mid_ref, energy_ref, d_sums,
-    feat_ext, pos_ext, feat_win, pos_win, edges, saved, sums, d_half, d_far,
+    layer_ref, zl_ref, zh_ref, near_sums, pack_ref,
+    zlo_ref, zho_ref, mid_ref, d_sums,
+    feat_ext, pos_ext, feat_win, pos_win, edges, saved, sums, energies, d_half, d_far, d_win,
 ):
     def spread_cell(cell, carry):
         place(layer_ref, cell, feat_ext, pos_ext, RUN, COLROWS)
@@ -348,7 +387,7 @@
         return carry
 
     lax.fori_loop(0, 16, spread_cell, 0)
-    pick = pick_ref[...].astype(jnp.bfloat16)
+    pick = pack_ref[PICK : PICK + 8].astype(jnp.bfloat16)
     lane = lane_kind()
     pos_win[USED:] = jnp.zeros((NJ_REST - USED, CHAN), jnp.bfloat16)
 
@@ -357,50 +396,50 @@
             own = take_window(g, REST, RUN, 0, feat_ext, pos_ext, feat_win, pos_win)
             feat_win[g, USED:] = jnp.zeros((NJ_REST - USED, CHAN), jnp.bfloat16)
             parity = ((g // 4) & 1) * 2 + (g & 1)
-            far = dot(pick, pos_win[...], NT) + off_ref[parity]
-            edge_columns(g, own, far, edges, saved, NJ_REST)
+            far = dot(pick, pos_win[...], NT)
+            edge_columns(g, own, far, pack_ref, REST_OFF + parity * (8 * NJ_REST // TILE), edges, saved, NJ_REST)
         for g in (4 * k, 4 * k + 1, 4 * k + 2, 4 * k + 3):
-            contract(g, edges, feat_win, rw_ref, sums, near_sums)
+            contract(g, edges, feat_win, pack_ref, sums, near_sums)
         return carry
 
     lax.fori_loop(0, GROUPS // 4, forward, 0)
 
-    high = lax.Precision.HIGHEST
-    head = dot(mix_ref[...], hid_ref[...], NT, high)
-    ow = ow_ref[...]
+    head = dot(pack_ref[MIXING:HIDDEN], pack_ref[HIDDEN:OUTPUT], NT, lax.Precision.HIGHEST)
+    head_parts = halves(head)
+    ow = pack_ref[OUTPUT : OUTPUT + 1, : OUTPUT - HIDDEN]
 
     def readout(k, carry):
         kinds, occs = [], []
-        for s in range(4):
-            start = column(k * 4 + s, RUN) + COLROWS
+        for s in range(8):
+            start = column(k * 8 + s, RUN) + COLROWS
             own = pos_ext[pl.ds(pl.multiple_of(start, COLROWS), COLROWS)]
             kinds.append(own_scalar(own, lane == 9))
             occs.append(own_scalar(own, lane == 10))
         kind = jnp.concatenate(kinds, axis=0)
         occ = jnp.concatenate(occs, axis=0)
-        rows = pl.ds(pl.multiple_of(k * 64, 64), 64)
+        rows = pl.ds(pl.multiple_of(k * 128, 128), 128)
         scalar = sums[0, rows]
         vectors = [sums[m, rows] for m in (1, 2, 3)]
         weights = []
         for q in range(3):
-            w = jnp.zeros((64, CHAN), jnp.float32)
-            for s in range(coup_ref.shape[0]):
-                w = jnp.where(kind == float(s), coup_ref[s, q : q + 1], w)
+            w = jnp.zeros((128, CHAN), jnp.float32)
+            for s in range(NSPEC):
+                w = jnp.where(kind == float(s), pack_ref[COUPLE + 3 * s + q : COUPLE + 3 * s + q + 1], w)
             weights.append(w)
         length = vectors[0] * vectors[0] + vectors[1] * vectors[1] + vectors[2] * vectors[2]
         product = weights[0] * scalar + weights[1] * scalar * scalar + weights[2] * length
-        hidden = dot(product, head, NN, high)
+        hidden = dot_parts(product, head_parts, NN)
         logistic = jax.nn.sigmoid(hidden)
         energy = occ * jnp.sum(ow * hidden * logistic, axis=1, keepdims=True)
-        energy_ref[rows] = jnp.broadcast_to(energy, (64, CHAN))
+        energies[rows] = jnp.broadcast_to(energy, (128, CHAN))
         d_hidden = occ * ow * logistic * (1.0 + hidden * (1.0 - logistic))
-        d_product = dot(d_hidden, head, NT, high)
+        d_product = dot_parts(d_hidden, head_parts, NT)
         d_sums[0, rows] = d_product * (weights[0] + 2.0 * weights[1] * scalar)
         for m in range(3):
             d_sums[m + 1, rows] = 2.0 * weights[2] * vectors[m] * d_product
         return carry
 
-    lax.fori_loop(0, 4, readout, 0)
+    lax.fori_loop(0, 2, readout, 0)
 
     def clear(c, carry):
         rows = pl.ds(pl.multiple_of(c * RUN, RUN), RUN)
@@ -409,18 +448,26 @@
         return carry
 
     lax.fori_loop(0, 64, clear, 0, unroll=2)
+    for g in range(GROUPS):
+        energy = energies[COLROWS * g : COLROWS * g + COLROWS]
+        first = energy.astype(jnp.bfloat16).astype(jnp.float32)
+        second = (energy - first).astype(jnp.bfloat16).astype(jnp.float32)
+        third = energy - first - second
+        mine = pl.ds(column(g, RUN) + COLROWS, COLROWS)
+        pos_ext[mine] = jnp.where(
+            lane == 3, first, jnp.where(lane == 4, second, jnp.where(lane == 5, third, 0.0))
+        )
     d_far[...] = jnp.zeros_like(d_far)
-    spread = spread_ref[...].astype(jnp.bfloat16)
 
     def backward(k, carry):
-        for s in range(2):
+        for s in range(4):
             back_group(
-                2 * k + s, NJ_REST, REST, RUN, 0, edges, feat_win, saved, d_sums, rw_ref, spread,
-                d_half.at[s], d_far.at[s], feat_ext, pos_ext,
+                4 * k + s, NJ_REST, REST, RUN, 0, edges, feat_win, saved, d_sums, pack_ref,
+                d_half.at[s], d_far.at[s], d_win.at[s], feat_ext, pos_ext,
             )
         return carry
 
-    lax.fori_loop(0, GROUPS // 2, backward, 0)
+    lax.fori_loop(0, GROUPS // 4, backward, 0)
 
     def gather_cell(cell, carry):
         collect(cell, ((0, zlo_ref, None), (COLROWS, mid_ref, None), (2 * COLROWS, zho_ref, None)), feat_ext, pos_ext, RUN)
@@ -430,22 +477,21 @@
 
 
 def near_back_kernel(
-    edges, feat_win, saved, d_sums, rest_mid, spread_ref, rw_ref, mid_ref, feat_ext, pos_ext, d_half, d_far
+    edges, feat_win, saved, d_sums, rest_mid, pack_ref, mid_ref, feat_ext, pos_ext, d_half, d_far, d_win
 ):
     feat_ext[...] = jnp.zeros_like(feat_ext)
     pos_ext[...] = jnp.zeros_like(pos_ext)
     d_far[...] = jnp.zeros_like(d_far)
-    spread = spread_ref[...].astype(jnp.bfloat16)
 
     def backward(k, carry):
-        for s in range(2):
+        for s in range(4):
             back_group(
-                2 * k + s, NJ_NEAR, NEAR, COLROWS, COLROWS, edges, feat_win, saved, d_sums, rw_ref, spread,
-                d_half.at[s], d_far.at[s], feat_ext, pos_ext,
+                4 * k + s, NJ_NEAR, NEAR, COLROWS, COLROWS, edges, feat_win, saved, d_sums, pack_ref,
+                d_half.at[s], d_far.at[s], d_win.at[s], feat_ext, pos_ext,
             )
         return carry
 
-    lax.fori_loop(0, GROUPS // 2, backward, 0)
+    lax.fori_loop(0, GROUPS // 4, backward, 0)
 
     def gather_cell(cell, carry):
         collect(cell, ((0, mid_ref, rest_mid),), feat_ext, pos_ext, COLROWS)
@@ -454,13 +500,12 @@
     lax.fori_loop(0, 16, gather_cell, 0)
 
 
-def finish_kernel(count_ref, pos_ref, mid_ref, low_ref, high_ref, energy_ref, e_ref, f_ref, g_ref):
+def finish_kernel(count_ref, pos_ref, mid_ref, arrived_ref, e_ref, f_ref, g_ref):
     lane = lax.broadcasted_iota(jnp.int32, (EXTRA, CHAN), 1)
     for cell in range(4):
         x, y = cell // 2, cell % 2
         hot = site_onehot([pos_ref[3 * cell + c] for c in range(3)], count_ref[x, 0, y]).astype(jnp.float32)
-        arrived = high_ref[y] if x else low_ref[y]
-        total = mid_ref[y, 1 + x] + arrived.astype(jnp.float32)
+        total = mid_ref[y, x] + arrived_ref[y, x].astype(jnp.float32)
         turned = hot.T.astype(jnp.bfloat16)
         rest = total[:SLOTS]
         grad = jnp.zeros((SLOTS, CHAN), jnp.float32)
@@ -469,20 +514,17 @@
             grad = grad + dot(turned, piece, NN)
             rest = rest - piece.astype(jnp.float32)
         g_ref[cell] = grad
+
+        def per_slot(lanes):
+            rows = [
+                jnp.sum(jnp.where((lane >= 16 * g + lanes[0]) & (lane <= 16 * g + lanes[1]), total[SLOTS:], 0.0), axis=1, keepdims=True)
+                for g in range(8)
+            ]
+            return jnp.sum(hot * jnp.concatenate(rows, axis=0), axis=0, keepdims=True)
+
         for c in range(3):
-            force = jnp.concatenate(
-                [
-                    jnp.sum(jnp.where(lane == 16 * g + c, total[SLOTS:], 0.0), axis=1, keepdims=True)
-                    for g in range(8)
-                ],
-                axis=0,
-            )
-            f_ref[3 * cell + c] = -jnp.sum(hot * force, axis=0, keepdims=True)
-        pieces = []
-        for cc in range(4):
-            g = (2 * x + cc // 2) * 4 + 2 * y + cc % 2
-            pieces.append(energy_ref[g * COLROWS : g * COLROWS + COLROWS, 0:1])
-        e_ref[cell] = jnp.sum(hot * jnp.concatenate(pieces, axis=0), axis=0, keepdims=True)
+            f_ref[3 * cell + c] = -per_slot((c, c))
+        e_ref[cell] = per_slot((3, 5))
 
 
 SMEM = pl.BlockSpec(memory_space=pltpu.SMEM)
@@ -495,13 +537,13 @@
 SORT_LIMIT = 65000
 
 
+def moved(part, axis, step):
+    count = lax.axis_size(axis)
+    return lax.ppermute(part, axis, [(i, (i + step) % count) for i in range(count)])
+
+
 def shifted(low_part, high_part, axis):
-    count = lax.axis_size(axis)
-    up = [(i, (i + 1) % count) for i in range(count)]
-    down = [(target, source) for source, target in up]
-    from_below = lax.ppermute(high_part, axis, up)
-    from_above = lax.ppermute(low_part, axis, down)
-    return from_below, from_above
+    return moved(high_part, axis, 1), moved(low_part, axis, -1)
 
 
 def call(kernel, name, outs, scratch, ins, limit, flops, spaces=()):
@@ -523,34 +565,42 @@
     bf16, f32 = jnp.bfloat16, jnp.float32
     pos = local_pos.reshape(12, 1, SLOTS)
     count = counts.transpose(0, 2, 1)
-    low, high = call(
+    block, pack = call(
         sort_kernel,
         "sort",
-        [((2, ROWS, CHAN), bf16)] * 2,
+        [((4, ROWS, CHAN), bf16), ((PACKED, CHAN), f32)],
         [
             pltpu.VMEM((4, CHAN, SLOTS), f32),
             pltpu.SMEM((2, 1, 2), jnp.int32),
             pltpu.VMEM((12, 1, SLOTS), f32),
             pltpu.VMEM((4, 1, SLOTS), jnp.int32),
             pltpu.VMEM((4, SLOTS, CHAN), bf16),
-            pltpu.SemaphoreType.DMA((4,)),
+            pltpu.VMEM((NSPEC, 3, CHAN), f32),
+            pltpu.VMEM((1, output_weights.shape[0]), f32),
+            pltpu.SemaphoreType.DMA((10,)),
         ],
-        (count, pos, species.reshape(4, 1, SLOTS), features.reshape(4, SLOTS, CHAN)),
+        (
+            count,
+            pos,
+            species.reshape(4, 1, SLOTS),
+            features.reshape(4, SLOTS, CHAN),
+            radial_weights.reshape(2 * NB, CHAN),
+            coupling.transpose(1, 0, 2),
+            mixing,
+            hidden_weights.T,
+            output_weights.reshape(1, -1),
+            jnp.asarray(constant_table()),
+        ),
         SORT_LIMIT,
         10**7,
-        (HBM,) * 4,
-    )
-    low, high = low.reshape(2, 1, ROWS, CHAN), high.reshape(2, 1, ROWS, CHAN)
-    xl, xh = shifted(low, high, "gx")
-    wide = jnp.concatenate([xl, low, high, xh], axis=1)
-    yl, yh = shifted(wide[:1], wide[1:], "gy")
-    layer = jnp.concatenate([yl, wide, yh], axis=0)
+        (HBM,) * 10,
+    )
+    block = block.reshape(2, 2, ROWS, CHAN)
+    wide = jnp.concatenate([block, moved(block, "gx", -1)], axis=1)
+    layer = jnp.concatenate([wide, moved(wide, "gy", -1)], axis=0)
     zl, zh = shifted(layer, layer, "gz")
     layer, zl, zh = (part.reshape(16, ROWS, CHAN) for part in (layer, zl, zh))
 
-    near_off = jnp.asarray(offset_table(NEAR, NJ_NEAR))
-    rest_off = jnp.asarray(offset_table(REST, NJ_REST))
-    pick, spread = jnp.asarray(pick_table()), jnp.asarray(spread_table())
     ext = ((64 * RUN, CHAN), f32)
     near_ext = ((64 * COLROWS, CHAN), f32)
     rows = ((4, GROUPS * COLROWS, CHAN), f32)
@@ -559,14 +609,14 @@
         "near",
         [rows, ((GROUPS, NJ_NEAR, CHAN), bf16), ((GROUPS, TERMS, NJ_NEAR), bf16), ((GROUPS, 8, COLROWS, NJ_NEAR), f32)],
         [near_ext, near_ext, ((NJ_NEAR, CHAN), bf16)],
-        (layer, near_off, pick, radial_weights),
+        (layer, pack),
         NEAR_LIMIT,
         2 * TERMS * NJ_NEAR * CHAN * GROUPS,
     )
-    z_low, z_high, rest_mid, energy, d_sums = call(
+    z_low, z_high, rest_mid, d_sums = call(
         rest_kernel,
         "rest",
-        [((16, ROWS, CHAN), bf16)] * 2 + [((16, ROWS, CHAN), f32), ((GROUPS * COLROWS, CHAN), f32), rows],
+        [((16, ROWS, CHAN), bf16)] * 2 + [((16, ROWS, CHAN), f32), rows],
         [
             ext,
             ext,
@@ -575,12 +625,13 @@
             ((GROUPS, TERMS, NJ_REST), bf16),
             ((GROUPS, 8, COLROWS, NJ_REST), f32),
             rows,
-            ((2, TERMS, CHAN), bf16),
-            ((2, 16, NJ_REST), bf16),
+            ((GROUPS * COLROWS, CHAN), f32),
+            ((4, TERMS, CHAN), bf16),
+            ((4, 8, NJ_REST), f32),
+            ((4, 2, NJ_REST, CHAN), f32),
         ],
         (
-            layer, zl, zh, sums, rest_off, pick, spread, radial_weights,
-            coupling.transpose(1, 0, 2), mixing, hidden_weights.T, output_weights.reshape(1, -1),
+            layer, zl, zh, sums, pack,
         ),
         REST_LIMIT,
         6 * TERMS * NJ_REST * CHAN * GROUPS,
@@ -589,8 +640,8 @@
         near_back_kernel,
         "near_back",
         [((16, ROWS, CHAN), f32)],
-        [near_ext, near_ext, ((2, TERMS, CHAN), bf16), ((2, 16, NJ_NEAR), bf16)],
-        (near_edges, near_win, near_saved, d_sums, rest_mid, spread, radial_weights),
+        [near_ext, near_ext, ((4, TERMS, CHAN), bf16), ((4, 8, NJ_NEAR), f32), ((4, 2, NJ_NEAR, CHAN), f32)],
+        (near_edges, near_win, near_saved, d_sums, rest_mid, pack),
         NEAR_LIMIT,
         4 * TERMS * NJ_NEAR * CHAN * GROUPS,
     )
@@ -601,15 +652,14 @@
     def summed(part):
         return mid[part] + from_below[part].astype(f32) + from_above[part].astype(f32)
 
-    y_below, y_above = shifted(summed(slice(0, 1)).astype(bf16), summed(slice(3, 4)).astype(bf16), "gy")
-    strip = summed(slice(1, 3)) + jnp.concatenate([y_below, y_above], axis=0).astype(f32)
-    x_below, x_above = shifted(strip[:, :1].astype(bf16), strip[:, 3:].astype(bf16), "gx")
+    strip = summed(slice(0, 2)) + moved(summed(slice(2, 4)).astype(bf16), "gy", 1).astype(f32)
+    arrived = moved(strip[:, 2:].astype(bf16), "gx", 1)
     atom_energy, forces, feature_grad = call(
         finish_kernel,
         "finish",
         [((4, 1, SLOTS), f32), ((12, 1, SLOTS), f32), ((4, SLOTS, CHAN), f32)],
         [],
-        (count, pos, strip, x_below.reshape(2, ROWS, CHAN), x_above.reshape(2, ROWS, CHAN), energy),
+        (count, pos, strip, arrived),
         8 << 10,
         10**7,
         (SMEM,),

time: 83.7 us -> 74.4 us (0.89)
  waiting for transfers between devices: 22.8 us -> 17.8 us
  Pallas kernels: 34.2 us -> 29.9 us
    ppermute x12 -> x8, waiting for transfers between devices: 22.8 us -> 17.8 us  [moved(): lax.ppermute(part, axis, [(i, (i + step) % count) for i in range(count)])]
    pallas_call x5, Pallas kernels: 34.2 us -> 29.9 us  [call(): pl.pallas_call(kernel, name=name, out_shape=shapes, in_specs=[*spaces] +...]
    unnamed x26 -> x8, local copies, waits for them, and re-layouts: 2.19 us -> 1.87 us
    ppermute x12 -> x8, starting transfers between devices: 21.3 us -> 21 us  [moved(): lax.ppermute(part, axis, [(i, (i + step) % count) for i in range(count)])]
  transfers between devices with their start and end apart: 12 -> 8, of which waited for: 11 -> 7; matrix products, arithmetic and copies ran while one was open for 0% -> 0% of each run, Pallas kernels for 13% -> 13%
where the time goes in v2:
time: 74.4 us; the launch traced here: 73.3 us
  Pallas kernels  29.9 us (40%)
  starting transfers between devices  21 us (28%)
  waiting for transfers between devices  17.8 us (24%)
  other arithmetic  1.95 us (3%)
  local copies, waits for them, and re-layouts  1.92 us (3%)
    pallas_call x5, Pallas kernels, call(): pl.pallas_call(kernel, name=name, out_shape=shapes, in_specs=[*spaces] +...  29.9 us
    ppermute x8, starting transfers between devices, moved(): lax.ppermute(part, axis, [(i, (i + step) % count) for i in range(count)])  21 us
    ppermute x8, waiting for transfers between devices, moved(): lax.ppermute(part, axis, [(i, (i + step) % count) for i in range(count)])  17.8 us
    unnamed x8, local copies, waits for them, and re-layouts  1.87 us
  transfers between devices with their start and end apart: 8, of which 7 were waited for; matrix products, arithmetic and copies ran while one was open for 0% of the time, Pallas kernels for 13%

profile of v2, /device:TPU:1, one launch (start us, length us, event | category | flops | bytes accessed | tf_op | source)
XLA Modules:
  0.0 73.3 jit_solution(1948902849735730890)
XLA Ops:
  0.6 2.1 %sort.1 = (bf16[4,72,128]{2,1,0:T(8,128)(2,1)}, f32[400,128]{1,0:T(8,128)}) custom-call(s32[2,1,2]{2,1,0:T(1,128)} %bitcast.29, f32[12,1,64]{2,1,0:T(1,128)} %bitcast.27, s32[4,1,64]{2,1,0:T(1,128)} %bitcast.44, bf16[4,64,128]{2,1,0:T(8,128)(2,1)} %bitcast.40, f32[16,128]{1,0:T(8,128)} %bitcast.42, f32[10,3,128]{2,1,0:T(4,128)} %bitcast.41, ...), custom_call_target="tpu_custom_call" | custom-call | flops 10000000 | bytes 278528 | tf_op jit(solution)/shard_map/sort/pallas_call | solution.py:552
  2.7 6.0 %collective-permute-start = (bf16[2,2,72,128]{3,2,1,0:T(8,128)(2,1)}, bf16[2,2,72,128]{3,2,1,0:T(8,128)(2,1)S(1)}, u32[]{:S(2)}, u32[]{:S(2)}) collective-permute-start(bf16[2,2,72,128]{3,2,1,0:T(8,128)(2,1)} %bitcast.37), channel_id=1, source_target_pairs={{0,224},{32,0},{64,32},{96,64},{128,96},{160,128},{192,160},{224,1... | collective-permute-start | bytes 221192 | tf_op jit(solution)/shard_map/ppermute | solution.py:542
  8.7 1.7 %collective-permute-done = bf16[2,2,72,128]{3,2,1,0:T(8,128)(2,1)S(1)} collective-permute-done((bf16[2,2,72,128]{3,2,1,0:T(8,128)(2,1)}, bf16[2,2,72,128]{3,2,1,0:T(8,128)(2,1)S(1)}, u32[]{:S(2)}, u32[]{:S(2)}) %collective-permute-start) | collective-permute-done | bytes 73760 | tf_op jit(solution)/shard_map/ppermute | solution.py:542
  10.4 0.9 %pad_maximum_fusion.1 = bf16[2,4,72,128]{3,2,1,0:T(8,128)(2,1)S(1)} fusion(bf16[2,2,72,128]{3,2,1,0:T(8,128)(2,1)S(1)} %collective-permute-done, bf16[2,2,72,128]{3,2,1,0:T(8,128)(2,1)} %bitcast.38), kind=kLoop, calls=%fused_computation.4 | loop fusion | flops 73728 | bytes 294912 | tf_op jit(solution)/shard_map/concatenate | solution.py:599
  11.3 1.7 %collective-permute-start.1 = (bf16[2,4,72,128]{3,2,1,0:T(8,128)(2,1)S(1)}, bf16[2,4,72,128]{3,2,1,0:T(8,128)(2,1)S(1)}, u32[]{:S(2)}, u32[]{:S(2)}) collective-permute-start(bf16[2,4,72,128]{3,2,1,0:T(8,128)(2,1)S(1)} %pad_maximum_fusion.1), channel_id=1, source_target_pairs={{0,24},{8,0},{16,8},{24,16},{1,25},{9,1},{17,9},{25,17},{2,26},{10... | collective-permute-start | bytes 442376 | tf_op jit(solution)/shard_map/ppermute | solution.py:542
  13.0 3.0 %collective-permute-done.1 = bf16[2,4,72,128]{3,2,1,0:T(8,128)(2,1)S(1)} collective-permute-done((bf16[2,4,72,128]{3,2,1,0:T(8,128)(2,1)S(1)}, bf16[2,4,72,128]{3,2,1,0:T(8,128)(2,1)S(1)}, u32[]{:S(2)}, u32[]{:S(2)}) %collective-permute-start.1) | collective-permute-done | bytes 147488 | tf_op jit(solution)/shard_map/ppermute | solution.py:542
  16.1 0.9 %pad_maximum_fusion = bf16[4,4,72,128]{3,2,1,0:T(8,128)(2,1)S(1)} fusion(bf16[2,4,72,128]{3,2,1,0:T(8,128)(2,1)S(1)} %collective-permute-done.1, bf16[2,2,72,128]{3,2,1,0:T(8,128)(2,1)S(1)} %collective-permute-done, bf16[2,2,72,128]{3,2,1,0:T(8,128)(2,1)} %bitcast.39), kind=kLoop, calls=%fused_computation | loop fusion | flops 294912 | bytes 589824 | tf_op jit(solution)/shard_map/concatenate | solution.py:600
  17.0 5.7 %collective-permute-start.3 = (bf16[4,4,72,128]{3,2,1,0:T(8,128)(2,1)S(1)}, bf16[4,4,72,128]{3,2,1,0:T(8,128)(2,1)S(1)}, u32[]{:S(2)}, u32[]{:S(2)}) collective-permute-start(bf16[4,4,72,128]{3,2,1,0:T(8,128)(2,1)S(1)} %pad_maximum_fusion), channel_id=1, source_target_pairs={{0,7},{1,0},{2,1},{3,2},{4,3},{5,4},{6,5},{7,6},{8,15},{9,8},{10,9... | collective-permute-start | bytes 884744 | tf_op jit(solution)/shard_map/ppermute | solution.py:542
  22.6 0.0 collective-permute-start.2
  22.6 0.0 copy-start
  22.6 0.9 %copy-done = f32[400,128]{1,0:T(8,128)S(1)} copy-done((f32[400,128]{1,0:T(8,128)S(1)}, f32[400,128]{1,0:T(8,128)}, u32[]{:S(2)}) %copy-start) | copy-done | bytes 204824
  23.6 3.7 %near.1 = (f32[4,256,128]{2,1,0:T(8,128)S(1)}, bf16[16,256,128]{2,1,0:T(8,128)(2,1)S(1)}, bf16[16,512,256]{2,1,0:T(8,128)(2,1)S(1)}, f32[16,8,16,256]{3,2,1,0:T(8,128)S(1)}) custom-call(bf16[16,72,128]{2,1,0:T(8,128)(2,1)S(1)} %bitcast.25, f32[400,128]{1,0:T(8,128)S(1)} %copy-done), custom_call_target="tpu_custom_call" | custom-call | flops 536870912 | bytes 7864320 | tf_op jit(solution)/shard_map/near/pallas_call | solution.py:552
  27.2 2.2 %collective-permute-done.3 = bf16[4,4,72,128]{3,2,1,0:T(8,128)(2,1)S(1)} collective-permute-done((bf16[4,4,72,128]{3,2,1,0:T(8,128)(2,1)S(1)}, bf16[4,4,72,128]{3,2,1,0:T(8,128)(2,1)S(1)}, u32[]{:S(2)}, u32[]{:S(2)}) %collective-permute-start.3) | collective-permute-done | bytes 294944 | tf_op jit(solution)/shard_map/ppermute | solution.py:542
  29.4 3.1 %collective-permute-done.2 = bf16[4,4,72,128]{3,2,1,0:T(8,128)(2,1)S(1)} collective-permute-done((bf16[4,4,72,128]{3,2,1,0:T(8,128)(2,1)S(1)}, bf16[4,4,72,128]{3,2,1,0:T(8,128)(2,1)S(1)}, u32[]{:S(2)}, u32[]{:S(2)}) %collective-permute-start.2) | collective-permute-done | bytes 294944 | tf_op jit(solution)/shard_map/ppermute | solution.py:542
  32.6 0.0 copy-start.1
  32.6 0.9 %copy-done.1 = f32[400,128]{1,0:T(8,128)S(1)} copy-done((f32[400,128]{1,0:T(8,128)S(1)}, f32[400,128]{1,0:T(8,128)}, u32[]{:S(2)}) %copy-start.1) | copy-done | bytes 204824
  33.5 16.6 %rest.1 = (bf16[16,72,128]{2,1,0:T(8,128)(2,1)S(1)}, bf16[16,72,128]{2,1,0:T(8,128)(2,1)S(1)}, f32[16,72,128]{2,1,0:T(8,128)S(1)}, f32[4,256,128]{2,1,0:T(8,128)S(1)}) custom-call(bf16[16,72,128]{2,1,0:T(8,128)(2,1)S(1)} %bitcast.26, bf16[16,72,128]{2,1,0:T(8,128)(2,1)S(1)} %bitcast.34, bf16[16,72,128]{2,1,0:T(8,128)(2,1)S(1)} %bitcast.33, ...), custom_call_target="tpu_custom_call" | custom-call | flops 3221225472 | bytes 1703936 | tf_op jit(solution)/shard_map/rest/pallas_call | solution.py:552
  50.1 0.1 collective-permute-start.4
  50.2 2.7 %collective-permute-start.5 = (bf16[4,4,72,128]{3,2,1,0:T(8,128)(2,1)S(1)}, bf16[4,4,72,128]{3,2,1,0:T(8,128)(2,1)S(1)}, u32[]{:S(2)}, u32[]{:S(2)}) collective-permute-start(bf16[4,4,72,128]{3,2,1,0:T(8,128)(2,1)S(1)} %bitcast.31), channel_id=1, source_target_pairs={{0,7},{1,0},{2,1},{3,2},{4,3},{5,4},{6,5},{7,6},{8,15},{9,8},{10,9... | collective-permute-start | bytes 884744 | tf_op jit(solution)/shard_map/ppermute | solution.py:542
  52.9 0.0 copy-start.2
  52.9 0.0 copy-start.3
  52.9 5.9 %near_back.1 = f32[16,72,128]{2,1,0:T(8,128)S(1)} custom-call(bf16[16,512,256]{2,1,0:T(8,128)(2,1)S(1)} %get-tuple-element.18.edges, bf16[16,256,128]{2,1,0:T(8,128)(2,1)S(1)} %get-tuple-element.19.feat_win, f32[16,8,16,256]{3,2,1,0:T(8,128)S(1)} %get-tuple-element.20.saved, f32[4,256,128]{2,1,0:T(8,128)S(1)} %get-tuple-element.22.d_sums, ...), custom_call_target="tpu_custom_call" | custom-call | flops 1073741824 | bytes 589824 | tf_op jit(solution)/shard_map/near_back/pallas_call | solution.py:552
  58.8 0.5 collective-permute-done.4
  59.3 0.0 collective-permute-done.5
  59.3 0.1 add_convert_fusion
  59.3 2.3 %collective-permute-start.6 = (bf16[2,4,72,128]{3,2,1,0:T(8,128)(2,1)S(1)}, bf16[2,4,72,128]{3,2,1,0:T(8,128)(2,1)S(1)}, u32[]{:S(2)}, u32[]{:S(2)}) collective-permute-start(bf16[2,4,72,128]{3,2,1,0:T(8,128)(2,1)S(1)} %add_convert_fusion), channel_id=1, source_target_pairs={{0,8},{8,16},{16,24},{24,0},{1,9},{9,17},{17,25},{25,1},{2,10},{10... | collective-permute-start | bytes 442376 | tf_op jit(solution)/shard_map/ppermute | solution.py:542
  61.6 2.1 %collective-permute-done.6 = bf16[2,4,72,128]{3,2,1,0:T(8,128)(2,1)S(1)} collective-permute-done((bf16[2,4,72,128]{3,2,1,0:T(8,128)(2,1)S(1)}, bf16[2,4,72,128]{3,2,1,0:T(8,128)(2,1)S(1)}, u32[]{:S(2)}, u32[]{:S(2)}) %collective-permute-start.6) | collective-permute-done | bytes 147488 | tf_op jit(solution)/shard_map/ppermute | solution.py:542
  63.7 0.1 convert_add_fusion.mid_ref
  63.8 2.7 %collective-permute-start.7 = (bf16[2,2,72,128]{3,2,1,0:T(8,128)(2,1)S(1)}, bf16[2,2,72,128]{3,2,1,0:T(8,128)(2,1)S(1)}, u32[]{:S(2)}, u32[]{:S(2)}) collective-permute-start(bf16[2,2,72,128]{3,2,1,0:T(8,128)(2,1)S(1)} %slice.49), channel_id=1, source_target_pairs={{0,32},{32,64},{64,96},{96,128},{128,160},{160,192},{192,224},{224... | collective-permute-start | bytes 221192 | tf_op jit(solution)/shard_map/ppermute | solution.py:542
  66.5 5.2 %collective-permute-done.7.arrived_ref = bf16[2,2,72,128]{3,2,1,0:T(8,128)(2,1)S(1)} collective-permute-done((bf16[2,2,72,128]{3,2,1,0:T(8,128)(2,1)S(1)}, bf16[2,2,72,128]{3,2,1,0:T(8,128)(2,1)S(1)}, u32[]{:S(2)}, u32[]{:S(2)}) %collective-permute-start.7) | collective-permute-done | bytes 73760 | tf_op jit(solution)/shard_map/ppermute | solution.py:542
  71.6 0.0 copy-done.2
  71.6 0.0 copy-done.3
  71.6 1.7 %finish.1 = (f32[4,1,64]{2,1,0:T(1,128)}, f32[12,1,64]{2,1,0:T(1,128)}, f32[4,64,128]{2,1,0:T(8,128)}) custom-call(s32[2,1,2]{2,1,0:T(1,128)S(1)} %bitcast.30, f32[12,1,64]{2,1,0:T(1,128)S(1)} %bitcast.28, f32[2,4,72,128]{3,2,1,0:T(8,128)S(1)} %convert_add_fusion.mid_ref, bf16[2,2,72,128]{3,2,1,0:T(8,128)(2,1)S(1)} %collective-permute-done.7.arrived_ref), custom_call_target="tpu_custom_call" | custom-call | flops 10000000 | bytes 135168 | tf_op jit(solution)/shard_map/finish/pallas_call | solution.py:552
  (2 shorter events, 0.1 us)
Async XLA Ops:
  2.7 7.7 %collective-permute-start = (bf16[2,2,72,128]{3,2,1,0:T(8,128)(2,1)}, bf16[2,2,72,128]{3,2,1,0:T(8,128)(2,1)S(1)}, u32[]{:S(2)}, u32[]{:S(2)}) collective-permute-start(bf16[2,2,72,128]{3,2,1,0:T(8,128)(2,1)} %bitcast.37), channel_id=1, source_target_pairs={{0,224},{32,0},{64,32},{96,64},{128,96},{160,128},{192,160},{224,1... | collective-permute-start | bytes 221192 | tf_op jit(solution)/shard_map/ppermute | solution.py:542
  11.3 4.7 %collective-permute-start.1 = (bf16[2,4,72,128]{3,2,1,0:T(8,128)(2,1)S(1)}, bf16[2,4,72,128]{3,2,1,0:T(8,128)(2,1)S(1)}, u32[]{:S(2)}, u32[]{:S(2)}) collective-permute-start(bf16[2,4,72,128]{3,2,1,0:T(8,128)(2,1)S(1)} %pad_maximum_fusion.1), channel_id=1, source_target_pairs={{0,24},{8,0},{16,8},{24,16},{1,25},{9,1},{17,9},{25,17},{2,26},{10... | collective-permute-start | bytes 442376 | tf_op jit(solution)/shard_map/ppermute | solution.py:542
  17.0 12.4 %collective-permute-start.3 = (bf16[4,4,72,128]{3,2,1,0:T(8,128)(2,1)S(1)}, bf16[4,4,72,128]{3,2,1,0:T(8,128)(2,1)S(1)}, u32[]{:S(2)}, u32[]{:S(2)}) collective-permute-start(bf16[4,4,72,128]{3,2,1,0:T(8,128)(2,1)S(1)} %pad_maximum_fusion), channel_id=1, source_target_pairs={{0,7},{1,0},{2,1},{3,2},{4,3},{5,4},{6,5},{7,6},{8,15},{9,8},{10,9... | collective-permute-start | bytes 884744 | tf_op jit(solution)/shard_map/ppermute | solution.py:542
  22.6 9.9 %collective-permute-start.2 = (bf16[4,4,72,128]{3,2,1,0:T(8,128)(2,1)S(1)}, bf16[4,4,72,128]{3,2,1,0:T(8,128)(2,1)S(1)}, u32[]{:S(2)}, u32[]{:S(2)}) collective-permute-start(bf16[4,4,72,128]{3,2,1,0:T(8,128)(2,1)S(1)} %pad_maximum_fusion), channel_id=1, source_target_pairs={{0,1},{1,2},{2,3},{3,4},{4,5},{5,6},{6,7},{7,0},{8,9},{9,10},{10,1... | collective-permute-start | bytes 884744 | tf_op jit(solution)/shard_map/ppermute | solution.py:542
  22.6 0.9 %copy-start = (f32[400,128]{1,0:T(8,128)S(1)}, f32[400,128]{1,0:T(8,128)}, u32[]{:S(2)}) copy-start(f32[400,128]{1,0:T(8,128)} %get-tuple-element.17.pack_ref) | copy-start | bytes 614404
  32.6 0.9 %copy-start.1 = (f32[400,128]{1,0:T(8,128)S(1)}, f32[400,128]{1,0:T(8,128)}, u32[]{:S(2)}) copy-start(f32[400,128]{1,0:T(8,128)} %get-tuple-element.17.pack_ref) | copy-start | bytes 614404
  50.1 9.1 %collective-permute-start.4 = (bf16[4,4,72,128]{3,2,1,0:T(8,128)(2,1)S(1)}, bf16[4,4,72,128]{3,2,1,0:T(8,128)(2,1)S(1)}, u32[]{:S(2)}, u32[]{:S(2)}) collective-permute-start(bf16[4,4,72,128]{3,2,1,0:T(8,128)(2,1)S(1)} %bitcast.32), channel_id=1, source_target_pairs={{0,1},{1,2},{2,3},{3,4},{4,5},{5,6},{6,7},{7,0},{8,9},{9,10},{10,1... | collective-permute-start | bytes 884744 | tf_op jit(solution)/shard_map/ppermute | solution.py:542
  50.2 9.1 %collective-permute-start.5 = (bf16[4,4,72,128]{3,2,1,0:T(8,128)(2,1)S(1)}, bf16[4,4,72,128]{3,2,1,0:T(8,128)(2,1)S(1)}, u32[]{:S(2)}, u32[]{:S(2)}) collective-permute-start(bf16[4,4,72,128]{3,2,1,0:T(8,128)(2,1)S(1)} %bitcast.31), channel_id=1, source_target_pairs={{0,7},{1,0},{2,1},{3,2},{4,3},{5,4},{6,5},{7,6},{8,15},{9,8},{10,9... | collective-permute-start | bytes 884744 | tf_op jit(solution)/shard_map/ppermute | solution.py:542
  52.9 18.7 %copy-start.2 = (f32[2,2,1,3,64]{4,2,3,1,0:T(1,128)S(1)}, f32[2,2,1,3,64]{4,2,3,1,0:T(1,128)}, u32[]{:S(2)}) copy-start(f32[2,2,1,3,64]{4,2,3,1,0:T(1,128)} %param.10) | copy-start | bytes 9220
  52.9 18.7 %copy-start.3 = (s32[2,2,1]{1,2,0:T(1,128)S(1)}, s32[2,2,1]{1,2,0:T(1,128)}, u32[]{:S(2)}) copy-start(s32[2,2,1]{1,2,0:T(1,128)} %param.11) | copy-start | bytes 52
  59.3 4.4 %collective-permute-start.6 = (bf16[2,4,72,128]{3,2,1,0:T(8,128)(2,1)S(1)}, bf16[2,4,72,128]{3,2,1,0:T(8,128)(2,1)S(1)}, u32[]{:S(2)}, u32[]{:S(2)}) collective-permute-start(bf16[2,4,72,128]{3,2,1,0:T(8,128)(2,1)S(1)} %add_convert_fusion), channel_id=1, source_target_pairs={{0,8},{8,16},{16,24},{24,0},{1,9},{9,17},{17,25},{25,1},{2,10},{10... | collective-permute-start | bytes 442376 | tf_op jit(solution)/shard_map/ppermute | solution.py:542
  63.8 7.8 %collective-permute-start.7 = (bf16[2,2,72,128]{3,2,1,0:T(8,128)(2,1)S(1)}, bf16[2,2,72,128]{3,2,1,0:T(8,128)(2,1)S(1)}, u32[]{:S(2)}, u32[]{:S(2)}) collective-permute-start(bf16[2,2,72,128]{3,2,1,0:T(8,128)(2,1)S(1)} %slice.49), channel_id=1, source_target_pairs={{0,32},{32,64},{64,96},{96,128},{128,160},{160,192},{192,224},{224... | collective-permute-start | bytes 221192 | tf_op jit(solution)/shard_map/ppermute | solution.py:542

commit v3 on v2

--- a/solution.py
+++ b/solution.py
@@ -500,6 +500,11 @@
     lax.fori_loop(0, 16, gather_cell, 0)
 
 
+def stage_kernel(block_ref, pack_ref, block_out, pack_out):
+    block_out[...] = block_ref[...]
+    pack_out[...] = pack_ref[...]
+
+
 def finish_kernel(count_ref, pos_ref, mid_ref, arrived_ref, e_ref, f_ref, g_ref):
     lane = lax.broadcasted_iota(jnp.int32, (EXTRA, CHAN), 1)
     for cell in range(4):
@@ -596,7 +601,17 @@
         (HBM,) * 10,
     )
     block = block.reshape(2, 2, ROWS, CHAN)
-    wide = jnp.concatenate([block, moved(block, "gx", -1)], axis=1)
+    arrived = moved(block, "gx", -1)
+    block, pack = call(
+        stage_kernel,
+        "stage",
+        [((4, ROWS, CHAN), bf16), ((PACKED, CHAN), f32)],
+        [],
+        (block.reshape(4, ROWS, CHAN), pack),
+        4 << 10,
+        10**6,
+    )
+    wide = jnp.concatenate([block.reshape(2, 2, ROWS, CHAN), arrived], axis=1)
     layer = jnp.concatenate([wide, moved(wide, "gy", -1)], axis=0)
     zl, zh = shifted(layer, layer, "gz")
     layer, zl, zh = (part.reshape(16, ROWS, CHAN) for part in (layer, zl, zh))

time: 74.4 us -> 71.7 us (0.964)
  other arithmetic: 1.95 us -> 0.17 us
    concatenate x1, other arithmetic: 0.91 us -> 0.03 us  [body(): layer = jnp.concatenate([wide, moved(wide, 'gy', -1)], axis=0)]
    concatenate x1, other arithmetic: 0.9 us -> 0.02 us  [body(): wide = jnp.concatenate([block.reshape(2, 2, ROWS, CHAN), arrived], axis=1)]
    pallas_call x5 -> x6, Pallas kernels: 29.9 us -> 29.9 us  [call(): pl.pallas_call(kernel, name=name, out_shape=shapes, in_specs=[*spaces] +...]
  transfers between devices with their start and end apart: 8 -> 8, of which waited for: 7 -> 6; matrix products, arithmetic and copies ran while one was open for 0% -> 0% of each run, Pallas kernels for 13% -> 14%
where the time goes in v3:
time: 71.7 us; the launch traced here: 70.6 us
  Pallas kernels  29.9 us (42%)
  starting transfers between devices  20.7 us (29%)
  waiting for transfers between devices  17.2 us (24%)
  local copies, waits for them, and re-layouts  1.87 us (3%)
  between operations  0.72 us (1%)
    pallas_call x6, Pallas kernels, call(): pl.pallas_call(kernel, name=name, out_shape=shapes, in_specs=[*spaces] +...  29.9 us
    ppermute x8, starting transfers between devices, moved(): lax.ppermute(part, axis, [(i, (i + step) % count) for i in range(count)])  20.7 us
    ppermute x8, waiting for transfers between devices, moved(): lax.ppermute(part, axis, [(i, (i + step) % count) for i in range(count)])  17.2 us
    unnamed x8, local copies, waits for them, and re-layouts  1.82 us
  transfers between devices with their start and end apart: 8, of which 6 were waited for; matrix products, arithmetic and copies ran while one was open for 0% of the time, Pallas kernels for 14%

profile of v3, /device:TPU:1, one launch (start us, length us, event | category | flops | bytes accessed | tf_op | source)
XLA Modules:
  0.0 70.6 jit_solution(13932875673123176057)
XLA Ops:
  0.6 2.1 %sort.1 = (bf16[4,72,128]{2,1,0:T(8,128)(2,1)}, f32[400,128]{1,0:T(8,128)}) custom-call(s32[2,1,2]{2,1,0:T(1,128)} %bitcast.33, f32[12,1,64]{2,1,0:T(1,128)} %bitcast.31, s32[4,1,64]{2,1,0:T(1,128)} %bitcast.45, bf16[4,64,128]{2,1,0:T(8,128)(2,1)} %bitcast.41, f32[16,128]{1,0:T(8,128)} %bitcast.43, f32[10,3,128]{2,1,0:T(4,128)} %bitcast.42, ...), custom_call_target="tpu_custom_call" | custom-call | flops 10000000 | bytes 278528 | tf_op jit(solution)/shard_map/sort/pallas_call | solution.py:557
  2.7 6.0 %collective-permute-start = (bf16[2,2,72,128]{3,2,1,0:T(8,128)(2,1)}, bf16[2,2,72,128]{3,2,1,0:T(8,128)(2,1)S(1)}, u32[]{:S(2)}, u32[]{:S(2)}) collective-permute-start(bf16[2,2,72,128]{3,2,1,0:T(8,128)(2,1)} %bitcast.30), channel_id=1, source_target_pairs={{0,224},{32,0},{64,32},{96,64},{128,96},{160,128},{192,160},{224,1... | collective-permute-start | bytes 221192 | tf_op jit(solution)/shard_map/ppermute | solution.py:547
  8.7 0.0 copy-start
  8.7 0.9 %copy-done = f32[400,128]{1,0:T(8,128)S(1)} copy-done((f32[400,128]{1,0:T(8,128)S(1)}, f32[400,128]{1,0:T(8,128)}, u32[]{:S(2)}) %copy-start) | copy-done | bytes 204824
  9.6 0.0 copy-start.1
  9.6 0.9 %copy-done.1 = bf16[4,72,128]{2,1,0:T(8,128)(2,1)S(1)} copy-done((bf16[4,72,128]{2,1,0:T(8,128)(2,1)S(1)}, bf16[4,72,128]{2,1,0:T(8,128)(2,1)}, u32[]{:S(2)}) %copy-start.1) | copy-done | bytes 73752
  10.5 0.0 collective-permute-done
  10.6 1.6 %collective-permute-start.1 = (bf16[2,4,72,128]{3,2,1,0:T(8,128)(2,1)S(1)}, bf16[2,4,72,128]{3,2,1,0:T(8,128)(2,1)S(1)}, u32[]{:S(2)}, u32[]{:S(2)}) collective-permute-start(bf16[2,4,72,128]{3,2,1,0:T(8,128)(2,1)S(1)} %pad_maximum_fusion.1), channel_id=1, source_target_pairs={{0,24},{8,0},{16,8},{24,16},{1,25},{9,1},{17,9},{25,17},{2,26},{10... | collective-permute-start | bytes 442376 | tf_op jit(solution)/shard_map/ppermute | solution.py:547
  12.1 3.1 %collective-permute-done.1 = bf16[2,4,72,128]{3,2,1,0:T(8,128)(2,1)S(1)} collective-permute-done((bf16[2,4,72,128]{3,2,1,0:T(8,128)(2,1)S(1)}, bf16[2,4,72,128]{3,2,1,0:T(8,128)(2,1)S(1)}, u32[]{:S(2)}, u32[]{:S(2)}) %collective-permute-start.1) | collective-permute-done | bytes 147488 | tf_op jit(solution)/shard_map/ppermute | solution.py:547
  15.3 5.7 %collective-permute-start.3 = (bf16[4,4,72,128]{3,2,1,0:T(8,128)(2,1)S(1)}, bf16[4,4,72,128]{3,2,1,0:T(8,128)(2,1)S(1)}, u32[]{:S(2)}, u32[]{:S(2)}) collective-permute-start(bf16[4,4,72,128]{3,2,1,0:T(8,128)(2,1)S(1)} %pad_maximum_fusion), channel_id=1, source_target_pairs={{0,7},{1,0},{2,1},{3,2},{4,3},{5,4},{6,5},{7,6},{8,15},{9,8},{10,9... | collective-permute-start | bytes 884744 | tf_op jit(solution)/shard_map/ppermute | solution.py:547
  20.9 0.0 collective-permute-start.2
  20.9 3.7 %near.1 = (f32[4,256,128]{2,1,0:T(8,128)S(1)}, bf16[16,256,128]{2,1,0:T(8,128)(2,1)S(1)}, bf16[16,512,256]{2,1,0:T(8,128)(2,1)S(1)}, f32[16,8,16,256]{3,2,1,0:T(8,128)S(1)}) custom-call(bf16[16,72,128]{2,1,0:T(8,128)(2,1)S(1)} %bitcast.28, f32[400,128]{1,0:T(8,128)S(1)} %get-tuple-element.21.pack_ref), custom_call_target="tpu_custom_call" | custom-call | flops 536870912 | bytes 7864320 | tf_op jit(solution)/shard_map/near/pallas_call | solution.py:557
  24.6 3.1 %collective-permute-done.3 = bf16[4,4,72,128]{3,2,1,0:T(8,128)(2,1)S(1)} collective-permute-done((bf16[4,4,72,128]{3,2,1,0:T(8,128)(2,1)S(1)}, bf16[4,4,72,128]{3,2,1,0:T(8,128)(2,1)S(1)}, u32[]{:S(2)}, u32[]{:S(2)}) %collective-permute-start.3) | collective-permute-done | bytes 294944 | tf_op jit(solution)/shard_map/ppermute | solution.py:547
  27.7 3.2 %collective-permute-done.2 = bf16[4,4,72,128]{3,2,1,0:T(8,128)(2,1)S(1)} collective-permute-done((bf16[4,4,72,128]{3,2,1,0:T(8,128)(2,1)S(1)}, bf16[4,4,72,128]{3,2,1,0:T(8,128)(2,1)S(1)}, u32[]{:S(2)}, u32[]{:S(2)}) %collective-permute-start.2) | collective-permute-done | bytes 294944 | tf_op jit(solution)/shard_map/ppermute | solution.py:547
  30.9 16.7 %rest.1 = (bf16[16,72,128]{2,1,0:T(8,128)(2,1)S(1)}, bf16[16,72,128]{2,1,0:T(8,128)(2,1)S(1)}, f32[16,72,128]{2,1,0:T(8,128)S(1)}, f32[4,256,128]{2,1,0:T(8,128)S(1)}) custom-call(bf16[16,72,128]{2,1,0:T(8,128)(2,1)S(1)} %bitcast.29, bf16[16,72,128]{2,1,0:T(8,128)(2,1)S(1)} %bitcast.38, bf16[16,72,128]{2,1,0:T(8,128)(2,1)S(1)} %bitcast.37, ...), custom_call_target="tpu_custom_call" | custom-call | flops 3221225472 | bytes 1703936 | tf_op jit(solution)/shard_map/rest/pallas_call | solution.py:557
  47.6 0.1 collective-permute-start.4
  47.6 2.7 %collective-permute-start.5 = (bf16[4,4,72,128]{3,2,1,0:T(8,128)(2,1)S(1)}, bf16[4,4,72,128]{3,2,1,0:T(8,128)(2,1)S(1)}, u32[]{:S(2)}, u32[]{:S(2)}) collective-permute-start(bf16[4,4,72,128]{3,2,1,0:T(8,128)(2,1)S(1)} %bitcast.35), channel_id=1, source_target_pairs={{0,7},{1,0},{2,1},{3,2},{4,3},{5,4},{6,5},{7,6},{8,15},{9,8},{10,9... | collective-permute-start | bytes 884744 | tf_op jit(solution)/shard_map/ppermute | solution.py:547
  50.3 0.0 copy-start.2
  50.3 0.0 copy-start.3
  50.3 5.8 %near_back.1 = f32[16,72,128]{2,1,0:T(8,128)S(1)} custom-call(bf16[16,512,256]{2,1,0:T(8,128)(2,1)S(1)} %get-tuple-element.22.edges, bf16[16,256,128]{2,1,0:T(8,128)(2,1)S(1)} %get-tuple-element.23.feat_win, f32[16,8,16,256]{3,2,1,0:T(8,128)S(1)} %get-tuple-element.24.saved, f32[4,256,128]{2,1,0:T(8,128)S(1)} %get-tuple-element.26.d_sums, ...), custom_call_target="tpu_custom_call" | custom-call | flops 1073741824 | bytes 589824 | tf_op jit(solution)/shard_map/near_back/pallas_call | solution.py:557
  56.2 0.5 collective-permute-done.4
  56.8 0.0 collective-permute-done.5
  56.8 0.1 add_convert_fusion
  56.8 2.1 %collective-permute-start.6 = (bf16[2,4,72,128]{3,2,1,0:T(8,128)(2,1)S(1)}, bf16[2,4,72,128]{3,2,1,0:T(8,128)(2,1)S(1)}, u32[]{:S(2)}, u32[]{:S(2)}) collective-permute-start(bf16[2,4,72,128]{3,2,1,0:T(8,128)(2,1)S(1)} %add_convert_fusion), channel_id=1, source_target_pairs={{0,8},{8,16},{16,24},{24,0},{1,9},{9,17},{17,25},{25,1},{2,10},{10... | collective-permute-start | bytes 442376 | tf_op jit(solution)/shard_map/ppermute | solution.py:547
  59.0 2.1 %collective-permute-done.6 = bf16[2,4,72,128]{3,2,1,0:T(8,128)(2,1)S(1)} collective-permute-done((bf16[2,4,72,128]{3,2,1,0:T(8,128)(2,1)S(1)}, bf16[2,4,72,128]{3,2,1,0:T(8,128)(2,1)S(1)}, u32[]{:S(2)}, u32[]{:S(2)}) %collective-permute-start.6) | collective-permute-done | bytes 147488 | tf_op jit(solution)/shard_map/ppermute | solution.py:547
  61.1 0.1 convert_add_fusion.mid_ref
  61.2 2.6 %collective-permute-start.7 = (bf16[2,2,72,128]{3,2,1,0:T(8,128)(2,1)S(1)}, bf16[2,2,72,128]{3,2,1,0:T(8,128)(2,1)S(1)}, u32[]{:S(2)}, u32[]{:S(2)}) collective-permute-start(bf16[2,2,72,128]{3,2,1,0:T(8,128)(2,1)S(1)} %slice.49), channel_id=1, source_target_pairs={{0,32},{32,64},{64,96},{96,128},{128,160},{160,192},{192,224},{224... | collective-permute-start | bytes 221192 | tf_op jit(solution)/shard_map/ppermute | solution.py:547
  63.8 5.2 %collective-permute-done.7.arrived_ref = bf16[2,2,72,128]{3,2,1,0:T(8,128)(2,1)S(1)} collective-permute-done((bf16[2,2,72,128]{3,2,1,0:T(8,128)(2,1)S(1)}, bf16[2,2,72,128]{3,2,1,0:T(8,128)(2,1)S(1)}, u32[]{:S(2)}, u32[]{:S(2)}) %collective-permute-start.7) | collective-permute-done | bytes 73760 | tf_op jit(solution)/shard_map/ppermute | solution.py:547
  68.9 0.0 copy-done.2
  68.9 0.0 copy-done.3
  69.0 1.7 %finish.1 = (f32[4,1,64]{2,1,0:T(1,128)}, f32[12,1,64]{2,1,0:T(1,128)}, f32[4,64,128]{2,1,0:T(8,128)}) custom-call(s32[2,1,2]{2,1,0:T(1,128)S(1)} %bitcast.34, f32[12,1,64]{2,1,0:T(1,128)S(1)} %bitcast.32, f32[2,4,72,128]{3,2,1,0:T(8,128)S(1)} %convert_add_fusion.mid_ref, bf16[2,2,72,128]{3,2,1,0:T(8,128)(2,1)S(1)} %collective-permute-done.7.arrived_ref), custom_call_target="tpu_custom_call" | custom-call | flops 10000000 | bytes 135168 | tf_op jit(solution)/shard_map/finish/pallas_call | solution.py:557
  (5 shorter events, 0.1 us)
Async XLA Ops:
  2.7 7.8 %collective-permute-start = (bf16[2,2,72,128]{3,2,1,0:T(8,128)(2,1)}, bf16[2,2,72,128]{3,2,1,0:T(8,128)(2,1)S(1)}, u32[]{:S(2)}, u32[]{:S(2)}) collective-permute-start(bf16[2,2,72,128]{3,2,1,0:T(8,128)(2,1)} %bitcast.30), channel_id=1, source_target_pairs={{0,224},{32,0},{64,32},{96,64},{128,96},{160,128},{192,160},{224,1... | collective-permute-start | bytes 221192 | tf_op jit(solution)/shard_map/ppermute | solution.py:547
  8.7 0.9 %copy-start = (f32[400,128]{1,0:T(8,128)S(1)}, f32[400,128]{1,0:T(8,128)}, u32[]{:S(2)}) copy-start(f32[400,128]{1,0:T(8,128)} %get-tuple-element.19.pack_ref) | copy-start | bytes 614404
  9.6 0.9 %copy-start.1 = (bf16[4,72,128]{2,1,0:T(8,128)(2,1)S(1)}, bf16[4,72,128]{2,1,0:T(8,128)(2,1)}, u32[]{:S(2)}) copy-start(bf16[4,72,128]{2,1,0:T(8,128)(2,1)} %get-tuple-element.18.block_ref) | copy-start | bytes 221188
  10.6 4.6 %collective-permute-start.1 = (bf16[2,4,72,128]{3,2,1,0:T(8,128)(2,1)S(1)}, bf16[2,4,72,128]{3,2,1,0:T(8,128)(2,1)S(1)}, u32[]{:S(2)}, u32[]{:S(2)}) collective-permute-start(bf16[2,4,72,128]{3,2,1,0:T(8,128)(2,1)S(1)} %pad_maximum_fusion.1), channel_id=1, source_target_pairs={{0,24},{8,0},{16,8},{24,16},{1,25},{9,1},{17,9},{25,17},{2,26},{10... | collective-permute-start | bytes 442376 | tf_op jit(solution)/shard_map/ppermute | solution.py:547
  15.3 12.5 %collective-permute-start.3 = (bf16[4,4,72,128]{3,2,1,0:T(8,128)(2,1)S(1)}, bf16[4,4,72,128]{3,2,1,0:T(8,128)(2,1)S(1)}, u32[]{:S(2)}, u32[]{:S(2)}) collective-permute-start(bf16[4,4,72,128]{3,2,1,0:T(8,128)(2,1)S(1)} %pad_maximum_fusion), channel_id=1, source_target_pairs={{0,7},{1,0},{2,1},{3,2},{4,3},{5,4},{6,5},{7,6},{8,15},{9,8},{10,9... | collective-permute-start | bytes 884744 | tf_op jit(solution)/shard_map/ppermute | solution.py:547
  20.9 10.0 %collective-permute-start.2 = (bf16[4,4,72,128]{3,2,1,0:T(8,128)(2,1)S(1)}, bf16[4,4,72,128]{3,2,1,0:T(8,128)(2,1)S(1)}, u32[]{:S(2)}, u32[]{:S(2)}) collective-permute-start(bf16[4,4,72,128]{3,2,1,0:T(8,128)(2,1)S(1)} %pad_maximum_fusion), channel_id=1, source_target_pairs={{0,1},{1,2},{2,3},{3,4},{4,5},{5,6},{6,7},{7,0},{8,9},{9,10},{10,1... | collective-permute-start | bytes 884744 | tf_op jit(solution)/shard_map/ppermute | solution.py:547
  47.6 9.2 %collective-permute-start.4 = (bf16[4,4,72,128]{3,2,1,0:T(8,128)(2,1)S(1)}, bf16[4,4,72,128]{3,2,1,0:T(8,128)(2,1)S(1)}, u32[]{:S(2)}, u32[]{:S(2)}) collective-permute-start(bf16[4,4,72,128]{3,2,1,0:T(8,128)(2,1)S(1)} %bitcast.36), channel_id=1, source_target_pairs={{0,1},{1,2},{2,3},{3,4},{4,5},{5,6},{6,7},{7,0},{8,9},{9,10},{10,1... | collective-permute-start | bytes 884744 | tf_op jit(solution)/shard_map/ppermute | solution.py:547
  47.6 9.1 %collective-permute-start.5 = (bf16[4,4,72,128]{3,2,1,0:T(8,128)(2,1)S(1)}, bf16[4,4,72,128]{3,2,1,0:T(8,128)(2,1)S(1)}, u32[]{:S(2)}, u32[]{:S(2)}) collective-permute-start(bf16[4,4,72,128]{3,2,1,0:T(8,128)(2,1)S(1)} %bitcast.35), channel_id=1, source_target_pairs={{0,7},{1,0},{2,1},{3,2},{4,3},{5,4},{6,5},{7,6},{8,15},{9,8},{10,9... | collective-permute-start | bytes 884744 | tf_op jit(solution)/shard_map/ppermute | solution.py:547
  50.3 18.6 %copy-start.2 = (f32[2,2,1,3,64]{4,2,3,1,0:T(1,128)S(1)}, f32[2,2,1,3,64]{4,2,3,1,0:T(1,128)}, u32[]{:S(2)}) copy-start(f32[2,2,1,3,64]{4,2,3,1,0:T(1,128)} %param.10) | copy-start | bytes 9220
  50.3 18.6 %copy-start.3 = (s32[2,2,1]{1,2,0:T(1,128)S(1)}, s32[2,2,1]{1,2,0:T(1,128)}, u32[]{:S(2)}) copy-start(s32[2,2,1]{1,2,0:T(1,128)} %param.11) | copy-start | bytes 52
  56.8 4.2 %collective-permute-start.6 = (bf16[2,4,72,128]{3,2,1,0:T(8,128)(2,1)S(1)}, bf16[2,4,72,128]{3,2,1,0:T(8,128)(2,1)S(1)}, u32[]{:S(2)}, u32[]{:S(2)}) collective-permute-start(bf16[2,4,72,128]{3,2,1,0:T(8,128)(2,1)S(1)} %add_convert_fusion), channel_id=1, source_target_pairs={{0,8},{8,16},{16,24},{24,0},{1,9},{9,17},{17,25},{25,1},{2,10},{10... | collective-permute-start | bytes 442376 | tf_op jit(solution)/shard_map/ppermute | solution.py:547
  61.2 7.8 %collective-permute-start.7 = (bf16[2,2,72,128]{3,2,1,0:T(8,128)(2,1)S(1)}, bf16[2,2,72,128]{3,2,1,0:T(8,128)(2,1)S(1)}, u32[]{:S(2)}, u32[]{:S(2)}) collective-permute-start(bf16[2,2,72,128]{3,2,1,0:T(8,128)(2,1)S(1)} %slice.49), channel_id=1, source_target_pairs={{0,32},{32,64},{64,96},{96,128},{128,160},{160,192},{192,224},{224... | collective-permute-start | bytes 221192 | tf_op jit(solution)/shard_map/ppermute | solution.py:547

commit v4 on v3

--- a/solution.py
+++ b/solution.py
@@ -21,24 +21,37 @@
 INNER = [(a, b) for a in (-1, 0, 1) for b in (-1, 0, 1)]
 OUTER = [(a, b) for a in (-2, 2) for b in (-1, 0, 1)] + [(b, a) for a in (-2, 2) for b in (-1, 0, 1)]
 NEAR, REST = [], []
-_at = 0
-for _a, _b in INNER + OUTER[:7]:
-    NEAR.append((_a, _b, COLROWS, COLROWS, _at))
-    _at += COLROWS
-NJ_NEAR = _at
-_at = 0
-for _a, _b in OUTER[7:]:
-    REST.append((_a, _b, COLROWS, COLROWS, _at))
-    _at += COLROWS
-for _first, _inner, _count in ((8, False, 8), (32, False, 8), (4, True, 12), (32, True, 12)):
-    for _a, _b in INNER if _inner else OUTER:
-        REST.append((_a, _b, _first, _count, _at))
-        _at += _count
-USED = _at
-NJ_REST = 512
+
+
+def reachable(a, b):
+    return {(2, 0): (0, 1), (-2, 0): (2, 3), (0, 2): (0, 2), (0, -2): (1, 3)}[
+        (a if abs(a) == 2 else 0, b if abs(b) == 2 else 0)
+    ]
+
+
+def add_piece(pieces, a, b, first, count, stride):
+    at = sum(piece[3] for piece in pieces)
+    pieces.append((a, b, first, count, at, stride))
+
+
+for _a, _b in INNER:
+    add_piece(NEAR, _a, _b, COLROWS, COLROWS, 1)
+for _a, _b in OUTER:
+    for _e in reachable(_a, _b):
+        add_piece(NEAR, _a, _b, COLROWS + _e, 4, 4)
+for _first in (4, 32):
+    for _a, _b in INNER:
+        add_piece(REST, _a, _b, _first, 12, 1)
+for _first in (8, 32):
+    for _a, _b in OUTER:
+        for _e in reachable(_a, _b):
+            add_piece(REST, _a, _b, _first + _e, 2, 4)
+NJ_NEAR = 256
+NJ_REST = 384
 TILE = 128
 FAR = 1000.0
 GROUPS = 16
+UNROLL = 8
 TERMS = 4 * NB * COLROWS
 
 
@@ -48,10 +61,10 @@
     table[:, :3, used:] = FAR
     for parity in range(4):
         px, py = parity // 2, parity % 2
-        for a, b, first, count, at in pieces:
+        for a, b, first, count, at, stride in pieces:
             table[parity, 0, at : at + count] = SIDE * ((px + a) // 2)
             table[parity, 1, at : at + count] = SIDE * ((py + b) // 2)
-            run = np.arange(first, first + count)
+            run = first + stride * np.arange(count)
             table[parity, 2, at : at + count] = SIDE * (run // COLROWS - 1)
     return table
 
@@ -217,14 +230,20 @@
 ROOT3 = float(np.sqrt(3.0))
 
 
-def take_window(g, pieces, run, skip, feat_ext, pos_ext, feat_win, pos_win):
+def piece_rows(base, piece, run, skip):
+    a, b, first, count, _, stride = piece
+    start = base + (a * 8 + b) * run + first - skip
+    return pl.ds(start, count, stride=stride) if stride > 1 else pl.ds(start, count)
+
+
+def take_window(g, pieces, run, skip, feat_ext, pos_ext, feat_win, feat_rows, pos_rows):
     base = column(g, run)
-    for a, b, first, count, at in pieces:
-        start = base + (a * 8 + b) * run + first - skip
-        feat_win[g, at : at + count] = feat_ext[pl.ds(start, count)].astype(jnp.bfloat16)
-        pos_win[at : at + count] = pos_ext[pl.ds(start, count)].astype(jnp.bfloat16)
-    own = pos_ext[pl.ds(pl.multiple_of(base + COLROWS - skip, COLROWS), COLROWS)]
-    return own
+    for piece in pieces:
+        rows, at, count = piece_rows(base, piece, run, skip), piece[4], piece[3]
+        feat_rows[at : at + count] = feat_ext[rows]
+        pos_rows[at : at + count] = pos_ext[rows]
+    feat_win[g] = feat_rows[...].astype(jnp.bfloat16)
+    return pos_ext[pl.ds(pl.multiple_of(base + COLROWS - skip, COLROWS), COLROWS)]
 
 
 def edge_columns(g, own, far, pack_ref, off_at, edges, saved, size):
@@ -322,8 +341,8 @@
             d_far[c : c + 1, at] = jnp.sum(ds[c], axis=0, keepdims=True)
     d_win[0] = dot(edges[g], d_half[...], TN)
     d_win[1, :, :8] = d_far[...].T
-    for a, b, first, count, at in pieces:
-        start = pl.ds(base + (a * 8 + b) * run + first - skip, count)
+    for piece in pieces:
+        start, at, count = piece_rows(base, piece, run, skip), piece[4], piece[3]
         d_feat_ext[start] = d_feat_ext[start] + d_win[0, at : at + count]
         d_pos_ext[start] = d_pos_ext[start] + d_win[1, at : at + count]
     mine = pl.ds(pl.multiple_of(base + COLROWS - skip, COLROWS), COLROWS)
@@ -354,31 +373,34 @@
         out[cell, SLOTS:] = scalars.astype(out.dtype)
 
 
-def near_kernel(layer_ref, pack_ref, sums, feat_win, edges, saved, feat_ext, pos_ext, pos_win):
+def near_kernel(layer_ref, pack_ref, sums, feat_win, edges, saved, feat_ext, pos_ext, feat_rows, pos_rows):
     def spread_cell(cell, carry):
         place(layer_ref, cell, feat_ext, pos_ext, COLROWS, 0)
         return carry
 
     lax.fori_loop(0, 16, spread_cell, 0)
+    feat_rows[...] = jnp.zeros_like(feat_rows)
+    pos_rows[...] = jnp.zeros_like(pos_rows)
     pick = pack_ref[PICK : PICK + 8].astype(jnp.bfloat16)
 
     def forward(k, carry):
-        for g in (4 * k, 4 * k + 1, 4 * k + 2, 4 * k + 3):
-            own = take_window(g, NEAR, COLROWS, COLROWS, feat_ext, pos_ext, feat_win, pos_win)
+        for s in range(UNROLL):
+            g = UNROLL * k + s
+            own = take_window(g, NEAR, COLROWS, COLROWS, feat_ext, pos_ext, feat_win, feat_rows.at[s], pos_rows.at[s])
             parity = ((g // 4) & 1) * 2 + (g & 1)
-            far = dot(pick, pos_win[...], NT)
+            far = dot(pick, pos_rows[s].astype(jnp.bfloat16), NT)
             edge_columns(g, own, far, pack_ref, NEAR_OFF + parity * (8 * NJ_NEAR // TILE), edges, saved, NJ_NEAR)
-        for g in (4 * k, 4 * k + 1, 4 * k + 2, 4 * k + 3):
-            contract(g, edges, feat_win, pack_ref, sums)
-        return carry
-
-    lax.fori_loop(0, GROUPS // 4, forward, 0)
+        for s in range(UNROLL):
+            contract(UNROLL * k + s, edges, feat_win, pack_ref, sums)
+        return carry
+
+    lax.fori_loop(0, GROUPS // UNROLL, forward, 0)
 
 
 def rest_kernel(
     layer_ref, zl_ref, zh_ref, near_sums, pack_ref,
     zlo_ref, zho_ref, mid_ref, d_sums,
-    feat_ext, pos_ext, feat_win, pos_win, edges, saved, sums, energies, d_half, d_far, d_win,
+    feat_ext, pos_ext, feat_win, feat_rows, pos_rows, edges, saved, sums, energies, d_half, d_far, d_win,
 ):
     def spread_cell(cell, carry):
         place(layer_ref, cell, feat_ext, pos_ext, RUN, COLROWS)
@@ -387,22 +409,23 @@
         return carry
 
     lax.fori_loop(0, 16, spread_cell, 0)
+    feat_rows[...] = jnp.zeros_like(feat_rows)
+    pos_rows[...] = jnp.zeros_like(pos_rows)
     pick = pack_ref[PICK : PICK + 8].astype(jnp.bfloat16)
     lane = lane_kind()
-    pos_win[USED:] = jnp.zeros((NJ_REST - USED, CHAN), jnp.bfloat16)
 
     def forward(k, carry):
-        for g in (4 * k, 4 * k + 1, 4 * k + 2, 4 * k + 3):
-            own = take_window(g, REST, RUN, 0, feat_ext, pos_ext, feat_win, pos_win)
-            feat_win[g, USED:] = jnp.zeros((NJ_REST - USED, CHAN), jnp.bfloat16)
+        for s in range(UNROLL):
+            g = UNROLL * k + s
+            own = take_window(g, REST, RUN, 0, feat_ext, pos_ext, feat_win, feat_rows.at[s], pos_rows.at[s])
             parity = ((g // 4) & 1) * 2 + (g & 1)
-            far = dot(pick, pos_win[...], NT)
+            far = dot(pick, pos_rows[s].astype(jnp.bfloat16), NT)
             edge_columns(g, own, far, pack_ref, REST_OFF + parity * (8 * NJ_REST // TILE), edges, saved, NJ_REST)
-        for g in (4 * k, 4 * k + 1, 4 * k + 2, 4 * k + 3):
-            contract(g, edges, feat_win, pack_ref, sums, near_sums)
-        return carry
-
-    lax.fori_loop(0, GROUPS // 4, forward, 0)
+        for s in range(UNROLL):
+            contract(UNROLL * k + s, edges, feat_win, pack_ref, sums, near_sums)
+        return carry
+
+    lax.fori_loop(0, GROUPS // UNROLL, forward, 0)
 
     head = dot(pack_ref[MIXING:HIDDEN], pack_ref[HIDDEN:OUTPUT], NT, lax.Precision.HIGHEST)
     head_parts = halves(head)
@@ -460,14 +483,14 @@
     d_far[...] = jnp.zeros_like(d_far)
 
     def backward(k, carry):
-        for s in range(4):
+        for s in range(UNROLL):
             back_group(
-                4 * k + s, NJ_REST, REST, RUN, 0, edges, feat_win, saved, d_sums, pack_ref,
+                UNROLL * k + s, NJ_REST, REST, RUN, 0, edges, feat_win, saved, d_sums, pack_ref,
                 d_half.at[s], d_far.at[s], d_win.at[s], feat_ext, pos_ext,
             )
         return carry
 
-    lax.fori_loop(0, GROUPS // 4, backward, 0)
+    lax.fori_loop(0, GROUPS // UNROLL, backward, 0)
 
     def gather_cell(cell, carry):
         collect(cell, ((0, zlo_ref, None), (COLROWS, mid_ref, None), (2 * COLROWS, zho_ref, None)), feat_ext, pos_ext, RUN)
@@ -484,14 +507,14 @@
     d_far[...] = jnp.zeros_like(d_far)
 
     def backward(k, carry):
-        for s in range(4):
+        for s in range(UNROLL):
             back_group(
-                4 * k + s, NJ_NEAR, NEAR, COLROWS, COLROWS, edges, feat_win, saved, d_sums, pack_ref,
+                UNROLL * k + s, NJ_NEAR, NEAR, COLROWS, COLROWS, edges, feat_win, saved, d_sums, pack_ref,
                 d_half.at[s], d_far.at[s], d_win.at[s], feat_ext, pos_ext,
             )
         return carry
 
-    lax.fori_loop(0, GROUPS // 4, backward, 0)
+    lax.fori_loop(0, GROUPS // UNROLL, backward, 0)
 
     def gather_cell(cell, carry):
         collect(cell, ((0, mid_ref, rest_mid),), feat_ext, pos_ext, COLROWS)
@@ -623,7 +646,7 @@
         near_kernel,
         "near",
         [rows, ((GROUPS, NJ_NEAR, CHAN), bf16), ((GROUPS, TERMS, NJ_NEAR), bf16), ((GROUPS, 8, COLROWS, NJ_NEAR), f32)],
-        [near_ext, near_ext, ((NJ_NEAR, CHAN), bf16)],
+        [near_ext, near_ext] + [((UNROLL, NJ_NEAR, CHAN), f32)] * 2,
         (layer, pack),
         NEAR_LIMIT,
         2 * TERMS * NJ_NEAR * CHAN * GROUPS,
@@ -636,14 +659,15 @@
             ext,
             ext,
             ((GROUPS, NJ_REST, CHAN), bf16),
-            ((NJ_REST, CHAN), bf16),
+            ((UNROLL, NJ_REST, CHAN), f32),
+            ((UNROLL, NJ_REST, CHAN), f32),
             ((GROUPS, TERMS, NJ_REST), bf16),
             ((GROUPS, 8, COLROWS, NJ_REST), f32),
             rows,
             ((GROUPS * COLROWS, CHAN), f32),
-            ((4, TERMS, CHAN), bf16),
-            ((4, 8, NJ_REST), f32),
-            ((4, 2, NJ_REST, CHAN), f32),
+            ((UNROLL, TERMS, CHAN), bf16),
+            ((UNROLL, 8, NJ_REST), f32),
+            ((UNROLL, 2, NJ_REST, CHAN), f32),
         ],
         (
             layer, zl, zh, sums, pack,
@@ -655,7 +679,7 @@
         near_back_kernel,
         "near_back",
         [((16, ROWS, CHAN), f32)],
-        [near_ext, near_ext, ((4, TERMS, CHAN), bf16), ((4, 8, NJ_NEAR), f32), ((4, 2, NJ_NEAR, CHAN), f32)],
+        [near_ext, near_ext, ((UNROLL, TERMS, CHAN), bf16), ((UNROLL, 8, NJ_NEAR), f32), ((UNROLL, 2, NJ_NEAR, CHAN), f32)],
         (near_edges, near_win, near_saved, d_sums, rest_mid, pack),
         NEAR_LIMIT,
         4 * TERMS * NJ_NEAR * CHAN * GROUPS,

time: 71.7 us -> 69.2 us (0.965)
  Pallas kernels: 29.9 us -> 27.1 us
    pallas_call x6, Pallas kernels: 29.9 us -> 27.1 us  [call(): pl.pallas_call(kernel, name=name, out_shape=shapes, in_specs=[*spaces] +...]
  transfers between devices with their start and end apart: 8 -> 8, of which waited for: 6 -> 6; matrix products, arithmetic and copies ran while one was open for 0% -> 0% of each run, Pallas kernels for 14% -> 13%
where the time goes in v4:
time: 69.2 us; the launch traced here: 68.1 us
  Pallas kernels  27.1 us (39%)
  starting transfers between devices  20.8 us (30%)
  waiting for transfers between devices  17.6 us (25%)
  local copies, waits for them, and re-layouts  1.87 us (3%)
  between operations  0.72 us (1%)
    pallas_call x6, Pallas kernels, call(): pl.pallas_call(kernel, name=name, out_shape=shapes, in_specs=[*spaces] +...  27.1 us
    ppermute x8, starting transfers between devices, moved(): lax.ppermute(part, axis, [(i, (i + step) % count) for i in range(count)])  20.8 us
    ppermute x8, waiting for transfers between devices, moved(): lax.ppermute(part, axis, [(i, (i + step) % count) for i in range(count)])  17.6 us
    unnamed x8, local copies, waits for them, and re-layouts  1.81 us
  transfers between devices with their start and end apart: 8, of which 6 were waited for; matrix products, arithmetic and copies ran while one was open for 0% of the time, Pallas kernels for 13%

profile of v4, /device:TPU:1, one launch (start us, length us, event | category | flops | bytes accessed | tf_op | source)
XLA Modules:
  0.0 68.1 jit_solution(10822447899683574790)
XLA Ops:
  0.6 2.1 %sort.1 = (bf16[4,72,128]{2,1,0:T(8,128)(2,1)}, f32[368,128]{1,0:T(8,128)}) custom-call(s32[2,1,2]{2,1,0:T(1,128)} %bitcast.33, f32[12,1,64]{2,1,0:T(1,128)} %bitcast.31, s32[4,1,64]{2,1,0:T(1,128)} %bitcast.45, bf16[4,64,128]{2,1,0:T(8,128)(2,1)} %bitcast.41, f32[16,128]{1,0:T(8,128)} %bitcast.43, f32[10,3,128]{2,1,0:T(4,128)} %bitcast.42, ...), custom_call_target="tpu_custom_call" | custom-call | flops 10000000 | bytes 262144 | tf_op jit(solution)/shard_map/sort/pallas_call | solution.py:580
  2.7 6.0 %collective-permute-start = (bf16[2,2,72,128]{3,2,1,0:T(8,128)(2,1)}, bf16[2,2,72,128]{3,2,1,0:T(8,128)(2,1)S(1)}, u32[]{:S(2)}, u32[]{:S(2)}) collective-permute-start(bf16[2,2,72,128]{3,2,1,0:T(8,128)(2,1)} %bitcast.30), channel_id=1, source_target_pairs={{0,224},{32,0},{64,32},{96,64},{128,96},{160,128},{192,160},{224,1... | collective-permute-start | bytes 221192 | tf_op jit(solution)/shard_map/ppermute | solution.py:570
  8.7 0.0 copy-start
  8.7 0.9 %copy-done = f32[368,128]{1,0:T(8,128)S(1)} copy-done((f32[368,128]{1,0:T(8,128)S(1)}, f32[368,128]{1,0:T(8,128)}, u32[]{:S(2)}) %copy-start) | copy-done | bytes 188440
  9.6 0.0 copy-start.1
  9.6 0.9 %copy-done.1 = bf16[4,72,128]{2,1,0:T(8,128)(2,1)S(1)} copy-done((bf16[4,72,128]{2,1,0:T(8,128)(2,1)S(1)}, bf16[4,72,128]{2,1,0:T(8,128)(2,1)}, u32[]{:S(2)}) %copy-start.1) | copy-done | bytes 73752
  10.5 0.0 collective-permute-done
  10.6 1.6 %collective-permute-start.1 = (bf16[2,4,72,128]{3,2,1,0:T(8,128)(2,1)S(1)}, bf16[2,4,72,128]{3,2,1,0:T(8,128)(2,1)S(1)}, u32[]{:S(2)}, u32[]{:S(2)}) collective-permute-start(bf16[2,4,72,128]{3,2,1,0:T(8,128)(2,1)S(1)} %pad_maximum_fusion.1), channel_id=1, source_target_pairs={{0,24},{8,0},{16,8},{24,16},{1,25},{9,1},{17,9},{25,17},{2,26},{10... | collective-permute-start | bytes 442376 | tf_op jit(solution)/shard_map/ppermute | solution.py:570
  12.1 3.1 %collective-permute-done.1 = bf16[2,4,72,128]{3,2,1,0:T(8,128)(2,1)S(1)} collective-permute-done((bf16[2,4,72,128]{3,2,1,0:T(8,128)(2,1)S(1)}, bf16[2,4,72,128]{3,2,1,0:T(8,128)(2,1)S(1)}, u32[]{:S(2)}, u32[]{:S(2)}) %collective-permute-start.1) | collective-permute-done | bytes 147488 | tf_op jit(solution)/shard_map/ppermute | solution.py:570
  15.3 5.7 %collective-permute-start.3 = (bf16[4,4,72,128]{3,2,1,0:T(8,128)(2,1)S(1)}, bf16[4,4,72,128]{3,2,1,0:T(8,128)(2,1)S(1)}, u32[]{:S(2)}, u32[]{:S(2)}) collective-permute-start(bf16[4,4,72,128]{3,2,1,0:T(8,128)(2,1)S(1)} %pad_maximum_fusion), channel_id=1, source_target_pairs={{0,7},{1,0},{2,1},{3,2},{4,3},{5,4},{6,5},{7,6},{8,15},{9,8},{10,9... | collective-permute-start | bytes 884744 | tf_op jit(solution)/shard_map/ppermute | solution.py:570
  20.9 0.0 collective-permute-start.2
  20.9 3.4 %near.1 = (f32[4,256,128]{2,1,0:T(8,128)S(1)}, bf16[16,256,128]{2,1,0:T(8,128)(2,1)S(1)}, bf16[16,512,256]{2,1,0:T(8,128)(2,1)S(1)}, f32[16,8,16,256]{3,2,1,0:T(8,128)S(1)}) custom-call(bf16[16,72,128]{2,1,0:T(8,128)(2,1)S(1)} %bitcast.28, f32[368,128]{1,0:T(8,128)S(1)} %get-tuple-element.21.pack_ref), custom_call_target="tpu_custom_call" | custom-call | flops 536870912 | bytes 7864320 | tf_op jit(solution)/shard_map/near/pallas_call | solution.py:580
  24.3 3.4 %collective-permute-done.3 = bf16[4,4,72,128]{3,2,1,0:T(8,128)(2,1)S(1)} collective-permute-done((bf16[4,4,72,128]{3,2,1,0:T(8,128)(2,1)S(1)}, bf16[4,4,72,128]{3,2,1,0:T(8,128)(2,1)S(1)}, u32[]{:S(2)}, u32[]{:S(2)}) %collective-permute-start.3) | collective-permute-done | bytes 294944 | tf_op jit(solution)/shard_map/ppermute | solution.py:570
  27.7 3.2 %collective-permute-done.2 = bf16[4,4,72,128]{3,2,1,0:T(8,128)(2,1)S(1)} collective-permute-done((bf16[4,4,72,128]{3,2,1,0:T(8,128)(2,1)S(1)}, bf16[4,4,72,128]{3,2,1,0:T(8,128)(2,1)S(1)}, u32[]{:S(2)}, u32[]{:S(2)}) %collective-permute-start.2) | collective-permute-done | bytes 294944 | tf_op jit(solution)/shard_map/ppermute | solution.py:570
  30.9 14.2 %rest.1 = (bf16[16,72,128]{2,1,0:T(8,128)(2,1)S(1)}, bf16[16,72,128]{2,1,0:T(8,128)(2,1)S(1)}, f32[16,72,128]{2,1,0:T(8,128)S(1)}, f32[4,256,128]{2,1,0:T(8,128)S(1)}) custom-call(bf16[16,72,128]{2,1,0:T(8,128)(2,1)S(1)} %bitcast.29, bf16[16,72,128]{2,1,0:T(8,128)(2,1)S(1)} %bitcast.38, bf16[16,72,128]{2,1,0:T(8,128)(2,1)S(1)} %bitcast.37, ...), custom_call_target="tpu_custom_call" | custom-call | flops 2415919104 | bytes 1703936 | tf_op jit(solution)/shard_map/rest/pallas_call | solution.py:580
  45.0 0.1 collective-permute-start.4
  45.1 2.7 %collective-permute-start.5 = (bf16[4,4,72,128]{3,2,1,0:T(8,128)(2,1)S(1)}, bf16[4,4,72,128]{3,2,1,0:T(8,128)(2,1)S(1)}, u32[]{:S(2)}, u32[]{:S(2)}) collective-permute-start(bf16[4,4,72,128]{3,2,1,0:T(8,128)(2,1)S(1)} %bitcast.35), channel_id=1, source_target_pairs={{0,7},{1,0},{2,1},{3,2},{4,3},{5,4},{6,5},{7,6},{8,15},{9,8},{10,9... | collective-permute-start | bytes 884744 | tf_op jit(solution)/shard_map/ppermute | solution.py:570
  47.8 0.0 copy-start.2
  47.8 0.0 copy-start.3
  47.8 5.7 %near_back.1 = f32[16,72,128]{2,1,0:T(8,128)S(1)} custom-call(bf16[16,512,256]{2,1,0:T(8,128)(2,1)S(1)} %get-tuple-element.22.edges, bf16[16,256,128]{2,1,0:T(8,128)(2,1)S(1)} %get-tuple-element.23.feat_win, f32[16,8,16,256]{3,2,1,0:T(8,128)S(1)} %get-tuple-element.24.saved, f32[4,256,128]{2,1,0:T(8,128)S(1)} %get-tuple-element.26.d_sums, ...), custom_call_target="tpu_custom_call" | custom-call | flops 1073741824 | bytes 589824 | tf_op jit(solution)/shard_map/near_back/pallas_call | solution.py:580
  53.6 0.7 collective-permute-done.4
  54.2 0.0 collective-permute-done.5
  54.2 0.1 add_convert_fusion
  54.3 2.2 %collective-permute-start.6 = (bf16[2,4,72,128]{3,2,1,0:T(8,128)(2,1)S(1)}, bf16[2,4,72,128]{3,2,1,0:T(8,128)(2,1)S(1)}, u32[]{:S(2)}, u32[]{:S(2)}) collective-permute-start(bf16[2,4,72,128]{3,2,1,0:T(8,128)(2,1)S(1)} %add_convert_fusion), channel_id=1, source_target_pairs={{0,8},{8,16},{16,24},{24,0},{1,9},{9,17},{17,25},{25,1},{2,10},{10... | collective-permute-start | bytes 442376 | tf_op jit(solution)/shard_map/ppermute | solution.py:570
  56.5 2.1 %collective-permute-done.6 = bf16[2,4,72,128]{3,2,1,0:T(8,128)(2,1)S(1)} collective-permute-done((bf16[2,4,72,128]{3,2,1,0:T(8,128)(2,1)S(1)}, bf16[2,4,72,128]{3,2,1,0:T(8,128)(2,1)S(1)}, u32[]{:S(2)}, u32[]{:S(2)}) %collective-permute-start.6) | collective-permute-done | bytes 147488 | tf_op jit(solution)/shard_map/ppermute | solution.py:570
  58.6 0.1 convert_add_fusion.mid_ref
  58.6 2.6 %collective-permute-start.7 = (bf16[2,2,72,128]{3,2,1,0:T(8,128)(2,1)S(1)}, bf16[2,2,72,128]{3,2,1,0:T(8,128)(2,1)S(1)}, u32[]{:S(2)}, u32[]{:S(2)}) collective-permute-start(bf16[2,2,72,128]{3,2,1,0:T(8,128)(2,1)S(1)} %slice.49), channel_id=1, source_target_pairs={{0,32},{32,64},{64,96},{96,128},{128,160},{160,192},{192,224},{224... | collective-permute-start | bytes 221192 | tf_op jit(solution)/shard_map/ppermute | solution.py:570
  61.3 5.2 %collective-permute-done.7.arrived_ref = bf16[2,2,72,128]{3,2,1,0:T(8,128)(2,1)S(1)} collective-permute-done((bf16[2,2,72,128]{3,2,1,0:T(8,128)(2,1)S(1)}, bf16[2,2,72,128]{3,2,1,0:T(8,128)(2,1)S(1)}, u32[]{:S(2)}, u32[]{:S(2)}) %collective-permute-start.7) | collective-permute-done | bytes 73760 | tf_op jit(solution)/shard_map/ppermute | solution.py:570
  66.4 0.0 copy-done.2
  66.5 0.0 copy-done.3
  66.5 1.7 %finish.1 = (f32[4,1,64]{2,1,0:T(1,128)}, f32[12,1,64]{2,1,0:T(1,128)}, f32[4,64,128]{2,1,0:T(8,128)}) custom-call(s32[2,1,2]{2,1,0:T(1,128)S(1)} %bitcast.34, f32[12,1,64]{2,1,0:T(1,128)S(1)} %bitcast.32, f32[2,4,72,128]{3,2,1,0:T(8,128)S(1)} %convert_add_fusion.mid_ref, bf16[2,2,72,128]{3,2,1,0:T(8,128)(2,1)S(1)} %collective-permute-done.7.arrived_ref), custom_call_target="tpu_custom_call" | custom-call | flops 10000000 | bytes 135168 | tf_op jit(solution)/shard_map/finish/pallas_call | solution.py:580
  (5 shorter events, 0.1 us)
Async XLA Ops:
  2.7 7.8 %collective-permute-start = (bf16[2,2,72,128]{3,2,1,0:T(8,128)(2,1)}, bf16[2,2,72,128]{3,2,1,0:T(8,128)(2,1)S(1)}, u32[]{:S(2)}, u32[]{:S(2)}) collective-permute-start(bf16[2,2,72,128]{3,2,1,0:T(8,128)(2,1)} %bitcast.30), channel_id=1, source_target_pairs={{0,224},{32,0},{64,32},{96,64},{128,96},{160,128},{192,160},{224,1... | collective-permute-start | bytes 221192 | tf_op jit(solution)/shard_map/ppermute | solution.py:570
  8.7 0.9 %copy-start = (f32[368,128]{1,0:T(8,128)S(1)}, f32[368,128]{1,0:T(8,128)}, u32[]{:S(2)}) copy-start(f32[368,128]{1,0:T(8,128)} %get-tuple-element.19.pack_ref) | copy-start | bytes 565252
  9.6 0.9 %copy-start.1 = (bf16[4,72,128]{2,1,0:T(8,128)(2,1)S(1)}, bf16[4,72,128]{2,1,0:T(8,128)(2,1)}, u32[]{:S(2)}) copy-start(bf16[4,72,128]{2,1,0:T(8,128)(2,1)} %get-tuple-element.18.block_ref) | copy-start | bytes 221188
  10.6 4.6 %collective-permute-start.1 = (bf16[2,4,72,128]{3,2,1,0:T(8,128)(2,1)S(1)}, bf16[2,4,72,128]{3,2,1,0:T(8,128)(2,1)S(1)}, u32[]{:S(2)}, u32[]{:S(2)}) collective-permute-start(bf16[2,4,72,128]{3,2,1,0:T(8,128)(2,1)S(1)} %pad_maximum_fusion.1), channel_id=1, source_target_pairs={{0,24},{8,0},{16,8},{24,16},{1,25},{9,1},{17,9},{25,17},{2,26},{10... | collective-permute-start | bytes 442376 | tf_op jit(solution)/shard_map/ppermute | solution.py:570
  15.3 12.5 %collective-permute-start.3 = (bf16[4,4,72,128]{3,2,1,0:T(8,128)(2,1)S(1)}, bf16[4,4,72,128]{3,2,1,0:T(8,128)(2,1)S(1)}, u32[]{:S(2)}, u32[]{:S(2)}) collective-permute-start(bf16[4,4,72,128]{3,2,1,0:T(8,128)(2,1)S(1)} %pad_maximum_fusion), channel_id=1, source_target_pairs={{0,7},{1,0},{2,1},{3,2},{4,3},{5,4},{6,5},{7,6},{8,15},{9,8},{10,9... | collective-permute-start | bytes 884744 | tf_op jit(solution)/shard_map/ppermute | solution.py:570
  20.9 10.0 %collective-permute-start.2 = (bf16[4,4,72,128]{3,2,1,0:T(8,128)(2,1)S(1)}, bf16[4,4,72,128]{3,2,1,0:T(8,128)(2,1)S(1)}, u32[]{:S(2)}, u32[]{:S(2)}) collective-permute-start(bf16[4,4,72,128]{3,2,1,0:T(8,128)(2,1)S(1)} %pad_maximum_fusion), channel_id=1, source_target_pairs={{0,1},{1,2},{2,3},{3,4},{4,5},{5,6},{6,7},{7,0},{8,9},{9,10},{10,1... | collective-permute-start | bytes 884744 | tf_op jit(solution)/shard_map/ppermute | solution.py:570
  45.0 9.2 %collective-permute-start.4 = (bf16[4,4,72,128]{3,2,1,0:T(8,128)(2,1)S(1)}, bf16[4,4,72,128]{3,2,1,0:T(8,128)(2,1)S(1)}, u32[]{:S(2)}, u32[]{:S(2)}) collective-permute-start(bf16[4,4,72,128]{3,2,1,0:T(8,128)(2,1)S(1)} %bitcast.36), channel_id=1, source_target_pairs={{0,1},{1,2},{2,3},{3,4},{4,5},{5,6},{6,7},{7,0},{8,9},{9,10},{10,1... | collective-permute-start | bytes 884744 | tf_op jit(solution)/shard_map/ppermute | solution.py:570
  45.1 9.1 %collective-permute-start.5 = (bf16[4,4,72,128]{3,2,1,0:T(8,128)(2,1)S(1)}, bf16[4,4,72,128]{3,2,1,0:T(8,128)(2,1)S(1)}, u32[]{:S(2)}, u32[]{:S(2)}) collective-permute-start(bf16[4,4,72,128]{3,2,1,0:T(8,128)(2,1)S(1)} %bitcast.35), channel_id=1, source_target_pairs={{0,7},{1,0},{2,1},{3,2},{4,3},{5,4},{6,5},{7,6},{8,15},{9,8},{10,9... | collective-permute-start | bytes 884744 | tf_op jit(solution)/shard_map/ppermute | solution.py:570
  47.8 18.7 %copy-start.2 = (f32[2,2,1,3,64]{4,2,3,1,0:T(1,128)S(1)}, f32[2,2,1,3,64]{4,2,3,1,0:T(1,128)}, u32[]{:S(2)}) copy-start(f32[2,2,1,3,64]{4,2,3,1,0:T(1,128)} %param.10) | copy-start | bytes 9220
  47.8 18.7 %copy-start.3 = (s32[2,2,1]{1,2,0:T(1,128)S(1)}, s32[2,2,1]{1,2,0:T(1,128)}, u32[]{:S(2)}) copy-start(s32[2,2,1]{1,2,0:T(1,128)} %param.11) | copy-start | bytes 52
  54.3 4.3 %collective-permute-start.6 = (bf16[2,4,72,128]{3,2,1,0:T(8,128)(2,1)S(1)}, bf16[2,4,72,128]{3,2,1,0:T(8,128)(2,1)S(1)}, u32[]{:S(2)}, u32[]{:S(2)}) collective-permute-start(bf16[2,4,72,128]{3,2,1,0:T(8,128)(2,1)S(1)} %add_convert_fusion), channel_id=1, source_target_pairs={{0,8},{8,16},{16,24},{24,0},{1,9},{9,17},{17,25},{25,1},{2,10},{10... | collective-permute-start | bytes 442376 | tf_op jit(solution)/shard_map/ppermute | solution.py:570
  58.6 7.8 %collective-permute-start.7 = (bf16[2,2,72,128]{3,2,1,0:T(8,128)(2,1)S(1)}, bf16[2,2,72,128]{3,2,1,0:T(8,128)(2,1)S(1)}, u32[]{:S(2)}, u32[]{:S(2)}) collective-permute-start(bf16[2,2,72,128]{3,2,1,0:T(8,128)(2,1)S(1)} %slice.49), channel_id=1, source_target_pairs={{0,32},{32,64},{64,96},{96,128},{128,160},{160,192},{192,224},{224... | collective-permute-start | bytes 221192 | tf_op jit(solution)/shard_map/ppermute | solution.py:570

commit v5 on v4

--- a/solution.py
+++ b/solution.py
@@ -209,7 +209,8 @@
     for cc in range(4):
         x, y = 2 * (cell % 4) + cc // 2, 2 * (cell // 4) + cc % 2
         base = pl.multiple_of((x * 8 + y) * run + shift, COLROWS)
-        feat_ext[pl.ds(base, COLROWS)] = msg[cell, COLROWS * cc : COLROWS * cc + COLROWS].astype(jnp.float32)
+        if feat_ext is not None:
+            feat_ext[pl.ds(base, COLROWS)] = msg[cell, COLROWS * cc : COLROWS * cc + COLROWS].astype(jnp.float32)
         for h in range(2):
             pos_ext[pl.ds(base + 8 * h, 8)] = jnp.where(group == 2 * cc + h, scalars, 0.0)
 
@@ -359,21 +360,23 @@
         for cc in range(4):
             x, y = 2 * (cell % 4) + cc // 2, 2 * (cell // 4) + cc % 2
             base = pl.multiple_of((x * 8 + y) * run + shift, COLROWS)
-            rows = d_feat_ext[pl.ds(base, COLROWS)]
-            if more is not None:
-                rows = rows + more[cell, COLROWS * cc : COLROWS * cc + COLROWS]
-            out[cell, COLROWS * cc : COLROWS * cc + COLROWS] = rows.astype(out.dtype)
+            if out.shape[1] == ROWS:
+                rows = d_feat_ext[pl.ds(base, COLROWS)]
+                out[cell, COLROWS * cc : COLROWS * cc + COLROWS] = rows.astype(out.dtype)
             for h in range(2):
                 place_at = 16 * (2 * cc + h)
                 block = d_pos_ext[pl.ds(base + 8 * h, 8)]
                 block = jnp.where(lane8 < 6, block, 0.0)
                 scalars = scalars + (pltpu.roll(block, place_at, 1) if place_at else block)
         if more is not None:
-            scalars = scalars + more[cell, SLOTS:]
-        out[cell, SLOTS:] = scalars.astype(out.dtype)
-
-
-def near_kernel(layer_ref, pack_ref, sums, feat_win, edges, saved, feat_ext, pos_ext, feat_rows, pos_rows):
+            scalars = scalars + more[cell]
+        out[cell, out.shape[1] - EXTRA :] = scalars.astype(out.dtype)
+
+
+def near_kernel(
+    layer_ref, pack_ref, sums, feat_win, edges, saved, weights_ref, head_ref,
+    feat_ext, pos_ext, feat_rows, pos_rows,
+):
     def spread_cell(cell, carry):
         place(layer_ref, cell, feat_ext, pos_ext, COLROWS, 0)
         return carry
@@ -396,14 +399,29 @@
 
     lax.fori_loop(0, GROUPS // UNROLL, forward, 0)
 
+    head_ref[...] = dot(pack_ref[MIXING:HIDDEN], pack_ref[HIDDEN:OUTPUT], NT, lax.Precision.HIGHEST)
+    lane = lane_kind()
+
+    def couple(g, carry):
+        own = pos_ext[pl.ds(pl.multiple_of(column(g, COLROWS), COLROWS), COLROWS)]
+        kind = own_scalar(own, lane == 9)
+        for q in range(3):
+            w = jnp.zeros((COLROWS, CHAN), jnp.float32)
+            for s in range(NSPEC):
+                w = jnp.where(kind == float(s), pack_ref[COUPLE + 3 * s + q : COUPLE + 3 * s + q + 1], w)
+            weights_ref[q, group_rows(g)] = w
+        return carry
+
+    lax.fori_loop(0, GROUPS, couple, 0, unroll=4)
+
 
 def rest_kernel(
-    layer_ref, zl_ref, zh_ref, near_sums, pack_ref,
+    layer_ref, zl_ref, zh_ref, near_sums, weights_ref, head_ref, pack_ref,
     zlo_ref, zho_ref, mid_ref, d_sums,
     feat_ext, pos_ext, feat_win, feat_rows, pos_rows, edges, saved, sums, energies, d_half, d_far, d_win,
 ):
     def spread_cell(cell, carry):
-        place(layer_ref, cell, feat_ext, pos_ext, RUN, COLROWS)
+        place(layer_ref, cell, None, pos_ext, RUN, COLROWS)
         place(zl_ref, cell, feat_ext, pos_ext, RUN, 0)
         place(zh_ref, cell, feat_ext, pos_ext, RUN, 2 * COLROWS)
         return carry
@@ -427,28 +445,20 @@
 
     lax.fori_loop(0, GROUPS // UNROLL, forward, 0)
 
-    head = dot(pack_ref[MIXING:HIDDEN], pack_ref[HIDDEN:OUTPUT], NT, lax.Precision.HIGHEST)
-    head_parts = halves(head)
+    head_parts = halves(head_ref[...])
     ow = pack_ref[OUTPUT : OUTPUT + 1, : OUTPUT - HIDDEN]
 
     def readout(k, carry):
-        kinds, occs = [], []
+        occs = []
         for s in range(8):
             start = column(k * 8 + s, RUN) + COLROWS
             own = pos_ext[pl.ds(pl.multiple_of(start, COLROWS), COLROWS)]
-            kinds.append(own_scalar(own, lane == 9))
             occs.append(own_scalar(own, lane == 10))
-        kind = jnp.concatenate(kinds, axis=0)
         occ = jnp.concatenate(occs, axis=0)
         rows = pl.ds(pl.multiple_of(k * 128, 128), 128)
         scalar = sums[0, rows]
         vectors = [sums[m, rows] for m in (1, 2, 3)]
-        weights = []
-        for q in range(3):
-            w = jnp.zeros((128, CHAN), jnp.float32)
-            for s in range(NSPEC):
-                w = jnp.where(kind == float(s), pack_ref[COUPLE + 3 * s + q : COUPLE + 3 * s + q + 1], w)
-            weights.append(w)
+        weights = [weights_ref[q, rows] for q in range(3)]
         length = vectors[0] * vectors[0] + vectors[1] * vectors[1] + vectors[2] * vectors[2]
         product = weights[0] * scalar + weights[1] * scalar * scalar + weights[2] * length
         hidden = dot_parts(product, head_parts, NN)
@@ -642,10 +652,10 @@
     ext = ((64 * RUN, CHAN), f32)
     near_ext = ((64 * COLROWS, CHAN), f32)
     rows = ((4, GROUPS * COLROWS, CHAN), f32)
-    sums, near_win, near_edges, near_saved = call(
+    sums, near_win, near_edges, near_saved, weights, head = call(
         near_kernel,
         "near",
-        [rows, ((GROUPS, NJ_NEAR, CHAN), bf16), ((GROUPS, TERMS, NJ_NEAR), bf16), ((GROUPS, 8, COLROWS, NJ_NEAR), f32)],
+        [rows, ((GROUPS, NJ_NEAR, CHAN), bf16), ((GROUPS, TERMS, NJ_NEAR), bf16), ((GROUPS, 8, COLROWS, NJ_NEAR), f32), ((3, GROUPS * COLROWS, CHAN), f32), ((CHAN, OUTPUT - HIDDEN), f32)],
         [near_ext, near_ext] + [((UNROLL, NJ_NEAR, CHAN), f32)] * 2,
         (layer, pack),
         NEAR_LIMIT,
@@ -654,7 +664,7 @@
     z_low, z_high, rest_mid, d_sums = call(
         rest_kernel,
         "rest",
-        [((16, ROWS, CHAN), bf16)] * 2 + [((16, ROWS, CHAN), f32), rows],
+        [((16, ROWS, CHAN), bf16)] * 2 + [((16, EXTRA, CHAN), f32), rows],
         [
             ext,
             ext,
@@ -670,7 +680,7 @@
             ((UNROLL, 2, NJ_REST, CHAN), f32),
         ],
         (
-            layer, zl, zh, sums, pack,
+            layer, zl, zh, sums, weights, head, pack,
         ),
         REST_LIMIT,
         6 * TERMS * NJ_REST * CHAN * GROUPS,

time: 69.2 us -> 68.4 us (0.988)
  waiting for transfers between devices: 17.6 us -> 16.9 us
  transfers between devices with their start and end apart: 8 -> 8, of which waited for: 6 -> 6; matrix products, arithmetic and copies ran while one was open for 0% -> 0% of each run, Pallas kernels for 13% -> 15%
where the time goes in v5:
time: 68.4 us; the launch traced here: 67.3 us
  Pallas kernels  26.9 us (39%)
  starting transfers between devices  20.8 us (30%)
  waiting for transfers between devices  16.9 us (25%)
  local copies, waits for them, and re-layouts  1.87 us (3%)
  between operations  0.72 us (1%)
    pallas_call x6, Pallas kernels, call(): pl.pallas_call(kernel, name=name, out_shape=shapes, in_specs=[*spaces] +...  26.9 us
    ppermute x8, starting transfers between devices, moved(): lax.ppermute(part, axis, [(i, (i + step) % count) for i in range(count)])  20.8 us
    ppermute x8, waiting for transfers between devices, moved(): lax.ppermute(part, axis, [(i, (i + step) % count) for i in range(count)])  16.9 us
    unnamed x8, local copies, waits for them, and re-layouts  1.81 us
  transfers between devices with their start and end apart: 8, of which 6 were waited for; matrix products, arithmetic and copies ran while one was open for 0% of the time, Pallas kernels for 15%

profile of v5, /device:TPU:1, one launch (start us, length us, event | category | flops | bytes accessed | tf_op | source)
XLA Modules:
  0.0 67.3 jit_solution(9991423904086239032)
XLA Ops:
  0.6 2.1 %sort.1 = (bf16[4,72,128]{2,1,0:T(8,128)(2,1)}, f32[368,128]{1,0:T(8,128)}) custom-call(s32[2,1,2]{2,1,0:T(1,128)} %bitcast.33, f32[12,1,64]{2,1,0:T(1,128)} %bitcast.31, s32[4,1,64]{2,1,0:T(1,128)} %bitcast.45, bf16[4,64,128]{2,1,0:T(8,128)(2,1)} %bitcast.41, f32[16,128]{1,0:T(8,128)} %bitcast.43, f32[10,3,128]{2,1,0:T(4,128)} %bitcast.42, ...), custom_call_target="tpu_custom_call" | custom-call | flops 10000000 | bytes 262144 | tf_op jit(solution)/shard_map/sort/pallas_call | solution.py:590
  2.7 6.0 %collective-permute-start = (bf16[2,2,72,128]{3,2,1,0:T(8,128)(2,1)}, bf16[2,2,72,128]{3,2,1,0:T(8,128)(2,1)S(1)}, u32[]{:S(2)}, u32[]{:S(2)}) collective-permute-start(bf16[2,2,72,128]{3,2,1,0:T(8,128)(2,1)} %bitcast.30), channel_id=1, source_target_pairs={{0,224},{32,0},{64,32},{96,64},{128,96},{160,128},{192,160},{224,1... | collective-permute-start | bytes 221192 | tf_op jit(solution)/shard_map/ppermute | solution.py:580
  8.7 0.0 copy-start
  8.7 0.9 %copy-done = f32[368,128]{1,0:T(8,128)S(1)} copy-done((f32[368,128]{1,0:T(8,128)S(1)}, f32[368,128]{1,0:T(8,128)}, u32[]{:S(2)}) %copy-start) | copy-done | bytes 188440
  9.6 0.0 copy-start.1
  9.6 0.9 %copy-done.1 = bf16[4,72,128]{2,1,0:T(8,128)(2,1)S(1)} copy-done((bf16[4,72,128]{2,1,0:T(8,128)(2,1)S(1)}, bf16[4,72,128]{2,1,0:T(8,128)(2,1)}, u32[]{:S(2)}) %copy-start.1) | copy-done | bytes 73752
  10.5 0.0 collective-permute-done
  10.6 1.6 %collective-permute-start.1 = (bf16[2,4,72,128]{3,2,1,0:T(8,128)(2,1)S(1)}, bf16[2,4,72,128]{3,2,1,0:T(8,128)(2,1)S(1)}, u32[]{:S(2)}, u32[]{:S(2)}) collective-permute-start(bf16[2,4,72,128]{3,2,1,0:T(8,128)(2,1)S(1)} %pad_maximum_fusion.1), channel_id=1, source_target_pairs={{0,24},{8,0},{16,8},{24,16},{1,25},{9,1},{17,9},{25,17},{2,26},{10... | collective-permute-start | bytes 442376 | tf_op jit(solution)/shard_map/ppermute | solution.py:580
  12.1 3.1 %collective-permute-done.1 = bf16[2,4,72,128]{3,2,1,0:T(8,128)(2,1)S(1)} collective-permute-done((bf16[2,4,72,128]{3,2,1,0:T(8,128)(2,1)S(1)}, bf16[2,4,72,128]{3,2,1,0:T(8,128)(2,1)S(1)}, u32[]{:S(2)}, u32[]{:S(2)}) %collective-permute-start.1) | collective-permute-done | bytes 147488 | tf_op jit(solution)/shard_map/ppermute | solution.py:580
  15.3 5.7 %collective-permute-start.3 = (bf16[4,4,72,128]{3,2,1,0:T(8,128)(2,1)S(1)}, bf16[4,4,72,128]{3,2,1,0:T(8,128)(2,1)S(1)}, u32[]{:S(2)}, u32[]{:S(2)}) collective-permute-start(bf16[4,4,72,128]{3,2,1,0:T(8,128)(2,1)S(1)} %pad_maximum_fusion), channel_id=1, source_target_pairs={{0,7},{1,0},{2,1},{3,2},{4,3},{5,4},{6,5},{7,6},{8,15},{9,8},{10,9... | collective-permute-start | bytes 884744 | tf_op jit(solution)/shard_map/ppermute | solution.py:580
  20.9 0.0 collective-permute-start.2
  20.9 4.1 %near.1 = (f32[4,256,128]{2,1,0:T(8,128)S(1)}, bf16[16,256,128]{2,1,0:T(8,128)(2,1)S(1)}, bf16[16,512,256]{2,1,0:T(8,128)(2,1)S(1)}, f32[16,8,16,256]{3,2,1,0:T(...) custom-call(bf16[16,72,128]{2,1,0:T(8,128)(2,1)S(1)} %bitcast.28, f32[368,128]{1,0:T(8,128)S(1)} %get-tuple-element.23.pack_ref), custom_call_target="tpu_custom_call" | custom-call | flops 536870912 | bytes 8265728 | tf_op jit(solution)/shard_map/near/pallas_call | solution.py:590
  25.0 2.7 %collective-permute-done.3 = bf16[4,4,72,128]{3,2,1,0:T(8,128)(2,1)S(1)} collective-permute-done((bf16[4,4,72,128]{3,2,1,0:T(8,128)(2,1)S(1)}, bf16[4,4,72,128]{3,2,1,0:T(8,128)(2,1)S(1)}, u32[]{:S(2)}, u32[]{:S(2)}) %collective-permute-start.3) | collective-permute-done | bytes 294944 | tf_op jit(solution)/shard_map/ppermute | solution.py:580
  27.7 3.2 %collective-permute-done.2 = bf16[4,4,72,128]{3,2,1,0:T(8,128)(2,1)S(1)} collective-permute-done((bf16[4,4,72,128]{3,2,1,0:T(8,128)(2,1)S(1)}, bf16[4,4,72,128]{3,2,1,0:T(8,128)(2,1)S(1)}, u32[]{:S(2)}, u32[]{:S(2)}) %collective-permute-start.2) | collective-permute-done | bytes 294944 | tf_op jit(solution)/shard_map/ppermute | solution.py:580
  30.9 13.3 %rest.1 = (bf16[16,72,128]{2,1,0:T(8,128)(2,1)S(1)}, bf16[16,72,128]{2,1,0:T(8,128)(2,1)S(1)}, f32[16,8,128]{2,1,0:T(8,128)S(1)}, f32[4,256,128]{2,1,0:T(8,128)S(1)}) custom-call(bf16[16,72,128]{2,1,0:T(8,128)(2,1)S(1)} %bitcast.29, bf16[16,72,128]{2,1,0:T(8,128)(2,1)S(1)} %bitcast.38, bf16[16,72,128]{2,1,0:T(8,128)(2,1)S(1)} %bitcast.37, ...), custom_call_target="tpu_custom_call" | custom-call | flops 2415919104 | bytes 1179648 | tf_op jit(solution)/shard_map/rest/pallas_call | solution.py:590
  44.2 0.1 collective-permute-start.4
  44.3 2.7 %collective-permute-start.5 = (bf16[4,4,72,128]{3,2,1,0:T(8,128)(2,1)S(1)}, bf16[4,4,72,128]{3,2,1,0:T(8,128)(2,1)S(1)}, u32[]{:S(2)}, u32[]{:S(2)}) collective-permute-start(bf16[4,4,72,128]{3,2,1,0:T(8,128)(2,1)S(1)} %bitcast.35), channel_id=1, source_target_pairs={{0,7},{1,0},{2,1},{3,2},{4,3},{5,4},{6,5},{7,6},{8,15},{9,8},{10,9... | collective-permute-start | bytes 884744 | tf_op jit(solution)/shard_map/ppermute | solution.py:580
  47.0 0.0 copy-start.2
  47.0 0.0 copy-start.3
  47.0 5.7 %near_back.1 = f32[16,72,128]{2,1,0:T(8,128)S(1)} custom-call(bf16[16,512,256]{2,1,0:T(8,128)(2,1)S(1)} %get-tuple-element.24.edges, bf16[16,256,128]{2,1,0:T(8,128)(2,1)S(1)} %get-tuple-element.25.feat_win, f32[16,8,16,256]{3,2,1,0:T(8,128)S(1)} %get-tuple-element.26.saved, f32[4,256,128]{2,1,0:T(8,128)S(1)} %get-tuple-element.30.d_sums, ...), custom_call_target="tpu_custom_call" | custom-call | flops 1073741824 | bytes 589824 | tf_op jit(solution)/shard_map/near_back/pallas_call | solution.py:590
  52.8 0.7 collective-permute-done.4
  53.4 0.0 collective-permute-done.5
  53.4 0.1 add_convert_fusion
  53.5 2.2 %collective-permute-start.6 = (bf16[2,4,72,128]{3,2,1,0:T(8,128)(2,1)S(1)}, bf16[2,4,72,128]{3,2,1,0:T(8,128)(2,1)S(1)}, u32[]{:S(2)}, u32[]{:S(2)}) collective-permute-start(bf16[2,4,72,128]{3,2,1,0:T(8,128)(2,1)S(1)} %add_convert_fusion), channel_id=1, source_target_pairs={{0,8},{8,16},{16,24},{24,0},{1,9},{9,17},{17,25},{25,1},{2,10},{10... | collective-permute-start | bytes 442376 | tf_op jit(solution)/shard_map/ppermute | solution.py:580
  55.7 2.1 %collective-permute-done.6 = bf16[2,4,72,128]{3,2,1,0:T(8,128)(2,1)S(1)} collective-permute-done((bf16[2,4,72,128]{3,2,1,0:T(8,128)(2,1)S(1)}, bf16[2,4,72,128]{3,2,1,0:T(8,128)(2,1)S(1)}, u32[]{:S(2)}, u32[]{:S(2)}) %collective-permute-start.6) | collective-permute-done | bytes 147488 | tf_op jit(solution)/shard_map/ppermute | solution.py:580
  57.8 0.1 convert_add_fusion.mid_ref
  57.8 2.6 %collective-permute-start.7 = (bf16[2,2,72,128]{3,2,1,0:T(8,128)(2,1)S(1)}, bf16[2,2,72,128]{3,2,1,0:T(8,128)(2,1)S(1)}, u32[]{:S(2)}, u32[]{:S(2)}) collective-permute-start(bf16[2,2,72,128]{3,2,1,0:T(8,128)(2,1)S(1)} %slice.49), channel_id=1, source_target_pairs={{0,32},{32,64},{64,96},{96,128},{128,160},{160,192},{192,224},{224... | collective-permute-start | bytes 221192 | tf_op jit(solution)/shard_map/ppermute | solution.py:580
  60.5 5.2 %collective-permute-done.7.arrived_ref = bf16[2,2,72,128]{3,2,1,0:T(8,128)(2,1)S(1)} collective-permute-done((bf16[2,2,72,128]{3,2,1,0:T(8,128)(2,1)S(1)}, bf16[2,2,72,128]{3,2,1,0:T(8,128)(2,1)S(1)}, u32[]{:S(2)}, u32[]{:S(2)}) %collective-permute-start.7) | collective-permute-done | bytes 73760 | tf_op jit(solution)/shard_map/ppermute | solution.py:580
  65.6 0.0 copy-done.2
  65.6 0.0 copy-done.3
  65.6 1.7 %finish.1 = (f32[4,1,64]{2,1,0:T(1,128)}, f32[12,1,64]{2,1,0:T(1,128)}, f32[4,64,128]{2,1,0:T(8,128)}) custom-call(s32[2,1,2]{2,1,0:T(1,128)S(1)} %bitcast.34, f32[12,1,64]{2,1,0:T(1,128)S(1)} %bitcast.32, f32[2,4,72,128]{3,2,1,0:T(8,128)S(1)} %convert_add_fusion.mid_ref, bf16[2,2,72,128]{3,2,1,0:T(8,128)(2,1)S(1)} %collective-permute-done.7.arrived_ref), custom_call_target="tpu_custom_call" | custom-call | flops 10000000 | bytes 135168 | tf_op jit(solution)/shard_map/finish/pallas_call | solution.py:590
  (5 shorter events, 0.1 us)
Async XLA Ops:
  2.7 7.8 %collective-permute-start = (bf16[2,2,72,128]{3,2,1,0:T(8,128)(2,1)}, bf16[2,2,72,128]{3,2,1,0:T(8,128)(2,1)S(1)}, u32[]{:S(2)}, u32[]{:S(2)}) collective-permute-start(bf16[2,2,72,128]{3,2,1,0:T(8,128)(2,1)} %bitcast.30), channel_id=1, source_target_pairs={{0,224},{32,0},{64,32},{96,64},{128,96},{160,128},{192,160},{224,1... | collective-permute-start | bytes 221192 | tf_op jit(solution)/shard_map/ppermute | solution.py:580
  8.7 0.9 %copy-start = (f32[368,128]{1,0:T(8,128)S(1)}, f32[368,128]{1,0:T(8,128)}, u32[]{:S(2)}) copy-start(f32[368,128]{1,0:T(8,128)} %get-tuple-element.21.pack_ref) | copy-start | bytes 565252
  9.6 0.9 %copy-start.1 = (bf16[4,72,128]{2,1,0:T(8,128)(2,1)S(1)}, bf16[4,72,128]{2,1,0:T(8,128)(2,1)}, u32[]{:S(2)}) copy-start(bf16[4,72,128]{2,1,0:T(8,128)(2,1)} %get-tuple-element.20.block_ref) | copy-start | bytes 221188
  10.6 4.6 %collective-permute-start.1 = (bf16[2,4,72,128]{3,2,1,0:T(8,128)(2,1)S(1)}, bf16[2,4,72,128]{3,2,1,0:T(8,128)(2,1)S(1)}, u32[]{:S(2)}, u32[]{:S(2)}) collective-permute-start(bf16[2,4,72,128]{3,2,1,0:T(8,128)(2,1)S(1)} %pad_maximum_fusion.1), channel_id=1, source_target_pairs={{0,24},{8,0},{16,8},{24,16},{1,25},{9,1},{17,9},{25,17},{2,26},{10... | collective-permute-start | bytes 442376 | tf_op jit(solution)/shard_map/ppermute | solution.py:580
  15.3 12.5 %collective-permute-start.3 = (bf16[4,4,72,128]{3,2,1,0:T(8,128)(2,1)S(1)}, bf16[4,4,72,128]{3,2,1,0:T(8,128)(2,1)S(1)}, u32[]{:S(2)}, u32[]{:S(2)}) collective-permute-start(bf16[4,4,72,128]{3,2,1,0:T(8,128)(2,1)S(1)} %pad_maximum_fusion), channel_id=1, source_target_pairs={{0,7},{1,0},{2,1},{3,2},{4,3},{5,4},{6,5},{7,6},{8,15},{9,8},{10,9... | collective-permute-start | bytes 884744 | tf_op jit(solution)/shard_map/ppermute | solution.py:580
  20.9 10.0 %collective-permute-start.2 = (bf16[4,4,72,128]{3,2,1,0:T(8,128)(2,1)S(1)}, bf16[4,4,72,128]{3,2,1,0:T(8,128)(2,1)S(1)}, u32[]{:S(2)}, u32[]{:S(2)}) collective-permute-start(bf16[4,4,72,128]{3,2,1,0:T(8,128)(2,1)S(1)} %pad_maximum_fusion), channel_id=1, source_target_pairs={{0,1},{1,2},{2,3},{3,4},{4,5},{5,6},{6,7},{7,0},{8,9},{9,10},{10,1... | collective-permute-start | bytes 884744 | tf_op jit(solution)/shard_map/ppermute | solution.py:580
  44.2 9.2 %collective-permute-start.4 = (bf16[4,4,72,128]{3,2,1,0:T(8,128)(2,1)S(1)}, bf16[4,4,72,128]{3,2,1,0:T(8,128)(2,1)S(1)}, u32[]{:S(2)}, u32[]{:S(2)}) collective-permute-start(bf16[4,4,72,128]{3,2,1,0:T(8,128)(2,1)S(1)} %bitcast.36), channel_id=1, source_target_pairs={{0,1},{1,2},{2,3},{3,4},{4,5},{5,6},{6,7},{7,0},{8,9},{9,10},{10,1... | collective-permute-start | bytes 884744 | tf_op jit(solution)/shard_map/ppermute | solution.py:580
  44.3 9.1 %collective-permute-start.5 = (bf16[4,4,72,128]{3,2,1,0:T(8,128)(2,1)S(1)}, bf16[4,4,72,128]{3,2,1,0:T(8,128)(2,1)S(1)}, u32[]{:S(2)}, u32[]{:S(2)}) collective-permute-start(bf16[4,4,72,128]{3,2,1,0:T(8,128)(2,1)S(1)} %bitcast.35), channel_id=1, source_target_pairs={{0,7},{1,0},{2,1},{3,2},{4,3},{5,4},{6,5},{7,6},{8,15},{9,8},{10,9... | collective-permute-start | bytes 884744 | tf_op jit(solution)/shard_map/ppermute | solution.py:580
  47.0 18.7 %copy-start.2 = (f32[2,2,1,3,64]{4,2,3,1,0:T(1,128)S(1)}, f32[2,2,1,3,64]{4,2,3,1,0:T(1,128)}, u32[]{:S(2)}) copy-start(f32[2,2,1,3,64]{4,2,3,1,0:T(1,128)} %param.10) | copy-start | bytes 9220
  47.0 18.7 %copy-start.3 = (s32[2,2,1]{1,2,0:T(1,128)S(1)}, s32[2,2,1]{1,2,0:T(1,128)}, u32[]{:S(2)}) copy-start(s32[2,2,1]{1,2,0:T(1,128)} %param.11) | copy-start | bytes 52
  53.5 4.3 %collective-permute-start.6 = (bf16[2,4,72,128]{3,2,1,0:T(8,128)(2,1)S(1)}, bf16[2,4,72,128]{3,2,1,0:T(8,128)(2,1)S(1)}, u32[]{:S(2)}, u32[]{:S(2)}) collective-permute-start(bf16[2,4,72,128]{3,2,1,0:T(8,128)(2,1)S(1)} %add_convert_fusion), channel_id=1, source_target_pairs={{0,8},{8,16},{16,24},{24,0},{1,9},{9,17},{17,25},{25,1},{2,10},{10... | collective-permute-start | bytes 442376 | tf_op jit(solution)/shard_map/ppermute | solution.py:580
  57.8 7.8 %collective-permute-start.7 = (bf16[2,2,72,128]{3,2,1,0:T(8,128)(2,1)S(1)}, bf16[2,2,72,128]{3,2,1,0:T(8,128)(2,1)S(1)}, u32[]{:S(2)}, u32[]{:S(2)}) collective-permute-start(bf16[2,2,72,128]{3,2,1,0:T(8,128)(2,1)S(1)} %slice.49), channel_id=1, source_target_pairs={{0,32},{32,64},{64,96},{96,128},{128,160},{160,192},{192,224},{224... | collective-permute-start | bytes 221192 | tf_op jit(solution)/shard_map/ppermute | solution.py:580
